TPU v7x, 32 devices: a whole 2x2x4 slice. The times are simulated.
32 devices in a mesh: chan: 8 (over z, x), band: 4 (over y, core).
Axes of the slice: x: 2, y: 2, z: 4, core: 2. Of those that a mesh axis runs over, the one named last changes fastest.
Arguments:
- spectra: bfloat16 [8, 2, 4096, 512], P('band', None, 'chan'), may hold values from -64 to 64
- half_width: int32 [512], replicated, may hold values from 1 to 32, as said below
- panel_block: int32 [4], replicated, may hold values from 0 to 7
- panel_offset: int32 [4], replicated, may hold values from 0 to 256
Outputs:
- cross: bfloat16 [4, 8, 2, 4096, 256], P(None, 'band', None, 'chan')
Inputs may be any that keep to these rules, and one draw needn't show every extreme that they name: `half_width`: some window's half-width is exactly 32.
All inputs are finite; a program needn't handle non-finite values.
Results may differ from a plain program's by a relative error of at most 0.0056.
Values may be sent and summed in bfloat16 or wider, within the bound.
No kernel may reach another device: no remote copies, remote signals or barrier semaphores. Data moves between devices by JAX's collectives and lax.ppermute only.
A program may use at most 64 MiB of HBM per device.

v0:
```python
import functools

import jax
import jax.numpy as jnp
from jax import lax
from jax.experimental import pallas as pl
from jax.experimental.pallas import tpu as pltpu
from jax.sharding import PartitionSpec as P


PANEL = 256
NPANEL = 4
HALO = 32
HALF = PANEL // 2
LANES = 128
LAG = 2
SUBS = 4
SPANS = (1, 3)


def spans_of(groups):
    counts = SPANS if sum(SPANS) == groups else (groups,)
    return [(sum(counts[:i]), n) for i, n in enumerate(counts)]


def plan(n_chan, n_chunks):
    both = min(LAG * (n_chan // 2 - 1) // 2, n_chunks)
    single = n_chunks - both
    n_sends = single + 2 * both
    return single, n_sends, max(single + LAG * (n_chan - 2), n_sends + LAG * (n_chan // 2 - 1))


def scale_kernel(channels, bins, p_ref, q_ref, h0_ref, h1_ref, w_ref, scale_ref, s_ref, t_ref):
    rows, _ = scale_ref.shape
    ext = rows + 2 * HALO
    far = lax.rem(lax.axis_index("band"), 2)
    width = w_ref[...]
    span = 2 * width + 1
    inner = p_ref[...] + q_ref[...]
    edge = h0_ref[...] + h1_ref[...]

    @pl.when(far == 0)
    def _():
        s_ref[:HALO, :] = edge
        s_ref[HALO:ext, :] = inner

    @pl.when(far == 1)
    def _():
        s_ref[: ext - HALO, :] = inner
        s_ref[ext - HALO : ext, :] = edge

    s_ref[ext:, :] = jnp.zeros((s_ref.shape[0] - ext, s_ref.shape[1]), jnp.float32)
    t_ref[...] = s_ref[...]
    step = 1
    while step * 2 <= 2 * HALO + 1:
        doubled = s_ref[0:ext, :] + s_ref[step : step + ext, :]
        s_ref[0:ext, :] = doubled
        step *= 2
        here = t_ref[0:ext, :]
        t_ref[0:ext, :] = jnp.where((span & step) != 0, doubled + t_ref[step : step + ext, :], here)
    skip = HALO - width
    step = 1
    n = ext
    while step < HALO:
        n = n - step
        t_ref[0:n, :] = jnp.where((skip & step) != 0, t_ref[step : step + n, :], t_ref[0:n, :])
        step *= 2
    total = t_ref[:rows, :]
    chan = lax.broadcasted_iota(jnp.int32, scale_ref.shape, 0) + (2 * lax.axis_index("chan") + far) * rows
    count = jnp.minimum(chan + width, channels - 1) - jnp.maximum(chan - width, 0) + 1
    scale_ref[...] = lax.rsqrt(total / (count.astype(jnp.float32) * bins) + 1e-06)


def norm_kernel(base, groups, subs, starts_ref, mine_ref, other_ref, x_ref, *rest):
    per = 2 * subs
    normed, own = rest[:groups], rest[groups : groups * (1 + per)]
    x_buf, scale_buf, normed_buf, n_ref, in_sem, scale_sem, out_sem = rest[groups * (1 + per) :]
    _, f_dev, parts, rows, _ = x_buf.shape
    half_rows = rows // 2
    far = lax.rem(lax.axis_index("band"), 2)
    reads = []
    for g in range(groups):
        lanes = pl.ds((base + g) * LANES, LANES)
        reads.append(pltpu.make_async_copy(x_ref.at[:, :, :, lanes], x_buf.at[g], in_sem.at[g]))
        reads[g].start()
    shares = []
    for i, ref in enumerate((mine_ref, other_ref)):
        at = far * half_rows if i == 0 else (1 - far) * half_rows
        at = pl.ds(pl.multiple_of(at, half_rows), half_rows)
        shares.append(pltpu.make_async_copy(ref, scale_buf.at[at, :], scale_sem.at[i]))
        shares[i].start()
    for copy in shares:
        copy.wait()
    size = HALF // subs
    writes = []
    for g in range(groups):
        reads[g].wait()
        scale = scale_buf[:, g * LANES : (g + 1) * LANES]
        for f in range(f_dev):
            for k in range(parts):
                value = (x_buf[g, f, k].astype(jnp.float32) * scale).astype(jnp.bfloat16)
                normed_buf[g, f, k] = value
                n_ref[f, k] = value.astype(jnp.float32)
        for p in range(NPANEL):
            start = starts_ref[p]
            for i in range(per):
                at = pl.ds(start + i * size, size)
                for f in range(f_dev):
                    for k in range(parts):
                        own[g * per + i][p, f, k] = n_ref[f, k, at, :].astype(jnp.bfloat16)
        writes.append(pltpu.make_async_copy(normed_buf.at[g], normed[g], out_sem.at[g]))
        writes[g].start()
    for copy in writes:
        copy.wait()


def cross_kernel(groups, n_chan, n_chunks, n_steps, single, scaling, block_ref, *refs):
    normed, refs = refs[:groups], refs[groups:]
    lists = []
    for size in (n_chunks, n_chunks, n_steps, n_steps):
        lists.append(refs[:size])
        refs = refs[size:]
    out_ref, src_ref, left_ref, sems, left_sem = refs
    per = n_chunks // groups
    size = HALF // per
    p = pl.program_id(0)

    def place(c):
        return jnp.where(lax.rem(c, 2) == 0, c // 2, n_chan - 1 - c // 2)

    here = place(lax.axis_index("chan"))

    def each(panel, slot, do):
        ahead = lax.rem(here - place(block_ref[panel]) + n_chan, n_chan)
        for d in range(n_chan):

            @pl.when(ahead == d)
            def _():
                for half in range(2):
                    for c in range(n_chunks):
                        g, j = c // per, c % per
                        if d == 0:
                            source = lists[half][c]
                        elif c < single:
                            source = lists[2 + half][c + LAG * ((d if half == 0 else n_chan - d) - 1)]
                        else:
                            t = single + 2 * (c - single) + half
                            way = 0 if d <= n_chan // 2 else 1
                            source = lists[2 + way][t + LAG * ((d if way == 0 else n_chan - d) - 1)]
                        do(
                            pltpu.make_async_copy(
                                source.at[panel],
                                src_ref.at[slot, :, :, g, pl.ds(half * HALF + j * size, size), :],
                                sems.at[slot],
                            )
                        )

    slot = lax.rem(p, 2)

    @pl.when(p == 0)
    def _():
        each(0, 0, lambda copy: copy.start())
        copies = [pltpu.make_async_copy(n, left_ref.at[g], left_sem.at[g]) for g, n in enumerate(normed)]
        for copy in copies:
            copy.start()
        for copy in copies:
            copy.wait()

    pltpu.make_async_copy(src_ref.at[slot], src_ref.at[slot], sems.at[slot]).wait()

    @pl.when(p + 1 < NPANEL)
    def _():
        each(p + 1, 1 - slot, lambda copy: copy.start())

    def dot(a, b):
        return lax.dot_general(a, b, (((1,), (1,)), ((), ())), preferred_element_type=jnp.float32)

    for f in range(src_ref.shape[1]):
        left = [[left_ref[g, f, k] for g in range(groups)] for k in range(2)]
        right = jnp.concatenate([src_ref[slot, f, k, g] for k in range(2) for g in range(groups)], axis=1)
        real = dot(jnp.concatenate(left[0] + left[1], axis=1), right)
        out_ref[0, f, 0] = (real * scaling).astype(jnp.bfloat16)
        imag = dot(jnp.concatenate(left[1] + [-n for n in left[0]], axis=1), right)
        out_ref[0, f, 1] = (imag * scaling).astype(jnp.bfloat16)


def local(spectra, half_width, panel_block, panel_offset):
    f_dev, parts, ch_dev, windows = spectra.shape
    n_chan, n_band = lax.axis_size("chan"), lax.axis_size("band")
    bins, channels = f_dev * n_band, ch_dev * n_chan
    groups = windows // LANES
    me = lax.axis_index("chan")
    hbm = pl.BlockSpec(memory_space=pl.ANY)

    ring = list(range(0, n_chan, 2)) + list(range(1, n_chan, 2))[::-1]

    is_me = jnp.broadcast_to((panel_block == me)[:, None, None, None, None], (NPANEL, 1, 1, 1, LANES))
    is_me = is_me.astype(jnp.float32)

    half_rows = ch_dev // 2
    keep_rows = half_rows + HALO
    band = lax.axis_index("band")
    near = band % 2 == 0

    def flip(block, bit):
        return lax.ppermute(block, "band", [(b, b ^ bit) for b in range(n_band)])

    def outward(block, bit):
        pairs = [
            (c * n_band + b, (c + (2 * (b % 2) - 1)) * n_band + (b ^ 1 ^ bit))
            for c in range(n_chan)
            for b in range(n_band)
            if 0 <= c + (2 * (b % 2) - 1) < n_chan
        ]
        return lax.ppermute(block, ("chan", "band"), pairs)

    power = jnp.sum(jnp.square(spectra.astype(jnp.float32)), axis=(0, 1))
    first, second = power[:keep_rows], power[half_rows - HALO :]
    share = jnp.where(near, first, second) + flip(jnp.where(near, second, first), 1)
    bit = 2
    while bit * 2 < n_band:
        share = share + flip(share, bit)
        bit *= 2
    spans = spans_of(groups)
    shares = [share[:, base * LANES : (base + n) * LANES] for base, n in spans]
    theirs = []
    for i in range(len(spans)):
        theirs.append(flip(shares[i], bit))
    edge = jnp.where(near, share[:HALO], share[keep_rows - HALO :])
    halos = [outward(edge, 0), outward(edge, bit)]
    widths = half_width.reshape(1, windows)

    piece = (NPANEL, f_dev, parts, HALF // SUBS, LANES)
    block = (f_dev, parts, ch_dev, LANES)
    cuts = 2 * SUBS
    normed, own = [], [[], []]
    for i, (base, n_groups) in enumerate(spans):
        span = n_groups * LANES
        scale = pl.pallas_call(
            functools.partial(scale_kernel, channels, bins),
            grid=(n_groups,),
            out_shape=jax.ShapeDtypeStruct((half_rows, span), jnp.float32),
            in_specs=[pl.BlockSpec((keep_rows, LANES), lambda g: (0, g))] * 2
            + [pl.BlockSpec((HALO, LANES), lambda g, base=base: (0, base + g))] * 2
            + [pl.BlockSpec((1, LANES), lambda g, base=base: (0, base + g))],
            out_specs=pl.BlockSpec((half_rows, LANES), lambda g: (0, g)),
            scratch_shapes=[pltpu.VMEM((half_rows + 4 * HALO, LANES), jnp.float32)] * 2,
            name="scale",
        )
        scale = scale(shares[i], theirs[i], *halos, widths)
        norm = pl.pallas_call(
            functools.partial(norm_kernel, base, n_groups, SUBS),
            out_shape=[jax.ShapeDtypeStruct(block, jnp.bfloat16)] * n_groups
            + [pltpu.VMEM(piece, jnp.bfloat16)] * (n_groups * cuts),
            in_specs=[pl.BlockSpec(memory_space=pltpu.SMEM)] + [hbm] * 3,
            out_specs=[hbm] * n_groups + [pl.BlockSpec(memory_space=pltpu.VMEM)] * (n_groups * cuts),
            scratch_shapes=[
                pltpu.VMEM((n_groups, *block), jnp.bfloat16),
                pltpu.VMEM((ch_dev, span), jnp.float32),
                pltpu.VMEM((n_groups, *block), jnp.bfloat16),
                pltpu.VMEM(block, jnp.float32),
                pltpu.SemaphoreType.DMA((n_groups,)),
                pltpu.SemaphoreType.DMA((2,)),
                pltpu.SemaphoreType.DMA((n_groups,)),
            ],
            name="norm",
        )
        other = flip(scale, 1)
        outs = norm(panel_offset, scale, other, spectra)
        normed += outs[:n_groups]
        outs = outs[n_groups:]
        for g in range(n_groups):
            own[0] += outs[g * cuts : g * cuts + SUBS]
            own[1] += outs[g * cuts + SUBS : (g + 1) * cuts]

    n_chunks = groups * SUBS
    single, n_sends, n_steps = plan(n_chan, n_chunks)
    got = [[], []]
    rest = [own[half][c] for c in range(single, n_chunks) for half in range(2)]
    sends = [own[half][:single] + rest for half in range(2)]

    marks = {LAG: lax.optimization_barrier(is_me)}
    for t in range(LAG + 1, n_sends):
        marks[t] = lax.optimization_barrier(marks[t - 1] * marks[t - 1])
    for t in range(n_steps):
        if t < LAG:
            value = [sends[half][t] for half in range(2)]
        elif t < n_sends:
            mask, *args = lax.optimization_barrier(
                (marks[t], sends[0][t], sends[1][t], got[0][t - LAG], got[1][t - LAG])
            )
            value = [jnp.where(mask > 0, args[half], args[2 + half]) for half in range(2)]
        else:
            value = [got[half][t - LAG] for half in range(2)]
        for half in range(2):
            step = 1 if half == 0 else -1
            pairs = [(ring[i], ring[(i + step) % n_chan]) for i in range(n_chan)]
            got[half].append(lax.ppermute(value[half], "chan", pairs))

    block = (1, f_dev, parts, ch_dev, PANEL)
    return pl.pallas_call(
        functools.partial(cross_kernel, groups, n_chan, n_chunks, n_steps, single, windows ** (-0.5)),
        grid=(NPANEL,),
        out_shape=jax.ShapeDtypeStruct((NPANEL, f_dev, parts, ch_dev, PANEL), jnp.bfloat16),
        in_specs=[pl.BlockSpec(memory_space=pltpu.SMEM)]
        + [hbm] * (groups + 2 * n_chunks + 2 * n_steps),
        out_specs=pl.BlockSpec(block, lambda p: (p, 0, 0, 0, 0)),
        scratch_shapes=[
            pltpu.VMEM((2, f_dev, parts, groups, PANEL, LANES), jnp.bfloat16),
            pltpu.VMEM((groups, f_dev, parts, ch_dev, LANES), jnp.bfloat16),
            pltpu.SemaphoreType.DMA((2,)),
            pltpu.SemaphoreType.DMA((groups,)),
        ],
        name="cross",
    )(panel_block, *normed, *own[0], *own[1], *got[0], *got[1])


def solution(mesh):
    placed = (P("band", None, "chan", None), P(), P(), P())
    return jax.shard_map(
        local,
        mesh=mesh,
        in_specs=placed,
        out_specs=P(None, "band", None, "chan", None),
        check_vma=False,
    )
```

profile of v0, /device:TPU:0, one launch (start us, length us, event | category | flops | bytes accessed | tf_op | source)
XLA Modules:
  0.0 148.7 jit_solution(10618062833582839289)
XLA Ops:
  0.0 2.2 %multiply_reduce_fusion = f32[512,512]{1,0:T(8,128)S(1)} fusion(bf16[2,2,512,512]{3,2,1,0:T(8,128)(2,1)} %x_ref.3), kind=kLoop, calls=%fused_computation | loop fusion | flops 2883584 | bytes 3145728 | tf_op jit(solution)/shard_map/reduce_sum | solution.py:217
  2.8 1.6 %collective-permute-done = f32[288,512]{1,0:T(8,128)S(1)} collective-permute-done((f32[288,512]{1,0:T(8,128)S(1)}, f32[288,512]{1,0:T(8,128)S(1)}, u32[]{:S(2)}, u32[]{:S(2)}) %collective-permute-start) | collective-permute-done | bytes 589856 | tf_op jit(solution)/shard_map/ppermute | solution.py:206
  4.7 2.9 %collective-permute-start.1 = (f32[288,128]{1,0:T(8,128)S(1)}, f32[288,128]{1,0:T(8,128)S(1)}, u32[]{:S(2)}, u32[]{:S(2)}) collective-permute-start(f32[288,128]{1,0:T(8,128)S(1)} %slice.26.p_ref), channel_id=1, source_target_pairs={{0,2},{1,3},{2,0},{3,1},{4,6},{5,7},{6,4},{7,5},{8,10},{9,11},{10,... | collective-permute-start | bytes 442376 | tf_op jit(solution)/shard_map/ppermute | solution.py:206
  9.0 2.7 %collective-permute-done.1.q_ref = f32[288,128]{1,0:T(8,128)S(1)} collective-permute-done((f32[288,128]{1,0:T(8,128)S(1)}, f32[288,128]{1,0:T(8,128)S(1)}, u32[]{:S(2)}, u32[]{:S(2)}) %collective-permute-start.1) | collective-permute-done | bytes 147488 | tf_op jit(solution)/shard_map/ppermute | solution.py:206
  12.4 2.0 %scale.2.mine_ref = f32[256,128]{1,0:T(8,128)} custom-call(f32[288,128]{1,0:T(8,128)} %copy-done.33, f32[288,128]{1,0:T(8,128)} %copy-done.64, f32[32,512]{1,0:T(8,128)} %copy-done.63, f32[32,512]{1,0:T(8,128)} %copy-done.62, s32[1,512]{1,0:T(1,128)} %bitcast.35), custom_call_target="tpu_custom_call" | custom-call | tf_op jit(solution)/shard_map/scale/pallas_call | solution.py:250
  14.4 5.0 %collective-permute-start.4 = (f32[256,128]{1,0:T(8,128)}, f32[256,128]{1,0:T(8,128)S(1)}, u32[]{:S(2)}, u32[]{:S(2)}) collective-permute-start(f32[256,128]{1,0:T(8,128)} %scale.2.mine_ref), channel_id=1, source_target_pairs={{0,1},{1,0},{2,3},{3,2},{4,5},{5,4},{6,7},{7,6},{8,9},{9,8},{10,11... | collective-permute-start | bytes 393224 | tf_op jit(solution)/shard_map/ppermute | solution.py:206
  21.2 2.8 %norm.2 = (bf16[2,2,512,128]{3,2,1,0:T(8,128)(2,1)}, bf16[4,2,2,32,128]{4,3,2,1,0:T(8,128)(2,1)S(1)}, bf16[4,2,2,32,128]{4,3,2,1,0:T(8,128)(2,1)S(1)}, bf16[4,2,...) custom-call(s32[4]{0:T(128)} %starts_ref.3, ...), custom_call_target="tpu_custom_call" | custom-call | tf_op jit(solution)/shard_map/norm/pallas_call | solution.py:269
  24.1 2.3 %collective-permute-start.7 = (bf16[4,2,2,32,128]{4,3,2,1,0:T(8,128)(2,1)S(1)}, bf16[4,2,2,32,128]{4,3,2,1,0:T(8,128)(2,1)S(1)}, u32[]{:S(2)}, u32[]{:S(2)}) collective-permute-start(bf16[4,2,2,32,128]{4,3,2,1,0:T(8,128)(2,1)S(1)} %get-tuple-element.130.refs_4_), channel_id=1, source_target_pairs={{0,8},{8,16},{16,24},{24,28},{28,20},{20,12},{12,4},{4,0},{1,9},{9... | collective-permute-start | bytes 393224 | tf_op jit(solution)/shard_map/ppermute | solution.py:298
  26.4 1.6 %collective-permute-start.8 = (bf16[4,2,2,32,128]{4,3,2,1,0:T(8,128)(2,1)S(1)}, bf16[4,2,2,32,128]{4,3,2,1,0:T(8,128)(2,1)S(1)}, u32[]{:S(2)}, u32[]{:S(2)}) collective-permute-start(bf16[4,2,2,32,128]{4,3,2,1,0:T(8,128)(2,1)S(1)} %get-tuple-element.131.refs_5_), channel_id=1, source_target_pairs={{0,8},{8,16},{16,24},{24,28},{28,20},{20,12},{12,4},{4,0},{1,9},{9... | collective-permute-start | bytes 393224 | tf_op jit(solution)/shard_map/ppermute | solution.py:298
  34.2 1.6 %collective-permute-start.5 = (f32[288,384]{1,0:T(8,128)S(1)}, f32[288,384]{1,0:T(8,128)S(1)}, u32[]{:S(2)}, u32[]{:S(2)}) collective-permute-start(f32[288,384]{1,0:T(8,128)S(1)} %slice.29.p_ref), channel_id=1, source_target_pairs={{0,2},{1,3},{2,0},{3,1},{4,6},{5,7},{6,4},{7,5},{8,10},{9,11},{10,... | collective-permute-start | bytes 1327112 | tf_op jit(solution)/shard_map/ppermute | solution.py:206
  36.8 1.9 %collective-permute-start.13 = (bf16[4,2,2,32,128]{4,3,2,1,0:T(8,128)(2,1)}, bf16[4,2,2,32,128]{4,3,2,1,0:T(8,128)(2,1)}, u32[]{:S(2)}, u32[]{:S(2)}) collective-permute-start(bf16[4,2,2,32,128]{4,3,2,1,0:T(8,128)(2,1)} %get-tuple-element.279), channel_id=1, source_target_pairs={{0,4},{8,0},{16,8},{24,16},{28,24},{20,28},{12,20},{4,12},{1,5},{9... | collective-permute-start | bytes 393224 | tf_op jit(solution)/shard_map/ppermute | solution.py:298
  38.8 7.0 %collective-permute-done.5.q_ref = f32[288,384]{1,0:T(8,128)S(1)} collective-permute-done((f32[288,384]{1,0:T(8,128)S(1)}, f32[288,384]{1,0:T(8,128)S(1)}, u32[]{:S(2)}, u32[]{:S(2)}) %collective-permute-start.5) | collective-permute-done | bytes 442400 | tf_op jit(solution)/shard_map/ppermute | solution.py:206
  46.6 3.5 %scale.3.mine_ref = f32[256,384]{1,0:T(8,128)} custom-call(f32[288,384]{1,0:T(8,128)} %copy-done.32, f32[288,384]{1,0:T(8,128)} %copy-done.61, f32[32,512]{1,0:T(8,128)} %copy-done.63, f32[32,512]{1,0:T(8,128)} %copy-done.62, s32[1,512]{1,0:T(1,128)} %bitcast.36), custom_call_target="tpu_custom_call" | custom-call | tf_op jit(solution)/shard_map/scale/pallas_call | solution.py:250
  50.8 1.7 %collective-permute-start.15 = (bf16[4,2,2,32,128]{4,3,2,1,0:T(8,128)(2,1)}, bf16[4,2,2,32,128]{4,3,2,1,0:T(8,128)(2,1)}, u32[]{:S(2)}, u32[]{:S(2)}) collective-permute-start(bf16[4,2,2,32,128]{4,3,2,1,0:T(8,128)(2,1)} %get-tuple-element.277), channel_id=1, source_target_pairs={{0,4},{8,0},{16,8},{24,16},{28,24},{20,28},{12,20},{4,12},{1,5},{9... | collective-permute-start | bytes 393224 | tf_op jit(solution)/shard_map/ppermute | solution.py:298
  52.9 4.0 %norm.3 = (bf16[2,2,512,128]{3,2,1,0:T(8,128)(2,1)}, bf16[2,2,512,128]{3,2,1,0:T(8,128)(2,1)}, bf16[2,2,512,128]{3,2,1,0:T(8,128)(2,1)}, bf16[4,2,2,32,128]{4,3,...) custom-call(s32[4]{0:T(128)} %starts_ref.3, ...), custom_call_target="tpu_custom_call" | custom-call | tf_op jit(solution)/shard_map/norm/pallas_call | solution.py:269
  60.1 1.6 %collective-permute-start.19 = (bf16[4,2,2,32,128]{4,3,2,1,0:T(8,128)(2,1)S(1)}, bf16[4,2,2,32,128]{4,3,2,1,0:T(8,128)(2,1)S(1)}, u32[]{:S(2)}, u32[]{:S(2)}) collective-permute-start(bf16[4,2,2,32,128]{4,3,2,1,0:T(8,128)(2,1)S(1)} %get-tuple-element.273), channel_id=1, source_target_pairs={{0,4},{8,0},{16,8},{24,16},{28,24},{20,28},{12,20},{4,12},{1,5},{9... | collective-permute-start | bytes 393224 | tf_op jit(solution)/shard_map/ppermute | solution.py:298
  63.3 1.6 %collective-permute-start.17 = (bf16[4,2,2,32,128]{4,3,2,1,0:T(8,128)(2,1)S(1)}, bf16[4,2,2,32,128]{4,3,2,1,0:T(8,128)(2,1)S(1)}, u32[]{:S(2)}, u32[]{:S(2)}) collective-permute-start(bf16[4,2,2,32,128]{4,3,2,1,0:T(8,128)(2,1)S(1)} %get-tuple-element.275), channel_id=1, source_target_pairs={{0,4},{8,0},{16,8},{24,16},{28,24},{20,28},{12,20},{4,12},{1,5},{9... | collective-permute-start | bytes 393224 | tf_op jit(solution)/shard_map/ppermute | solution.py:298
  65.6 1.8 %collective-permute-done.16.refs_41_ = bf16[4,2,2,32,128]{4,3,2,1,0:T(8,128)(2,1)S(1)} collective-permute-done((bf16[4,2,2,32,128]{4,3,2,1,0:T(8,128)(2,1)S(1)}, bf16[4,2,2,32,128]{4,3,2,1,0:T(8,128)(2,1)S(1)}, u32[]{:S(2)}, u32[]{:S(2)}) %collective-permute-start.16) | collective-permute-done | bytes 131104 | tf_op jit(solution)/shard_map/ppermute | solution.py:298
  68.1 1.6 %collective-permute-start.23 = (bf16[4,2,2,32,128]{4,3,2,1,0:T(8,128)(2,1)S(1)}, bf16[4,2,2,32,128]{4,3,2,1,0:T(8,128)(2,1)S(1)}, u32[]{:S(2)}, u32[]{:S(2)}) collective-permute-start(bf16[4,2,2,32,128]{4,3,2,1,0:T(8,128)(2,1)S(1)} %get-tuple-element.269), channel_id=1, source_target_pairs={{0,4},{8,0},{16,8},{24,16},{28,24},{20,28},{12,20},{4,12},{1,5},{9... | collective-permute-start | bytes 393224 | tf_op jit(solution)/shard_map/ppermute | solution.py:298
  71.0 1.6 %collective-permute-start.21 = (bf16[4,2,2,32,128]{4,3,2,1,0:T(8,128)(2,1)S(1)}, bf16[4,2,2,32,128]{4,3,2,1,0:T(8,128)(2,1)S(1)}, u32[]{:S(2)}, u32[]{:S(2)}) collective-permute-start(bf16[4,2,2,32,128]{4,3,2,1,0:T(8,128)(2,1)S(1)} %get-tuple-element.271), channel_id=1, source_target_pairs={{0,4},{8,0},{16,8},{24,16},{28,24},{20,28},{12,20},{4,12},{1,5},{9... | collective-permute-start | bytes 393224 | tf_op jit(solution)/shard_map/ppermute | solution.py:298
  73.0 1.4 collective-permute-done.23.refs_68_
  74.4 1.3 collective-permute-done.20.refs_43_
  76.5 1.2 collective-permute-start.27
  79.3 1.2 collective-permute-start.25
  81.6 1.8 %collective-permute-done.24.refs_45_ = bf16[4,2,2,32,128]{4,3,2,1,0:T(8,128)(2,1)S(1)} collective-permute-done((bf16[4,2,2,32,128]{4,3,2,1,0:T(8,128)(2,1)S(1)}, bf16[4,2,2,32,128]{4,3,2,1,0:T(8,128)(2,1)S(1)}, u32[]{:S(2)}, u32[]{:S(2)}) %collective-permute-start.24) | collective-permute-done | bytes 131104 | tf_op jit(solution)/shard_map/ppermute | solution.py:298
  84.4 1.7 %collective-permute-start.28 = (bf16[4,2,2,32,128]{4,3,2,1,0:T(8,128)(2,1)S(1)}, bf16[4,2,2,32,128]{4,3,2,1,0:T(8,128)(2,1)S(1)}, u32[]{:S(2)}, u32[]{:S(2)}) collective-permute-start(bf16[4,2,2,32,128]{4,3,2,1,0:T(8,128)(2,1)S(1)} %get-tuple-element.262), channel_id=1, source_target_pairs={{0,8},{8,16},{16,24},{24,28},{28,20},{20,12},{12,4},{4,0},{1,9},{9... | collective-permute-start | bytes 393224 | tf_op jit(solution)/shard_map/ppermute | solution.py:298
  87.3 1.7 %collective-permute-start.26 = (bf16[4,2,2,32,128]{4,3,2,1,0:T(8,128)(2,1)S(1)}, bf16[4,2,2,32,128]{4,3,2,1,0:T(8,128)(2,1)}, u32[]{:S(2)}, u32[]{:S(2)}) collective-permute-start(bf16[4,2,2,32,128]{4,3,2,1,0:T(8,128)(2,1)S(1)} %get-tuple-element.264), channel_id=1, source_target_pairs={{0,8},{8,16},{16,24},{24,28},{28,20},{20,12},{12,4},{4,0},{1,9},{9... | collective-permute-start | bytes 393224 | tf_op jit(solution)/shard_map/ppermute | solution.py:298
  91.2 1.8 %collective-permute-start.35 = (bf16[4,2,2,32,128]{4,3,2,1,0:T(8,128)(2,1)S(1)}, bf16[4,2,2,32,128]{4,3,2,1,0:T(8,128)(2,1)}, u32[]{:S(2)}, u32[]{:S(2)}) collective-permute-start(bf16[4,2,2,32,128]{4,3,2,1,0:T(8,128)(2,1)S(1)} %get-tuple-element.257), channel_id=1, source_target_pairs={{0,4},{8,0},{16,8},{24,16},{28,24},{20,28},{12,20},{4,12},{1,5},{9... | collective-permute-start | bytes 393224 | tf_op jit(solution)/shard_map/ppermute | solution.py:298
  94.4 1.8 %collective-permute-start.33 = (bf16[4,2,2,32,128]{4,3,2,1,0:T(8,128)(2,1)S(1)}, bf16[4,2,2,32,128]{4,3,2,1,0:T(8,128)(2,1)S(1)}, u32[]{:S(2)}, u32[]{:S(2)}) collective-permute-start(bf16[4,2,2,32,128]{4,3,2,1,0:T(8,128)(2,1)S(1)} %get-tuple-element.259), channel_id=1, source_target_pairs={{0,4},{8,0},{16,8},{24,16},{28,24},{20,28},{12,20},{4,12},{1,5},{9... | collective-permute-start | bytes 393224 | tf_op jit(solution)/shard_map/ppermute | solution.py:298
  96.5 1.3 collective-permute-done.35.refs_74_
  97.8 1.8 %collective-permute-done.32.refs_49_ = bf16[4,2,2,32,128]{4,3,2,1,0:T(8,128)(2,1)} collective-permute-done((bf16[4,2,2,32,128]{4,3,2,1,0:T(8,128)(2,1)S(1)}, bf16[4,2,2,32,128]{4,3,2,1,0:T(8,128)(2,1)}, u32[]{:S(2)}, u32[]{:S(2)}) %collective-permute-start.32) | collective-permute-done | bytes 131104 | tf_op jit(solution)/shard_map/ppermute | solution.py:298
  101.2 1.7 %collective-permute-start.36 = (bf16[4,2,2,32,128]{4,3,2,1,0:T(8,128)(2,1)S(1)}, bf16[4,2,2,32,128]{4,3,2,1,0:T(8,128)(2,1)S(1)}, u32[]{:S(2)}, u32[]{:S(2)}) collective-permute-start(bf16[4,2,2,32,128]{4,3,2,1,0:T(8,128)(2,1)S(1)} %get-tuple-element.254), channel_id=1, source_target_pairs={{0,8},{8,16},{16,24},{24,28},{28,20},{20,12},{12,4},{4,0},{1,9},{9... | collective-permute-start | bytes 393224 | tf_op jit(solution)/shard_map/ppermute | solution.py:298
  103.3 1.7 %collective-permute-start.34 = (bf16[4,2,2,32,128]{4,3,2,1,0:T(8,128)(2,1)S(1)}, bf16[4,2,2,32,128]{4,3,2,1,0:T(8,128)(2,1)S(1)}, u32[]{:S(2)}, u32[]{:S(2)}) collective-permute-start(bf16[4,2,2,32,128]{4,3,2,1,0:T(8,128)(2,1)S(1)} %get-tuple-element.256), channel_id=1, source_target_pairs={{0,8},{8,16},{16,24},{24,28},{28,20},{20,12},{12,4},{4,0},{1,9},{9... | collective-permute-start | bytes 393224 | tf_op jit(solution)/shard_map/ppermute | solution.py:298
  105.0 2.2 %collective-permute-done.39.refs_76_ = bf16[4,2,2,32,128]{4,3,2,1,0:T(8,128)(2,1)S(1)} collective-permute-done((bf16[4,2,2,32,128]{4,3,2,1,0:T(8,128)(2,1)S(1)}, bf16[4,2,2,32,128]{4,3,2,1,0:T(8,128)(2,1)S(1)}, u32[]{:S(2)}, u32[]{:S(2)}) %collective-permute-start.39) | collective-permute-done | bytes 131104 | tf_op jit(solution)/shard_map/ppermute | solution.py:298
  107.5 2.2 %collective-permute-done.37.refs_75_ = bf16[4,2,2,32,128]{4,3,2,1,0:T(8,128)(2,1)S(1)} collective-permute-done((bf16[4,2,2,32,128]{4,3,2,1,0:T(8,128)(2,1)S(1)}, bf16[4,2,2,32,128]{4,3,2,1,0:T(8,128)(2,1)S(1)}, u32[]{:S(2)}, u32[]{:S(2)}) %collective-permute-start.37) | collective-permute-done | bytes 131104 | tf_op jit(solution)/shard_map/ppermute | solution.py:298
  110.5 1.6 %collective-permute-start.38 = (bf16[4,2,2,32,128]{4,3,2,1,0:T(8,128)(2,1)S(1)}, bf16[4,2,2,32,128]{4,3,2,1,0:T(8,128)(2,1)S(1)}, u32[]{:S(2)}, u32[]{:S(2)}) collective-permute-start(bf16[4,2,2,32,128]{4,3,2,1,0:T(8,128)(2,1)S(1)} %get-tuple-element.252), channel_id=1, source_target_pairs={{0,8},{8,16},{16,24},{24,28},{28,20},{20,12},{12,4},{4,0},{1,9},{9... | collective-permute-start | bytes 393224 | tf_op jit(solution)/shard_map/ppermute | solution.py:298
  112.7 1.6 %collective-permute-start.40 = (bf16[4,2,2,32,128]{4,3,2,1,0:T(8,128)(2,1)S(1)}, bf16[4,2,2,32,128]{4,3,2,1,0:T(8,128)(2,1)S(1)}, u32[]{:S(2)}, u32[]{:S(2)}) collective-permute-start(bf16[4,2,2,32,128]{4,3,2,1,0:T(8,128)(2,1)S(1)} %get-tuple-element.250), channel_id=1, source_target_pairs={{0,8},{8,16},{16,24},{24,28},{28,20},{20,12},{12,4},{4,0},{1,9},{9... | collective-permute-start | bytes 393224 | tf_op jit(solution)/shard_map/ppermute | solution.py:298
  114.2 2.2 %collective-permute-done.41.refs_77_ = bf16[4,2,2,32,128]{4,3,2,1,0:T(8,128)(2,1)S(1)} collective-permute-done((bf16[4,2,2,32,128]{4,3,2,1,0:T(8,128)(2,1)S(1)}, bf16[4,2,2,32,128]{4,3,2,1,0:T(8,128)(2,1)S(1)}, u32[]{:S(2)}, u32[]{:S(2)}) %collective-permute-start.41) | collective-permute-done | bytes 131104 | tf_op jit(solution)/shard_map/ppermute | solution.py:298
  117.4 1.7 %collective-permute-start.42 = (bf16[4,2,2,32,128]{4,3,2,1,0:T(8,128)(2,1)S(1)}, bf16[4,2,2,32,128]{4,3,2,1,0:T(8,128)(2,1)S(1)}, u32[]{:S(2)}, u32[]{:S(2)}) collective-permute-start(bf16[4,2,2,32,128]{4,3,2,1,0:T(8,128)(2,1)S(1)} %get-tuple-element.248), channel_id=1, source_target_pairs={{0,8},{8,16},{16,24},{24,28},{28,20},{20,12},{12,4},{4,0},{1,9},{9... | collective-permute-start | bytes 393224 | tf_op jit(solution)/shard_map/ppermute | solution.py:298
  119.7 1.6 %collective-permute-start.43 = (bf16[4,2,2,32,128]{4,3,2,1,0:T(8,128)(2,1)S(1)}, bf16[4,2,2,32,128]{4,3,2,1,0:T(8,128)(2,1)S(1)}, u32[]{:S(2)}, u32[]{:S(2)}) collective-permute-start(bf16[4,2,2,32,128]{4,3,2,1,0:T(8,128)(2,1)S(1)} %collective-permute-done.40.refs_53_), channel_id=1, source_target_pairs={{0,8},{8,16},{16,24},{24,28},{28,20},{20,12},{12,4},{4,0},{1,9},{9... | collective-permute-start | bytes 393224 | tf_op jit(solution)/shard_map/ppermute | solution.py:298
  121.4 2.0 %collective-permute-done.50.refs_79_ = bf16[4,2,2,32,128]{4,3,2,1,0:T(8,128)(2,1)S(1)} collective-permute-done((bf16[4,2,2,32,128]{4,3,2,1,0:T(8,128)(2,1)S(1)}, bf16[4,2,2,32,128]{4,3,2,1,0:T(8,128)(2,1)S(1)}, u32[]{:S(2)}, u32[]{:S(2)}) %collective-permute-start.50) | collective-permute-done | bytes 131104 | tf_op jit(solution)/shard_map/ppermute | solution.py:298
  123.7 1.7 %collective-permute-start.44 = (bf16[4,2,2,32,128]{4,3,2,1,0:T(8,128)(2,1)S(1)}, bf16[4,2,2,32,128]{4,3,2,1,0:T(8,128)(2,1)S(1)}, u32[]{:S(2)}, u32[]{:S(2)}) collective-permute-start(bf16[4,2,2,32,128]{4,3,2,1,0:T(8,128)(2,1)S(1)} %collective-permute-done.42.refs_54_), channel_id=1, source_target_pairs={{0,8},{8,16},{16,24},{24,28},{28,20},{20,12},{12,4},{4,0},{1,9},{9... | collective-permute-start | bytes 393224 | tf_op jit(solution)/shard_map/ppermute | solution.py:298
  126.4 1.6 %collective-permute-start.45 = (bf16[4,2,2,32,128]{4,3,2,1,0:T(8,128)(2,1)S(1)}, bf16[4,2,2,32,128]{4,3,2,1,0:T(8,128)(2,1)S(1)}, u32[]{:S(2)}, u32[]{:S(2)}) collective-permute-start(bf16[4,2,2,32,128]{4,3,2,1,0:T(8,128)(2,1)S(1)} %collective-permute-done.43.refs_55_), channel_id=1, source_target_pairs={{0,8},{8,16},{16,24},{24,28},{28,20},{20,12},{12,4},{4,0},{1,9},{9... | collective-permute-start | bytes 393224 | tf_op jit(solution)/shard_map/ppermute | solution.py:298
  128.7 1.7 %collective-permute-start.46 = (bf16[4,2,2,32,128]{4,3,2,1,0:T(8,128)(2,1)S(1)}, bf16[4,2,2,32,128]{4,3,2,1,0:T(8,128)(2,1)S(1)}, u32[]{:S(2)}, u32[]{:S(2)}) collective-permute-start(bf16[4,2,2,32,128]{4,3,2,1,0:T(8,128)(2,1)S(1)} %collective-permute-done.44.refs_56_), channel_id=1, source_target_pairs={{0,8},{8,16},{16,24},{24,28},{28,20},{20,12},{12,4},{4,0},{1,9},{9... | collective-permute-start | bytes 393224 | tf_op jit(solution)/shard_map/ppermute | solution.py:298
  131.4 1.6 %collective-permute-start.47 = (bf16[4,2,2,32,128]{4,3,2,1,0:T(8,128)(2,1)S(1)}, bf16[4,2,2,32,128]{4,3,2,1,0:T(8,128)(2,1)S(1)}, u32[]{:S(2)}, u32[]{:S(2)}) collective-permute-start(bf16[4,2,2,32,128]{4,3,2,1,0:T(8,128)(2,1)S(1)} %collective-permute-done.45.refs_57_), channel_id=1, source_target_pairs={{0,8},{8,16},{16,24},{24,28},{28,20},{20,12},{12,4},{4,0},{1,9},{9... | collective-permute-start | bytes 393224 | tf_op jit(solution)/shard_map/ppermute | solution.py:298
  133.7 1.7 %collective-permute-start.48 = (bf16[4,2,2,32,128]{4,3,2,1,0:T(8,128)(2,1)S(1)}, bf16[4,2,2,32,128]{4,3,2,1,0:T(8,128)(2,1)S(1)}, u32[]{:S(2)}, u32[]{:S(2)}) collective-permute-start(bf16[4,2,2,32,128]{4,3,2,1,0:T(8,128)(2,1)S(1)} %collective-permute-done.46.refs_58_), channel_id=1, source_target_pairs={{0,8},{8,16},{16,24},{24,28},{28,20},{20,12},{12,4},{4,0},{1,9},{9... | collective-permute-start | bytes 393224 | tf_op jit(solution)/shard_map/ppermute | solution.py:298
  136.3 1.9 %collective-permute-done.56.refs_85_ = bf16[4,2,2,32,128]{4,3,2,1,0:T(8,128)(2,1)S(1)} collective-permute-done((bf16[4,2,2,32,128]{4,3,2,1,0:T(8,128)(2,1)S(1)}, bf16[4,2,2,32,128]{4,3,2,1,0:T(8,128)(2,1)S(1)}, u32[]{:S(2)}, u32[]{:S(2)}) %collective-permute-start.56) | collective-permute-done | bytes 131104 | tf_op jit(solution)/shard_map/ppermute | solution.py:298
  139.3 9.4 %cross.1 = bf16[4,2,2,512,256]{4,3,2,1,0:T(8,128)(2,1)} custom-call(s32[4]{0:T(128)} %block_ref.1, bf16[2,2,512,128]{3,2,1,0:T(8,128)(2,1)} %get-tuple-element.126.refs_0_, bf16[2,2,512,128]{3,2,1,0:T(8,128)(2,1)} %get-tuple-element.127.refs_1_, bf16[2,2,512,128]{3,2,1,0:T(8,128)(2,1)} %get-tuple-element.128.refs_2_, ...), custom_call_target="tpu_custom_call" | custom-call | tf_op jit(solution)/shard_map/cross/pallas_call | solution.py:301
  (319 shorter events, 41.1 us)
Async XLA Ops:
  4.7 7.1 %collective-permute-start.1 = (f32[288,128]{1,0:T(8,128)S(1)}, f32[288,128]{1,0:T(8,128)S(1)}, u32[]{:S(2)}, u32[]{:S(2)}) collective-permute-start(f32[288,128]{1,0:T(8,128)S(1)} %slice.26.p_ref), channel_id=1, source_target_pairs={{0,2},{1,3},{2,0},{3,1},{4,6},{5,7},{6,4},{7,5},{8,10},{9,11},{10,... | collective-permute-start | bytes 442376 | tf_op jit(solution)/shard_map/ppermute | solution.py:206
  14.4 6.1 %collective-permute-start.4 = (f32[256,128]{1,0:T(8,128)}, f32[256,128]{1,0:T(8,128)S(1)}, u32[]{:S(2)}, u32[]{:S(2)}) collective-permute-start(f32[256,128]{1,0:T(8,128)} %scale.2.mine_ref), channel_id=1, source_target_pairs={{0,1},{1,0},{2,3},{3,2},{4,5},{5,4},{6,7},{7,6},{8,9},{9,8},{10,11... | collective-permute-start | bytes 393224 | tf_op jit(solution)/shard_map/ppermute | solution.py:206
  24.1 11.6 %collective-permute-start.7 = (bf16[4,2,2,32,128]{4,3,2,1,0:T(8,128)(2,1)S(1)}, bf16[4,2,2,32,128]{4,3,2,1,0:T(8,128)(2,1)S(1)}, u32[]{:S(2)}, u32[]{:S(2)}) collective-permute-start(bf16[4,2,2,32,128]{4,3,2,1,0:T(8,128)(2,1)S(1)} %get-tuple-element.130.refs_4_), channel_id=1, source_target_pairs={{0,8},{8,16},{16,24},{24,28},{28,20},{20,12},{12,4},{4,0},{1,9},{9... | collective-permute-start | bytes 393224 | tf_op jit(solution)/shard_map/ppermute | solution.py:298
  26.4 9.4 %collective-permute-start.8 = (bf16[4,2,2,32,128]{4,3,2,1,0:T(8,128)(2,1)S(1)}, bf16[4,2,2,32,128]{4,3,2,1,0:T(8,128)(2,1)S(1)}, u32[]{:S(2)}, u32[]{:S(2)}) collective-permute-start(bf16[4,2,2,32,128]{4,3,2,1,0:T(8,128)(2,1)S(1)} %get-tuple-element.131.refs_5_), channel_id=1, source_target_pairs={{0,8},{8,16},{16,24},{24,28},{28,20},{20,12},{12,4},{4,0},{1,9},{9... | collective-permute-start | bytes 393224 | tf_op jit(solution)/shard_map/ppermute | solution.py:298
  28.0 7.8 %collective-permute-start.9 = (bf16[4,2,2,32,128]{4,3,2,1,0:T(8,128)(2,1)S(1)}, bf16[4,2,2,32,128]{4,3,2,1,0:T(8,128)(2,1)S(1)}, u32[]{:S(2)}, u32[]{:S(2)}) collective-permute-start(bf16[4,2,2,32,128]{4,3,2,1,0:T(8,128)(2,1)S(1)} %get-tuple-element.146.refs_20_), channel_id=1, source_target_pairs={{0,4},{8,0},{16,8},{24,16},{28,24},{20,28},{12,20},{4,12},{1,5},{9... | collective-permute-start | bytes 393224 | tf_op jit(solution)/shard_map/ppermute | solution.py:298
  28.4 7.6 %collective-permute-start.11 = (bf16[4,2,2,32,128]{4,3,2,1,0:T(8,128)(2,1)S(1)}, bf16[4,2,2,32,128]{4,3,2,1,0:T(8,128)(2,1)S(1)}, u32[]{:S(2)}, u32[]{:S(2)}) collective-permute-start(bf16[4,2,2,32,128]{4,3,2,1,0:T(8,128)(2,1)S(1)} %get-tuple-element.147.refs_21_), channel_id=1, source_target_pairs={{0,4},{8,0},{16,8},{24,16},{28,24},{20,28},{12,20},{4,12},{1,5},{9... | collective-permute-start | bytes 393224 | tf_op jit(solution)/shard_map/ppermute | solution.py:298
  34.2 11.7 %collective-permute-start.5 = (f32[288,384]{1,0:T(8,128)S(1)}, f32[288,384]{1,0:T(8,128)S(1)}, u32[]{:S(2)}, u32[]{:S(2)}) collective-permute-start(f32[288,384]{1,0:T(8,128)S(1)} %slice.29.p_ref), channel_id=1, source_target_pairs={{0,2},{1,3},{2,0},{3,1},{4,6},{5,7},{6,4},{7,5},{8,10},{9,11},{10,... | collective-permute-start | bytes 1327112 | tf_op jit(solution)/shard_map/ppermute | solution.py:206
  36.8 20.4 %collective-permute-start.13 = (bf16[4,2,2,32,128]{4,3,2,1,0:T(8,128)(2,1)}, bf16[4,2,2,32,128]{4,3,2,1,0:T(8,128)(2,1)}, u32[]{:S(2)}, u32[]{:S(2)}) collective-permute-start(bf16[4,2,2,32,128]{4,3,2,1,0:T(8,128)(2,1)} %get-tuple-element.279), channel_id=1, source_target_pairs={{0,4},{8,0},{16,8},{24,16},{28,24},{20,28},{12,20},{4,12},{1,5},{9... | collective-permute-start | bytes 393224 | tf_op jit(solution)/shard_map/ppermute | solution.py:298
  38.6 18.6 %collective-permute-start.10 = (bf16[4,2,2,32,128]{4,3,2,1,0:T(8,128)(2,1)}, bf16[4,2,2,32,128]{4,3,2,1,0:T(8,128)(2,1)}, u32[]{:S(2)}, u32[]{:S(2)}) collective-permute-start(bf16[4,2,2,32,128]{4,3,2,1,0:T(8,128)(2,1)} %get-tuple-element.280), channel_id=1, source_target_pairs={{0,8},{8,16},{16,24},{24,28},{28,20},{20,12},{12,4},{4,0},{1,9},{9... | collective-permute-start | bytes 393224 | tf_op jit(solution)/shard_map/ppermute | solution.py:298
  50.8 7.0 %collective-permute-start.15 = (bf16[4,2,2,32,128]{4,3,2,1,0:T(8,128)(2,1)}, bf16[4,2,2,32,128]{4,3,2,1,0:T(8,128)(2,1)}, u32[]{:S(2)}, u32[]{:S(2)}) collective-permute-start(bf16[4,2,2,32,128]{4,3,2,1,0:T(8,128)(2,1)} %get-tuple-element.277), channel_id=1, source_target_pairs={{0,4},{8,0},{16,8},{24,16},{28,24},{20,28},{12,20},{4,12},{1,5},{9... | collective-permute-start | bytes 393224 | tf_op jit(solution)/shard_map/ppermute | solution.py:298
  52.5 5.9 %collective-permute-start.12 = (bf16[4,2,2,32,128]{4,3,2,1,0:T(8,128)(2,1)}, bf16[4,2,2,32,128]{4,3,2,1,0:T(8,128)(2,1)}, u32[]{:S(2)}, u32[]{:S(2)}) collective-permute-start(bf16[4,2,2,32,128]{4,3,2,1,0:T(8,128)(2,1)} %get-tuple-element.278), channel_id=1, source_target_pairs={{0,8},{8,16},{16,24},{24,28},{28,20},{20,12},{12,4},{4,0},{1,9},{9... | collective-permute-start | bytes 393224 | tf_op jit(solution)/shard_map/ppermute | solution.py:298
  60.1 5.5 %collective-permute-start.19 = (bf16[4,2,2,32,128]{4,3,2,1,0:T(8,128)(2,1)S(1)}, bf16[4,2,2,32,128]{4,3,2,1,0:T(8,128)(2,1)S(1)}, u32[]{:S(2)}, u32[]{:S(2)}) collective-permute-start(bf16[4,2,2,32,128]{4,3,2,1,0:T(8,128)(2,1)S(1)} %get-tuple-element.273), channel_id=1, source_target_pairs={{0,4},{8,0},{16,8},{24,16},{28,24},{20,28},{12,20},{4,12},{1,5},{9... | collective-permute-start | bytes 393224 | tf_op jit(solution)/shard_map/ppermute | solution.py:298
  61.8 5.6 %collective-permute-start.16 = (bf16[4,2,2,32,128]{4,3,2,1,0:T(8,128)(2,1)S(1)}, bf16[4,2,2,32,128]{4,3,2,1,0:T(8,128)(2,1)S(1)}, u32[]{:S(2)}, u32[]{:S(2)}) collective-permute-start(bf16[4,2,2,32,128]{4,3,2,1,0:T(8,128)(2,1)S(1)} %get-tuple-element.274), channel_id=1, source_target_pairs={{0,8},{8,16},{16,24},{24,28},{28,20},{20,12},{12,4},{4,0},{1,9},{9... | collective-permute-start | bytes 393224 | tf_op jit(solution)/shard_map/ppermute | solution.py:298
  63.3 7.0 %collective-permute-start.17 = (bf16[4,2,2,32,128]{4,3,2,1,0:T(8,128)(2,1)S(1)}, bf16[4,2,2,32,128]{4,3,2,1,0:T(8,128)(2,1)S(1)}, u32[]{:S(2)}, u32[]{:S(2)}) collective-permute-start(bf16[4,2,2,32,128]{4,3,2,1,0:T(8,128)(2,1)S(1)} %get-tuple-element.275), channel_id=1, source_target_pairs={{0,4},{8,0},{16,8},{24,16},{28,24},{20,28},{12,20},{4,12},{1,5},{9... | collective-permute-start | bytes 393224 | tf_op jit(solution)/shard_map/ppermute | solution.py:298
  64.9 5.3 %collective-permute-start.14 = (bf16[4,2,2,32,128]{4,3,2,1,0:T(8,128)(2,1)S(1)}, bf16[4,2,2,32,128]{4,3,2,1,0:T(8,128)(2,1)S(1)}, u32[]{:S(2)}, u32[]{:S(2)}) collective-permute-start(bf16[4,2,2,32,128]{4,3,2,1,0:T(8,128)(2,1)S(1)} %get-tuple-element.276), channel_id=1, source_target_pairs={{0,8},{8,16},{16,24},{24,28},{28,20},{20,12},{12,4},{4,0},{1,9},{9... | collective-permute-start | bytes 393224 | tf_op jit(solution)/shard_map/ppermute | solution.py:298
  68.1 6.3 %collective-permute-start.23 = (bf16[4,2,2,32,128]{4,3,2,1,0:T(8,128)(2,1)S(1)}, bf16[4,2,2,32,128]{4,3,2,1,0:T(8,128)(2,1)S(1)}, u32[]{:S(2)}, u32[]{:S(2)}) collective-permute-start(bf16[4,2,2,32,128]{4,3,2,1,0:T(8,128)(2,1)S(1)} %get-tuple-element.269), channel_id=1, source_target_pairs={{0,4},{8,0},{16,8},{24,16},{28,24},{20,28},{12,20},{4,12},{1,5},{9... | collective-permute-start | bytes 393224 | tf_op jit(solution)/shard_map/ppermute | solution.py:298
  69.8 6.0 %collective-permute-start.20 = (bf16[4,2,2,32,128]{4,3,2,1,0:T(8,128)(2,1)S(1)}, bf16[4,2,2,32,128]{4,3,2,1,0:T(8,128)(2,1)S(1)}, u32[]{:S(2)}, u32[]{:S(2)}) collective-permute-start(bf16[4,2,2,32,128]{4,3,2,1,0:T(8,128)(2,1)S(1)} %get-tuple-element.270), channel_id=1, source_target_pairs={{0,8},{8,16},{16,24},{24,28},{28,20},{20,12},{12,4},{4,0},{1,9},{9... | collective-permute-start | bytes 393224 | tf_op jit(solution)/shard_map/ppermute | solution.py:298
  71.0 7.6 %collective-permute-start.21 = (bf16[4,2,2,32,128]{4,3,2,1,0:T(8,128)(2,1)S(1)}, bf16[4,2,2,32,128]{4,3,2,1,0:T(8,128)(2,1)S(1)}, u32[]{:S(2)}, u32[]{:S(2)}) collective-permute-start(bf16[4,2,2,32,128]{4,3,2,1,0:T(8,128)(2,1)S(1)} %get-tuple-element.271), channel_id=1, source_target_pairs={{0,4},{8,0},{16,8},{24,16},{28,24},{20,28},{12,20},{4,12},{1,5},{9... | collective-permute-start | bytes 393224 | tf_op jit(solution)/shard_map/ppermute | solution.py:298
  72.6 6.0 %collective-permute-start.18 = (bf16[4,2,2,32,128]{4,3,2,1,0:T(8,128)(2,1)S(1)}, bf16[4,2,2,32,128]{4,3,2,1,0:T(8,128)(2,1)S(1)}, u32[]{:S(2)}, u32[]{:S(2)}) collective-permute-start(bf16[4,2,2,32,128]{4,3,2,1,0:T(8,128)(2,1)S(1)} %get-tuple-element.272), channel_id=1, source_target_pairs={{0,8},{8,16},{16,24},{24,28},{28,20},{20,12},{12,4},{4,0},{1,9},{9... | collective-permute-start | bytes 393224 | tf_op jit(solution)/shard_map/ppermute | solution.py:298
  76.5 5.2 %collective-permute-start.27 = (bf16[4,2,2,32,128]{4,3,2,1,0:T(8,128)(2,1)S(1)}, bf16[4,2,2,32,128]{4,3,2,1,0:T(8,128)(2,1)S(1)}, u32[]{:S(2)}, u32[]{:S(2)}) collective-permute-start(bf16[4,2,2,32,128]{4,3,2,1,0:T(8,128)(2,1)S(1)} %get-tuple-element.265), channel_id=1, source_target_pairs={{0,4},{8,0},{16,8},{24,16},{28,24},{20,28},{12,20},{4,12},{1,5},{9... | collective-permute-start | bytes 393224 | tf_op jit(solution)/shard_map/ppermute | solution.py:298
  77.7 5.7 %collective-permute-start.24 = (bf16[4,2,2,32,128]{4,3,2,1,0:T(8,128)(2,1)S(1)}, bf16[4,2,2,32,128]{4,3,2,1,0:T(8,128)(2,1)S(1)}, u32[]{:S(2)}, u32[]{:S(2)}) collective-permute-start(bf16[4,2,2,32,128]{4,3,2,1,0:T(8,128)(2,1)S(1)} %get-tuple-element.266), channel_id=1, source_target_pairs={{0,8},{8,16},{16,24},{24,28},{28,20},{20,12},{12,4},{4,0},{1,9},{9... | collective-permute-start | bytes 393224 | tf_op jit(solution)/shard_map/ppermute | solution.py:298
  79.3 6.9 %collective-permute-start.25 = (bf16[4,2,2,32,128]{4,3,2,1,0:T(8,128)(2,1)S(1)}, bf16[4,2,2,32,128]{4,3,2,1,0:T(8,128)(2,1)S(1)}, u32[]{:S(2)}, u32[]{:S(2)}) collective-permute-start(bf16[4,2,2,32,128]{4,3,2,1,0:T(8,128)(2,1)S(1)} %get-tuple-element.267), channel_id=1, source_target_pairs={{0,4},{8,0},{16,8},{24,16},{28,24},{20,28},{12,20},{4,12},{1,5},{9... | collective-permute-start | bytes 393224 | tf_op jit(solution)/shard_map/ppermute | solution.py:298
  80.5 5.6 %collective-permute-start.22 = (bf16[4,2,2,32,128]{4,3,2,1,0:T(8,128)(2,1)S(1)}, bf16[4,2,2,32,128]{4,3,2,1,0:T(8,128)(2,1)S(1)}, u32[]{:S(2)}, u32[]{:S(2)}) collective-permute-start(bf16[4,2,2,32,128]{4,3,2,1,0:T(8,128)(2,1)S(1)} %get-tuple-element.268), channel_id=1, source_target_pairs={{0,8},{8,16},{16,24},{24,28},{28,20},{20,12},{12,4},{4,0},{1,9},{9... | collective-permute-start | bytes 393224 | tf_op jit(solution)/shard_map/ppermute | solution.py:298
  84.1 6.2 %collective-permute-start.31 = (bf16[4,2,2,32,128]{4,3,2,1,0:T(8,128)(2,1)S(1)}, bf16[4,2,2,32,128]{4,3,2,1,0:T(8,128)(2,1)S(1)}, u32[]{:S(2)}, u32[]{:S(2)}) collective-permute-start(bf16[4,2,2,32,128]{4,3,2,1,0:T(8,128)(2,1)S(1)} %get-tuple-element.261), channel_id=1, source_target_pairs={{0,4},{8,0},{16,8},{24,16},{28,24},{20,28},{12,20},{4,12},{1,5},{9... | collective-permute-start | bytes 393224 | tf_op jit(solution)/shard_map/ppermute | solution.py:298
  84.4 6.1 %collective-permute-start.28 = (bf16[4,2,2,32,128]{4,3,2,1,0:T(8,128)(2,1)S(1)}, bf16[4,2,2,32,128]{4,3,2,1,0:T(8,128)(2,1)S(1)}, u32[]{:S(2)}, u32[]{:S(2)}) collective-permute-start(bf16[4,2,2,32,128]{4,3,2,1,0:T(8,128)(2,1)S(1)} %get-tuple-element.262), channel_id=1, source_target_pairs={{0,8},{8,16},{16,24},{24,28},{28,20},{20,12},{12,4},{4,0},{1,9},{9... | collective-permute-start | bytes 393224 | tf_op jit(solution)/shard_map/ppermute | solution.py:298
  86.9 6.4 %collective-permute-start.29 = (bf16[4,2,2,32,128]{4,3,2,1,0:T(8,128)(2,1)S(1)}, bf16[4,2,2,32,128]{4,3,2,1,0:T(8,128)(2,1)S(1)}, u32[]{:S(2)}, u32[]{:S(2)}) collective-permute-start(bf16[4,2,2,32,128]{4,3,2,1,0:T(8,128)(2,1)S(1)} %get-tuple-element.263), channel_id=1, source_target_pairs={{0,4},{8,0},{16,8},{24,16},{28,24},{20,28},{12,20},{4,12},{1,5},{9... | collective-permute-start | bytes 393224 | tf_op jit(solution)/shard_map/ppermute | solution.py:298
  87.3 6.1 %collective-permute-start.26 = (bf16[4,2,2,32,128]{4,3,2,1,0:T(8,128)(2,1)S(1)}, bf16[4,2,2,32,128]{4,3,2,1,0:T(8,128)(2,1)}, u32[]{:S(2)}, u32[]{:S(2)}) collective-permute-start(bf16[4,2,2,32,128]{4,3,2,1,0:T(8,128)(2,1)S(1)} %get-tuple-element.264), channel_id=1, source_target_pairs={{0,8},{8,16},{16,24},{24,28},{28,20},{20,12},{12,4},{4,0},{1,9},{9... | collective-permute-start | bytes 393224 | tf_op jit(solution)/shard_map/ppermute | solution.py:298
  91.2 6.5 %collective-permute-start.35 = (bf16[4,2,2,32,128]{4,3,2,1,0:T(8,128)(2,1)S(1)}, bf16[4,2,2,32,128]{4,3,2,1,0:T(8,128)(2,1)}, u32[]{:S(2)}, u32[]{:S(2)}) collective-permute-start(bf16[4,2,2,32,128]{4,3,2,1,0:T(8,128)(2,1)S(1)} %get-tuple-element.257), channel_id=1, source_target_pairs={{0,4},{8,0},{16,8},{24,16},{28,24},{20,28},{12,20},{4,12},{1,5},{9... | collective-permute-start | bytes 393224 | tf_op jit(solution)/shard_map/ppermute | solution.py:298
  93.1 6.5 %collective-permute-start.32 = (bf16[4,2,2,32,128]{4,3,2,1,0:T(8,128)(2,1)S(1)}, bf16[4,2,2,32,128]{4,3,2,1,0:T(8,128)(2,1)}, u32[]{:S(2)}, u32[]{:S(2)}) collective-permute-start(bf16[4,2,2,32,128]{4,3,2,1,0:T(8,128)(2,1)S(1)} %get-tuple-element.258), channel_id=1, source_target_pairs={{0,8},{8,16},{16,24},{24,28},{28,20},{20,12},{12,4},{4,0},{1,9},{9... | collective-permute-start | bytes 393224 | tf_op jit(solution)/shard_map/ppermute | solution.py:298
  94.4 8.5 %collective-permute-start.33 = (bf16[4,2,2,32,128]{4,3,2,1,0:T(8,128)(2,1)S(1)}, bf16[4,2,2,32,128]{4,3,2,1,0:T(8,128)(2,1)S(1)}, u32[]{:S(2)}, u32[]{:S(2)}) collective-permute-start(bf16[4,2,2,32,128]{4,3,2,1,0:T(8,128)(2,1)S(1)} %get-tuple-element.259), channel_id=1, source_target_pairs={{0,4},{8,0},{16,8},{24,16},{28,24},{20,28},{12,20},{4,12},{1,5},{9... | collective-permute-start | bytes 393224 | tf_op jit(solution)/shard_map/ppermute | solution.py:298
  96.2 6.6 %collective-permute-start.30 = (bf16[4,2,2,32,128]{4,3,2,1,0:T(8,128)(2,1)S(1)}, bf16[4,2,2,32,128]{4,3,2,1,0:T(8,128)(2,1)S(1)}, u32[]{:S(2)}, u32[]{:S(2)}) collective-permute-start(bf16[4,2,2,32,128]{4,3,2,1,0:T(8,128)(2,1)S(1)} %get-tuple-element.260), channel_id=1, source_target_pairs={{0,8},{8,16},{16,24},{24,28},{28,20},{20,12},{12,4},{4,0},{1,9},{9... | collective-permute-start | bytes 393224 | tf_op jit(solution)/shard_map/ppermute | solution.py:298
  100.8 6.4 %collective-permute-start.39 = (bf16[4,2,2,32,128]{4,3,2,1,0:T(8,128)(2,1)S(1)}, bf16[4,2,2,32,128]{4,3,2,1,0:T(8,128)(2,1)S(1)}, u32[]{:S(2)}, u32[]{:S(2)}) collective-permute-start(bf16[4,2,2,32,128]{4,3,2,1,0:T(8,128)(2,1)S(1)} %get-tuple-element.253), channel_id=1, source_target_pairs={{0,4},{8,0},{16,8},{24,16},{28,24},{20,28},{12,20},{4,12},{1,5},{9... | collective-permute-start | bytes 393224 | tf_op jit(solution)/shard_map/ppermute | solution.py:298
  101.2 6.4 %collective-permute-start.36 = (bf16[4,2,2,32,128]{4,3,2,1,0:T(8,128)(2,1)S(1)}, bf16[4,2,2,32,128]{4,3,2,1,0:T(8,128)(2,1)S(1)}, u32[]{:S(2)}, u32[]{:S(2)}) collective-permute-start(bf16[4,2,2,32,128]{4,3,2,1,0:T(8,128)(2,1)S(1)} %get-tuple-element.254), channel_id=1, source_target_pairs={{0,8},{8,16},{16,24},{24,28},{28,20},{20,12},{12,4},{4,0},{1,9},{9... | collective-permute-start | bytes 393224 | tf_op jit(solution)/shard_map/ppermute | solution.py:298
  102.9 6.8 %collective-permute-start.37 = (bf16[4,2,2,32,128]{4,3,2,1,0:T(8,128)(2,1)S(1)}, bf16[4,2,2,32,128]{4,3,2,1,0:T(8,128)(2,1)S(1)}, u32[]{:S(2)}, u32[]{:S(2)}) collective-permute-start(bf16[4,2,2,32,128]{4,3,2,1,0:T(8,128)(2,1)S(1)} %get-tuple-element.255), channel_id=1, source_target_pairs={{0,4},{8,0},{16,8},{24,16},{28,24},{20,28},{12,20},{4,12},{1,5},{9... | collective-permute-start | bytes 393224 | tf_op jit(solution)/shard_map/ppermute | solution.py:298
  103.3 6.7 %collective-permute-start.34 = (bf16[4,2,2,32,128]{4,3,2,1,0:T(8,128)(2,1)S(1)}, bf16[4,2,2,32,128]{4,3,2,1,0:T(8,128)(2,1)S(1)}, u32[]{:S(2)}, u32[]{:S(2)}) collective-permute-start(bf16[4,2,2,32,128]{4,3,2,1,0:T(8,128)(2,1)S(1)} %get-tuple-element.256), channel_id=1, source_target_pairs={{0,8},{8,16},{16,24},{24,28},{28,20},{20,12},{12,4},{4,0},{1,9},{9... | collective-permute-start | bytes 393224 | tf_op jit(solution)/shard_map/ppermute | solution.py:298
  110.0 6.4 %collective-permute-start.41 = (bf16[4,2,2,32,128]{4,3,2,1,0:T(8,128)(2,1)S(1)}, bf16[4,2,2,32,128]{4,3,2,1,0:T(8,128)(2,1)S(1)}, u32[]{:S(2)}, u32[]{:S(2)}) collective-permute-start(bf16[4,2,2,32,128]{4,3,2,1,0:T(8,128)(2,1)S(1)} %get-tuple-element.251), channel_id=1, source_target_pairs={{0,4},{8,0},{16,8},{24,16},{28,24},{20,28},{12,20},{4,12},{1,5},{9... | collective-permute-start | bytes 393224 | tf_op jit(solution)/shard_map/ppermute | solution.py:298
  110.5 6.3 %collective-permute-start.38 = (bf16[4,2,2,32,128]{4,3,2,1,0:T(8,128)(2,1)S(1)}, bf16[4,2,2,32,128]{4,3,2,1,0:T(8,128)(2,1)S(1)}, u32[]{:S(2)}, u32[]{:S(2)}) collective-permute-start(bf16[4,2,2,32,128]{4,3,2,1,0:T(8,128)(2,1)S(1)} %get-tuple-element.252), channel_id=1, source_target_pairs={{0,8},{8,16},{16,24},{24,28},{28,20},{20,12},{12,4},{4,0},{1,9},{9... | collective-permute-start | bytes 393224 | tf_op jit(solution)/shard_map/ppermute | solution.py:298
  112.2 7.1 %collective-permute-start.49 = (bf16[4,2,2,32,128]{4,3,2,1,0:T(8,128)(2,1)S(1)}, bf16[4,2,2,32,128]{4,3,2,1,0:T(8,128)(2,1)S(1)}, u32[]{:S(2)}, u32[]{:S(2)}) collective-permute-start(bf16[4,2,2,32,128]{4,3,2,1,0:T(8,128)(2,1)S(1)} %get-tuple-element.249), channel_id=1, source_target_pairs={{0,4},{8,0},{16,8},{24,16},{28,24},{20,28},{12,20},{4,12},{1,5},{9... | collective-permute-start | bytes 393224 | tf_op jit(solution)/shard_map/ppermute | solution.py:298
  112.7 7.1 %collective-permute-start.40 = (bf16[4,2,2,32,128]{4,3,2,1,0:T(8,128)(2,1)S(1)}, bf16[4,2,2,32,128]{4,3,2,1,0:T(8,128)(2,1)S(1)}, u32[]{:S(2)}, u32[]{:S(2)}) collective-permute-start(bf16[4,2,2,32,128]{4,3,2,1,0:T(8,128)(2,1)S(1)} %get-tuple-element.250), channel_id=1, source_target_pairs={{0,8},{8,16},{16,24},{24,28},{28,20},{20,12},{12,4},{4,0},{1,9},{9... | collective-permute-start | bytes 393224 | tf_op jit(solution)/shard_map/ppermute | solution.py:298
  116.9 6.4 %collective-permute-start.50 = (bf16[4,2,2,32,128]{4,3,2,1,0:T(8,128)(2,1)S(1)}, bf16[4,2,2,32,128]{4,3,2,1,0:T(8,128)(2,1)S(1)}, u32[]{:S(2)}, u32[]{:S(2)}) collective-permute-start(bf16[4,2,2,32,128]{4,3,2,1,0:T(8,128)(2,1)S(1)} %get-tuple-element.247), channel_id=1, source_target_pairs={{0,4},{8,0},{16,8},{24,16},{28,24},{20,28},{12,20},{4,12},{1,5},{9... | collective-permute-start | bytes 393224 | tf_op jit(solution)/shard_map/ppermute | solution.py:298
  117.4 6.4 %collective-permute-start.42 = (bf16[4,2,2,32,128]{4,3,2,1,0:T(8,128)(2,1)S(1)}, bf16[4,2,2,32,128]{4,3,2,1,0:T(8,128)(2,1)S(1)}, u32[]{:S(2)}, u32[]{:S(2)}) collective-permute-start(bf16[4,2,2,32,128]{4,3,2,1,0:T(8,128)(2,1)S(1)} %get-tuple-element.248), channel_id=1, source_target_pairs={{0,8},{8,16},{16,24},{24,28},{28,20},{20,12},{12,4},{4,0},{1,9},{9... | collective-permute-start | bytes 393224 | tf_op jit(solution)/shard_map/ppermute | solution.py:298
  119.3 6.7 %collective-permute-start.51 = (bf16[4,2,2,32,128]{4,3,2,1,0:T(8,128)(2,1)S(1)}, bf16[4,2,2,32,128]{4,3,2,1,0:T(8,128)(2,1)S(1)}, u32[]{:S(2)}, u32[]{:S(2)}) collective-permute-start(bf16[4,2,2,32,128]{4,3,2,1,0:T(8,128)(2,1)S(1)} %collective-permute-done.49.refs_78_), channel_id=1, source_target_pairs={{0,4},{8,0},{16,8},{24,16},{28,24},{20,28},{12,20},{4,12},{1,5},{9... | collective-permute-start | bytes 393224 | tf_op jit(solution)/shard_map/ppermute | solution.py:298
  119.7 6.7 %collective-permute-start.43 = (bf16[4,2,2,32,128]{4,3,2,1,0:T(8,128)(2,1)S(1)}, bf16[4,2,2,32,128]{4,3,2,1,0:T(8,128)(2,1)S(1)}, u32[]{:S(2)}, u32[]{:S(2)}) collective-permute-start(bf16[4,2,2,32,128]{4,3,2,1,0:T(8,128)(2,1)S(1)} %collective-permute-done.40.refs_53_), channel_id=1, source_target_pairs={{0,8},{8,16},{16,24},{24,28},{28,20},{20,12},{12,4},{4,0},{1,9},{9... | collective-permute-start | bytes 393224 | tf_op jit(solution)/shard_map/ppermute | solution.py:298
  123.4 5.0 %collective-permute-start.52 = (bf16[4,2,2,32,128]{4,3,2,1,0:T(8,128)(2,1)S(1)}, bf16[4,2,2,32,128]{4,3,2,1,0:T(8,128)(2,1)S(1)}, u32[]{:S(2)}, u32[]{:S(2)}) collective-permute-start(bf16[4,2,2,32,128]{4,3,2,1,0:T(8,128)(2,1)S(1)} %collective-permute-done.50.refs_79_), channel_id=1, source_target_pairs={{0,4},{8,0},{16,8},{24,16},{28,24},{20,28},{12,20},{4,12},{1,5},{9... | collective-permute-start | bytes 393224 | tf_op jit(solution)/shard_map/ppermute | solution.py:298
  123.7 5.0 %collective-permute-start.44 = (bf16[4,2,2,32,128]{4,3,2,1,0:T(8,128)(2,1)S(1)}, bf16[4,2,2,32,128]{4,3,2,1,0:T(8,128)(2,1)S(1)}, u32[]{:S(2)}, u32[]{:S(2)}) collective-permute-start(bf16[4,2,2,32,128]{4,3,2,1,0:T(8,128)(2,1)S(1)} %collective-permute-done.42.refs_54_), channel_id=1, source_target_pairs={{0,8},{8,16},{16,24},{24,28},{28,20},{20,12},{12,4},{4,0},{1,9},{9... | collective-permute-start | bytes 393224 | tf_op jit(solution)/shard_map/ppermute | solution.py:298
  126.0 5.0 %collective-permute-start.53 = (bf16[4,2,2,32,128]{4,3,2,1,0:T(8,128)(2,1)S(1)}, bf16[4,2,2,32,128]{4,3,2,1,0:T(8,128)(2,1)S(1)}, u32[]{:S(2)}, u32[]{:S(2)}) collective-permute-start(bf16[4,2,2,32,128]{4,3,2,1,0:T(8,128)(2,1)S(1)} %collective-permute-done.51.refs_80_), channel_id=1, source_target_pairs={{0,4},{8,0},{16,8},{24,16},{28,24},{20,28},{12,20},{4,12},{1,5},{9... | collective-permute-start | bytes 393224 | tf_op jit(solution)/shard_map/ppermute | solution.py:298
  126.4 5.0 %collective-permute-start.45 = (bf16[4,2,2,32,128]{4,3,2,1,0:T(8,128)(2,1)S(1)}, bf16[4,2,2,32,128]{4,3,2,1,0:T(8,128)(2,1)S(1)}, u32[]{:S(2)}, u32[]{:S(2)}) collective-permute-start(bf16[4,2,2,32,128]{4,3,2,1,0:T(8,128)(2,1)S(1)} %collective-permute-done.43.refs_55_), channel_id=1, source_target_pairs={{0,8},{8,16},{16,24},{24,28},{28,20},{20,12},{12,4},{4,0},{1,9},{9... | collective-permute-start | bytes 393224 | tf_op jit(solution)/shard_map/ppermute | solution.py:298
  128.3 5.0 %collective-permute-start.54 = (bf16[4,2,2,32,128]{4,3,2,1,0:T(8,128)(2,1)S(1)}, bf16[4,2,2,32,128]{4,3,2,1,0:T(8,128)(2,1)S(1)}, u32[]{:S(2)}, u32[]{:S(2)}) collective-permute-start(bf16[4,2,2,32,128]{4,3,2,1,0:T(8,128)(2,1)S(1)} %collective-permute-done.52.refs_81_), channel_id=1, source_target_pairs={{0,4},{8,0},{16,8},{24,16},{28,24},{20,28},{12,20},{4,12},{1,5},{9... | collective-permute-start | bytes 393224 | tf_op jit(solution)/shard_map/ppermute | solution.py:298
  (104 other events, 2545.3 us)
where the time goes:
time: 150 us; the launch traced here: 149 us
  starting transfers between devices  63.2 us (42%)
  waiting for transfers between devices  40 us (27%)
  Pallas kernels  21.7 us (14%)
  other arithmetic  15 us (10%)
  local copies, waits for them, and re-layouts  7.61 us (5%)
    ppermute x50, starting transfers between devices, local(): got[half].append(lax.ppermute(value[half], 'chan', pairs))  51.8 us
    ppermute x50, waiting for transfers between devices, local(): got[half].append(lax.ppermute(value[half], 'chan', pairs))  27.4 us
    ppermute x5, waiting for transfers between devices, flip(): return lax.ppermute(block, 'band', [(b, b ^ bit) for b in range(n_band)])  12.6 us
    ppermute x5, starting transfers between devices, flip(): return lax.ppermute(block, 'band', [(b, b ^ bit) for b in range(n_band)])  10 us
    pallas_call x1, Pallas kernels, local(): pl.pallas_call(functools.partial(cross_kernel, groups, n_chan, n_chunks,...  9.39 us
    unnamed x190, local copies, waits for them, and re-layouts  7.48 us
    pallas_call x2, Pallas kernels, local(): outs = norm(panel_offset, scale, other, spectra)  6.81 us
    broadcast_in_dim x17, other arithmetic, local(): jnp.where(mask > 0, args[half], args[2 + half])  6.13 us
  transfers between devices with their start and end apart: 57, of which 35 were waited for; matrix products, arithmetic and copies ran while one was open for 7% of the time, Pallas kernels for 5%

commit v1 on v0

v1 whole, which is shorter than its diff:
```python
import functools

import jax
import jax.numpy as jnp
from jax import lax
from jax.experimental import pallas as pl
from jax.experimental.pallas import tpu as pltpu
from jax.sharding import PartitionSpec as P


PANEL = 256
NPANEL = 4
HALO = 32
HALF = PANEL // 2
LANES = 128
LAG = 2
SUBS = 4
SPANS = (1, 3)


def spans_of(groups):
    counts = SPANS if sum(SPANS) == groups else (groups,)
    return [(sum(counts[:i]), n) for i, n in enumerate(counts)]


def plan(n_chan, n_chunks):
    both = min(LAG * (n_chan // 2 - 1) // 2, n_chunks)
    single = n_chunks - both
    n_sends = single + 2 * both
    return single, n_sends, max(single + LAG * (n_chan - 2), n_sends + LAG * (n_chan // 2 - 1))


def scale_kernel(channels, bins, p_ref, q_ref, edge_ref, w_ref, scale_ref, s_ref, t_ref):
    rows, _ = scale_ref.shape
    ext = rows + 2 * HALO
    far = lax.rem(lax.axis_index("band"), 2)
    width = w_ref[...]
    span = 2 * width + 1
    inner = p_ref[...] + q_ref[...]
    edge = edge_ref[...]

    @pl.when(far == 0)
    def _():
        s_ref[:HALO, :] = edge
        s_ref[HALO:ext, :] = inner

    @pl.when(far == 1)
    def _():
        s_ref[: ext - HALO, :] = inner
        s_ref[ext - HALO : ext, :] = edge

    s_ref[ext:, :] = jnp.zeros((s_ref.shape[0] - ext, s_ref.shape[1]), jnp.float32)
    t_ref[...] = s_ref[...]
    step = 1
    while step * 2 <= 2 * HALO + 1:
        doubled = s_ref[0:ext, :] + s_ref[step : step + ext, :]
        s_ref[0:ext, :] = doubled
        step *= 2
        here = t_ref[0:ext, :]
        t_ref[0:ext, :] = jnp.where((span & step) != 0, doubled + t_ref[step : step + ext, :], here)
    skip = HALO - width
    step = 1
    n = ext
    while step < HALO:
        n = n - step
        t_ref[0:n, :] = jnp.where((skip & step) != 0, t_ref[step : step + n, :], t_ref[0:n, :])
        step *= 2
    total = t_ref[:rows, :]
    chan = lax.broadcasted_iota(jnp.int32, scale_ref.shape, 0) + (2 * lax.axis_index("chan") + far) * rows
    count = jnp.minimum(chan + width, channels - 1) - jnp.maximum(chan - width, 0) + 1
    scale_ref[...] = lax.rsqrt(total / (count.astype(jnp.float32) * bins) + 1e-06)


def norm_kernel(base, groups, subs, starts_ref, mine_ref, other_ref, x_ref, *rest):
    per = 2 * subs
    normed, own = rest[:groups], rest[groups : groups * (1 + per)]
    x_buf, scale_buf, n_ref, in_sem, scale_sem = rest[groups * (1 + per) :]
    _, f_dev, parts, rows, _ = x_buf.shape
    half_rows = rows // 2
    far = lax.rem(lax.axis_index("band"), 2)
    reads = []
    for g in range(groups):
        lanes = pl.ds((base + g) * LANES, LANES)
        reads.append(pltpu.make_async_copy(x_ref.at[:, :, :, lanes], x_buf.at[g], in_sem.at[g]))
        reads[g].start()
    shares = []
    for i, ref in enumerate((mine_ref, other_ref)):
        at = far * half_rows if i == 0 else (1 - far) * half_rows
        at = pl.ds(pl.multiple_of(at, half_rows), half_rows)
        shares.append(pltpu.make_async_copy(ref, scale_buf.at[at, :], scale_sem.at[i]))
        shares[i].start()
    for copy in shares:
        copy.wait()
    size = HALF // subs
    for g in range(groups):
        reads[g].wait()
        scale = scale_buf[:, g * LANES : (g + 1) * LANES]
        for f in range(f_dev):
            for k in range(parts):
                value = (x_buf[g, f, k].astype(jnp.float32) * scale).astype(jnp.bfloat16)
                normed[g][f, k] = value
                n_ref[f, k] = value.astype(jnp.float32)
        for p in range(NPANEL):
            start = starts_ref[p]
            for i in range(per):
                at = pl.ds(start + i * size, size)
                for f in range(f_dev):
                    for k in range(parts):
                        own[g * per + i][p, f, k] = n_ref[f, k, at, :].astype(jnp.bfloat16)


def cross_kernel(groups, n_chan, n_chunks, n_steps, single, scaling, block_ref, *refs):
    normed, refs = refs[:groups], refs[groups:]
    lists = []
    for size in (n_chunks, n_chunks, n_steps, n_steps):
        lists.append(refs[:size])
        refs = refs[size:]
    (out_ref,) = refs
    per = n_chunks // groups
    panel = pl.program_id(0)

    def place(c):
        return jnp.where(lax.rem(c, 2) == 0, c // 2, n_chan - 1 - c // 2)

    def source(d, half, c):
        if d == 0:
            return lists[half][c]
        if c < single:
            return lists[2 + half][c + LAG * ((d if half == 0 else n_chan - d) - 1)]
        t = single + 2 * (c - single) + half
        way = 0 if d <= n_chan // 2 else 1
        return lists[2 + way][t + LAG * ((d if way == 0 else n_chan - d) - 1)]

    def dot(a, b):
        return lax.dot_general(a, b, (((1,), (1,)), ((), ())), preferred_element_type=jnp.float32)

    ahead = lax.rem(place(lax.axis_index("chan")) - place(block_ref[panel]) + n_chan, n_chan)
    for d in range(n_chan):

        @pl.when(ahead == d)
        def _():
            for f in range(out_ref.shape[1]):
                left = [[n[f, k] for n in normed] for k in range(2)]
                right = jnp.concatenate(
                    [
                        jnp.concatenate(
                            [source(d, half, g * per + j)[panel, f, k] for half in range(2) for j in range(per)], axis=0
                        )
                        for k in range(2)
                        for g in range(groups)
                    ],
                    axis=1,
                )
                real = dot(jnp.concatenate(left[0] + left[1], axis=1), right)
                out_ref[0, f, 0] = (real * scaling).astype(jnp.bfloat16)
                imag = dot(jnp.concatenate(left[1] + [-n for n in left[0]], axis=1), right)
                out_ref[0, f, 1] = (imag * scaling).astype(jnp.bfloat16)


def local(spectra, half_width, panel_block, panel_offset):
    f_dev, parts, ch_dev, windows = spectra.shape
    n_chan, n_band = lax.axis_size("chan"), lax.axis_size("band")
    bins, channels = f_dev * n_band, ch_dev * n_chan
    groups = windows // LANES
    me = lax.axis_index("chan")
    hbm = pl.BlockSpec(memory_space=pl.ANY)
    vmem = pl.BlockSpec(memory_space=pltpu.VMEM)

    ring = list(range(0, n_chan, 2)) + list(range(1, n_chan, 2))[::-1]

    is_me = jnp.broadcast_to((panel_block == me)[:, None, None, None, None], (NPANEL, 1, 1, 1, LANES))
    is_me = is_me.astype(jnp.float32)

    half_rows = ch_dev // 2
    keep_rows = half_rows + HALO
    band = lax.axis_index("band")
    near = band % 2 == 0

    def flip(block, bit):
        return lax.ppermute(block, "band", [(b, b ^ bit) for b in range(n_band)])

    def outward(block):
        pairs = [
            (c * n_band + b, (c + (2 * (b % 2) - 1)) * n_band + (b ^ 1))
            for c in range(n_chan)
            for b in range(n_band)
            if 0 <= c + (2 * (b % 2) - 1) < n_chan
        ]
        return lax.ppermute(block, ("chan", "band"), pairs)

    power = jnp.sum(jnp.square(spectra.astype(jnp.float32)), axis=(0, 1))
    first, second = power[:keep_rows], power[half_rows - HALO :]
    share = jnp.where(near, first, second) + flip(jnp.where(near, second, first), 1)
    bit = 2
    while bit * 2 < n_band:
        share = share + flip(share, bit)
        bit *= 2
    spans = spans_of(groups)
    shares = [share[:, base * LANES : (base + n) * LANES] for base, n in spans]
    theirs = []
    for i in range(len(spans)):
        theirs.append(flip(shares[i], bit))
    edge = jnp.where(near, share[:HALO], share[keep_rows - HALO :])
    edge = edge + flip(edge, bit)
    halo = outward(edge)
    widths = half_width.reshape(1, windows)

    piece = (NPANEL, f_dev, parts, HALF // SUBS, LANES)
    block = (f_dev, parts, ch_dev, LANES)
    cuts = 2 * SUBS
    normed, own = [], [[], []]
    for i, (base, n_groups) in enumerate(spans):
        span = n_groups * LANES
        scale = pl.pallas_call(
            functools.partial(scale_kernel, channels, bins),
            grid=(n_groups,),
            out_shape=jax.ShapeDtypeStruct((half_rows, span), jnp.float32),
            in_specs=[pl.BlockSpec((keep_rows, LANES), lambda g: (0, g))] * 2
            + [pl.BlockSpec((HALO, LANES), lambda g, base=base: (0, base + g))]
            + [pl.BlockSpec((1, LANES), lambda g, base=base: (0, base + g))],
            out_specs=pl.BlockSpec((half_rows, LANES), lambda g: (0, g)),
            scratch_shapes=[pltpu.VMEM((half_rows + 4 * HALO, LANES), jnp.float32)] * 2,
            compiler_params=pltpu.CompilerParams(vmem_limit_bytes=6 << 20),
            name="scale",
        )
        scale = scale(shares[i], theirs[i], halo, widths)
        norm = pl.pallas_call(
            functools.partial(norm_kernel, base, n_groups, SUBS),
            out_shape=[pltpu.VMEM(block, jnp.bfloat16)] * n_groups
            + [pltpu.VMEM(piece, jnp.bfloat16)] * (n_groups * cuts),
            in_specs=[pl.BlockSpec(memory_space=pltpu.SMEM)] + [hbm] * 3,
            out_specs=[vmem] * (n_groups * (1 + cuts)),
            scratch_shapes=[
                pltpu.VMEM((n_groups, *block), jnp.bfloat16),
                pltpu.VMEM((ch_dev, span), jnp.float32),
                pltpu.VMEM(block, jnp.float32),
                pltpu.SemaphoreType.DMA((n_groups,)),
                pltpu.SemaphoreType.DMA((2,)),
            ],
            compiler_params=pltpu.CompilerParams(vmem_limit_bytes=16 << 20),
            name="norm",
        )
        other = flip(scale, 1)
        outs = norm(panel_offset, scale, other, spectra)
        normed += outs[:n_groups]
        outs = outs[n_groups:]
        for g in range(n_groups):
            own[0] += outs[g * cuts : g * cuts + SUBS]
            own[1] += outs[g * cuts + SUBS : (g + 1) * cuts]

    n_chunks = groups * SUBS
    single, n_sends, n_steps = plan(n_chan, n_chunks)
    got = [[], []]
    rest = [own[half][c] for c in range(single, n_chunks) for half in range(2)]
    sends = [own[half][:single] + rest for half in range(2)]

    marks = {LAG: [lax.optimization_barrier(is_me), lax.optimization_barrier(is_me + is_me)]}
    for t in range(LAG + 1, n_sends):
        marks[t] = []
        for half in range(2):
            marks[t].append(lax.optimization_barrier(jnp.minimum(marks[t - 1][half], 2.0 - half)))
    for t in range(n_steps):
        for half in range(2):
            value = sends[half][t] if t < n_sends else got[half][t - LAG]
            if LAG <= t < n_sends:
                mask, mine, back = lax.optimization_barrier((marks[t][half], value, got[half][t - LAG]))
                value = jnp.where(mask > 0, mine, back)
            step = 1 if half == 0 else -1
            pairs = [(ring[i], ring[(i + step) % n_chan]) for i in range(n_chan)]
            got[half].append(lax.ppermute(value, "chan", pairs))

    block = (1, f_dev, parts, ch_dev, PANEL)
    return pl.pallas_call(
        functools.partial(cross_kernel, groups, n_chan, n_chunks, n_steps, single, windows ** (-0.5)),
        grid=(NPANEL,),
        out_shape=jax.ShapeDtypeStruct((NPANEL, f_dev, parts, ch_dev, PANEL), jnp.bfloat16),
        in_specs=[pl.BlockSpec(memory_space=pltpu.SMEM)]
        + [vmem] * (groups + 2 * n_chunks + 2 * n_steps),
        out_specs=pl.BlockSpec(block, lambda p: (p, 0, 0, 0, 0)),
        compiler_params=pltpu.CompilerParams(vmem_limit_bytes=20 << 20),
        name="cross",
    )(panel_block, *normed, *own[0], *own[1], *got[0], *got[1])


def solution(mesh):
    placed = (P("band", None, "chan", None), P(), P(), P())
    return jax.shard_map(
        local,
        mesh=mesh,
        in_specs=placed,
        out_specs=P(None, "band", None, "chan", None),
        check_vma=False,
    )
```

time: 150 us -> 123 us (0.82)
  Pallas kernels: 21.7 us -> 12.2 us
  other arithmetic: 15 us -> 5.55 us
  local copies, waits for them, and re-layouts: 7.61 us -> 0.22 us
    unnamed x190 -> x8, local copies, waits for them, and re-layouts: 7.48 us -> 0.01 us
    broadcast_in_dim x17 -> x34, other arithmetic: 6.13 us -> 0.18 us  [local(): value = jnp.where(mask > 0, mine, back)]
    select_n x17 -> x34, other arithmetic: 5.83 us -> 0.75 us  [local(): value = jnp.where(mask > 0, mine, back)]
    ppermute x50, waiting for transfers between devices: 27.4 us -> 32.5 us  [local(): got[half].append(lax.ppermute(value, 'chan', pairs))]
    ppermute x5 -> x6, waiting for transfers between devices: 12.6 us -> 8.6 us  [flip(): return lax.ppermute(block, 'band', [(b, b ^ bit) for b in range(n_band)])]
    pallas_call x2, Pallas kernels: 5.51 us -> 1.62 us  [local(): scale = scale(shares[i], theirs[i], halo, widths)]
    pallas_call x2, Pallas kernels: 6.81 us -> 3.48 us  [local(): outs = norm(panel_offset, scale, other, spectra)]
    pallas_call x1, Pallas kernels: 9.39 us -> 7.14 us  [local(): pl.pallas_call(functools.partial(cross_kernel, groups, n_chan, n_chunks,...]
  transfers between devices with their start and end apart: 57 -> 57, of which waited for: 35 -> 35; matrix products, arithmetic and copies ran while one was open for 7% -> 1% of each run, Pallas kernels for 5% -> 3%
where the time goes in v1:
time: 123 us; the launch traced here: 122 us
  starting transfers between devices  62.9 us (51%)
  waiting for transfers between devices  41.1 us (33%)
  Pallas kernels  12.2 us (10%)
  other arithmetic  5.55 us (5%)
    ppermute x50, starting transfers between devices, local(): got[half].append(lax.ppermute(value, 'chan', pairs))  53.7 us
    ppermute x50, waiting for transfers between devices, local(): got[half].append(lax.ppermute(value, 'chan', pairs))  32.5 us
    ppermute x6, waiting for transfers between devices, flip(): return lax.ppermute(block, 'band', [(b, b ^ bit) for b in range(n_band)])  8.6 us
    ppermute x6, starting transfers between devices, flip(): return lax.ppermute(block, 'band', [(b, b ^ bit) for b in range(n_band)])  8.48 us
    pallas_call x1, Pallas kernels, local(): pl.pallas_call(functools.partial(cross_kernel, groups, n_chan, n_chunks,...  7.14 us
    pallas_call x2, Pallas kernels, local(): outs = norm(panel_offset, scale, other, spectra)  3.48 us
  transfers between devices with their start and end apart: 57, of which 35 were waited for; matrix products, arithmetic and copies ran while one was open for 1% of the time, Pallas kernels for 3%

profile of v1, /device:TPU:0, one launch (start us, length us, event | category | flops | bytes accessed | tf_op | source)
XLA Modules:
  0.0 122.4 jit_solution(14498499764814004823)
XLA Ops:
  0.0 2.3 %multiply_reduce_fusion = f32[512,512]{1,0:T(8,128)S(1)} fusion(bf16[2,2,512,512]{3,2,1,0:T(8,128)(2,1)} %x_ref.3), kind=kLoop, calls=%fused_computation | loop fusion | flops 2883584 | bytes 3145728 | tf_op jit(solution)/shard_map/reduce_sum | solution.py:191
  4.1 1.6 %collective-permute-done = f32[288,512]{1,0:T(8,128)} collective-permute-done((f32[288,512]{1,0:T(8,128)}, f32[288,512]{1,0:T(8,128)}, u32[]{:S(2)}, u32[]{:S(2)}) %collective-permute-start) | collective-permute-done | bytes 589856 | tf_op jit(solution)/shard_map/ppermute | solution.py:180
  6.9 2.9 %collective-permute-start.2 = (f32[32,512]{1,0:T(8,128)S(1)}, f32[32,512]{1,0:T(8,128)S(1)}, u32[]{:S(2)}, u32[]{:S(2)}) collective-permute-start(f32[32,512]{1,0:T(8,128)S(1)} %slice_select_fusion.1), channel_id=1, source_target_pairs={{0,2},{1,3},{2,0},{3,1},{4,6},{5,7},{6,4},{7,5},{8,10},{9,11},{10,... | collective-permute-start | bytes 196616 | tf_op jit(solution)/shard_map/ppermute | solution.py:180
  10.0 2.4 %collective-permute-done.2 = f32[32,512]{1,0:T(8,128)S(1)} collective-permute-done((f32[32,512]{1,0:T(8,128)S(1)}, f32[32,512]{1,0:T(8,128)S(1)}, u32[]{:S(2)}, u32[]{:S(2)}) %collective-permute-start.2) | collective-permute-done | bytes 65568 | tf_op jit(solution)/shard_map/ppermute | solution.py:180
  13.1 2.5 %collective-permute-done.1.q_ref = f32[288,128]{1,0:T(8,128)S(1)} collective-permute-done((f32[288,128]{1,0:T(8,128)S(1)}, f32[288,128]{1,0:T(8,128)S(1)}, u32[]{:S(2)}, u32[]{:S(2)}) %collective-permute-start.1) | collective-permute-done | bytes 147488 | tf_op jit(solution)/shard_map/ppermute | solution.py:180
  15.9 2.8 %collective-permute-start.4 = (f32[256,128]{1,0:T(8,128)S(1)}, f32[256,128]{1,0:T(8,128)S(1)}, u32[]{:S(2)}, u32[]{:S(2)}) collective-permute-start(f32[256,128]{1,0:T(8,128)S(1)} %scale.2.mine_ref), channel_id=1, source_target_pairs={{0,1},{1,0},{2,3},{3,2},{4,5},{5,4},{6,7},{7,6},{8,9},{9,8},{10,11... | collective-permute-start | bytes 393224 | tf_op jit(solution)/shard_map/ppermute | solution.py:180
  19.7 1.3 %norm.2 = (bf16[2,2,512,128]{3,2,1,0:T(8,128)(2,1)S(1)}, bf16[4,2,2,32,128]{4,3,2,1,0:T(8,128)(2,1)S(1)}, bf16[4,2,2,32,128]{4,3,2,1,0:T(8,128)(2,1)S(1)}, bf16[...) custom-call(s32[4]{0:T(128)S(1)} %copy-done.3, ...), custom_call_target="tpu_custom_call" | custom-call | tf_op jit(solution)/shard_map/norm/pallas_call | solution.py:244
  21.1 3.0 %collective-permute-start.7 = (bf16[4,2,2,32,128]{4,3,2,1,0:T(8,128)(2,1)S(1)}, bf16[4,2,2,32,128]{4,3,2,1,0:T(8,128)(2,1)S(1)}, u32[]{:S(2)}, u32[]{:S(2)}) collective-permute-start(bf16[4,2,2,32,128]{4,3,2,1,0:T(8,128)(2,1)S(1)} %get-tuple-element.147.refs_4_), channel_id=1, source_target_pairs={{0,8},{8,16},{16,24},{24,28},{28,20},{20,12},{12,4},{4,0},{1,9},{9... | collective-permute-start | bytes 393224 | tf_op jit(solution)/shard_map/ppermute | solution.py:270
  24.1 2.1 %collective-permute-start.5 = (f32[288,384]{1,0:T(8,128)S(1)}, f32[288,384]{1,0:T(8,128)S(1)}, u32[]{:S(2)}, u32[]{:S(2)}) collective-permute-start(f32[288,384]{1,0:T(8,128)S(1)} %slice.29.p_ref), channel_id=1, source_target_pairs={{0,2},{1,3},{2,0},{3,1},{4,6},{5,7},{6,4},{7,5},{8,10},{9,11},{10,... | collective-permute-start | bytes 1327112 | tf_op jit(solution)/shard_map/ppermute | solution.py:180
  26.2 1.6 %collective-permute-start.8 = (bf16[4,2,2,32,128]{4,3,2,1,0:T(8,128)(2,1)S(1)}, bf16[4,2,2,32,128]{4,3,2,1,0:T(8,128)(2,1)S(1)}, u32[]{:S(2)}, u32[]{:S(2)}) collective-permute-start(bf16[4,2,2,32,128]{4,3,2,1,0:T(8,128)(2,1)S(1)} %get-tuple-element.148.refs_5_), channel_id=1, source_target_pairs={{0,8},{8,16},{16,24},{24,28},{28,20},{20,12},{12,4},{4,0},{1,9},{9... | collective-permute-start | bytes 393224 | tf_op jit(solution)/shard_map/ppermute | solution.py:270
  28.3 2.1 %collective-permute-start.9 = (bf16[4,2,2,32,128]{4,3,2,1,0:T(8,128)(2,1)S(1)}, bf16[4,2,2,32,128]{4,3,2,1,0:T(8,128)(2,1)S(1)}, u32[]{:S(2)}, u32[]{:S(2)}) collective-permute-start(bf16[4,2,2,32,128]{4,3,2,1,0:T(8,128)(2,1)S(1)} %broadcast_select_fusion.33), channel_id=1, source_target_pairs={{0,8},{8,16},{16,24},{24,28},{28,20},{20,12},{12,4},{4,0},{1,9},{9... | collective-permute-start | bytes 393224 | tf_op jit(solution)/shard_map/ppermute | solution.py:270
  30.3 2.1 %collective-permute-done.8.refs_37_ = bf16[4,2,2,32,128]{4,3,2,1,0:T(8,128)(2,1)S(1)} collective-permute-done((bf16[4,2,2,32,128]{4,3,2,1,0:T(8,128)(2,1)S(1)}, bf16[4,2,2,32,128]{4,3,2,1,0:T(8,128)(2,1)S(1)}, u32[]{:S(2)}, u32[]{:S(2)}) %collective-permute-start.8) | collective-permute-done | bytes 131104 | tf_op jit(solution)/shard_map/ppermute | solution.py:270
  32.4 1.5 %collective-permute-start.10 = (bf16[4,2,2,32,128]{4,3,2,1,0:T(8,128)(2,1)S(1)}, bf16[4,2,2,32,128]{4,3,2,1,0:T(8,128)(2,1)S(1)}, u32[]{:S(2)}, u32[]{:S(2)}) collective-permute-start(bf16[4,2,2,32,128]{4,3,2,1,0:T(8,128)(2,1)S(1)} %broadcast_select_fusion.32), channel_id=1, source_target_pairs={{0,8},{8,16},{16,24},{24,28},{28,20},{20,12},{12,4},{4,0},{1,9},{9... | collective-permute-start | bytes 393224 | tf_op jit(solution)/shard_map/ppermute | solution.py:270
  34.6 2.0 %collective-permute-done.33.refs_62_ = bf16[4,2,2,32,128]{4,3,2,1,0:T(8,128)(2,1)S(1)} collective-permute-done((bf16[4,2,2,32,128]{4,3,2,1,0:T(8,128)(2,1)S(1)}, bf16[4,2,2,32,128]{4,3,2,1,0:T(8,128)(2,1)S(1)}, u32[]{:S(2)}, u32[]{:S(2)}) %collective-permute-start.33) | collective-permute-done | bytes 131104 | tf_op jit(solution)/shard_map/ppermute | solution.py:270
  36.6 1.3 %scale.3.mine_ref = f32[256,384]{1,0:T(8,128)S(1)} custom-call(f32[288,384]{1,0:T(8,128)S(1)} %slice.29.p_ref, f32[288,384]{1,0:T(8,128)S(1)} %collective-permute-done.5.q_ref, f32[32,512]{1,0:T(8,128)S(1)} %collective-permute-done.3.edge_ref, s32[1,512]{1,0:T(1,128)S(1)} %bitcast.70), custom_call_target="tpu_custom_call" | custom-call | tf_op jit(solution)/shard_map/scale/pallas_call | solution.py:226
  39.7 2.2 %norm.3 = (bf16[2,2,512,128]{3,2,1,0:T(8,128)(2,1)S(1)}, bf16[2,2,512,128]{3,2,1,0:T(8,128)(2,1)S(1)}, bf16[2,2,512,128]{3,2,1,0:T(8,128)(2,1)S(1)}, bf16[4,2,2,...) custom-call(s32[4]{0:T(128)S(1)} %copy-done.3, ...), custom_call_target="tpu_custom_call" | custom-call | tf_op jit(solution)/shard_map/norm/pallas_call | solution.py:244
  41.9 2.0 %collective-permute-done.35.refs_64_ = bf16[4,2,2,32,128]{4,3,2,1,0:T(8,128)(2,1)S(1)} collective-permute-done((bf16[4,2,2,32,128]{4,3,2,1,0:T(8,128)(2,1)S(1)}, bf16[4,2,2,32,128]{4,3,2,1,0:T(8,128)(2,1)S(1)}, u32[]{:S(2)}, u32[]{:S(2)}) %collective-permute-start.35) | collective-permute-done | bytes 131104 | tf_op jit(solution)/shard_map/ppermute | solution.py:270
  44.0 1.5 %collective-permute-start.11 = (bf16[4,2,2,32,128]{4,3,2,1,0:T(8,128)(2,1)S(1)}, bf16[4,2,2,32,128]{4,3,2,1,0:T(8,128)(2,1)S(1)}, u32[]{:S(2)}, u32[]{:S(2)}) collective-permute-start(bf16[4,2,2,32,128]{4,3,2,1,0:T(8,128)(2,1)S(1)} %broadcast_select_fusion.31), channel_id=1, source_target_pairs={{0,8},{8,16},{16,24},{24,28},{28,20},{20,12},{12,4},{4,0},{1,9},{9... | collective-permute-start | bytes 393224 | tf_op jit(solution)/shard_map/ppermute | solution.py:270
  45.5 1.6 %collective-permute-start.12 = (bf16[4,2,2,32,128]{4,3,2,1,0:T(8,128)(2,1)S(1)}, bf16[4,2,2,32,128]{4,3,2,1,0:T(8,128)(2,1)S(1)}, u32[]{:S(2)}, u32[]{:S(2)}) collective-permute-start(bf16[4,2,2,32,128]{4,3,2,1,0:T(8,128)(2,1)S(1)} %broadcast_select_fusion.30), channel_id=1, source_target_pairs={{0,8},{8,16},{16,24},{24,28},{28,20},{20,12},{12,4},{4,0},{1,9},{9... | collective-permute-start | bytes 393224 | tf_op jit(solution)/shard_map/ppermute | solution.py:270
  48.3 2.1 %collective-permute-done.11.refs_40_ = bf16[4,2,2,32,128]{4,3,2,1,0:T(8,128)(2,1)S(1)} collective-permute-done((bf16[4,2,2,32,128]{4,3,2,1,0:T(8,128)(2,1)S(1)}, bf16[4,2,2,32,128]{4,3,2,1,0:T(8,128)(2,1)S(1)}, u32[]{:S(2)}, u32[]{:S(2)}) %collective-permute-start.11) | collective-permute-done | bytes 131104 | tf_op jit(solution)/shard_map/ppermute | solution.py:270
  50.4 1.5 %collective-permute-start.13 = (bf16[4,2,2,32,128]{4,3,2,1,0:T(8,128)(2,1)S(1)}, bf16[4,2,2,32,128]{4,3,2,1,0:T(8,128)(2,1)S(1)}, u32[]{:S(2)}, u32[]{:S(2)}) collective-permute-start(bf16[4,2,2,32,128]{4,3,2,1,0:T(8,128)(2,1)S(1)} %broadcast_select_fusion.29), channel_id=1, source_target_pairs={{0,8},{8,16},{16,24},{24,28},{28,20},{20,12},{12,4},{4,0},{1,9},{9... | collective-permute-start | bytes 393224 | tf_op jit(solution)/shard_map/ppermute | solution.py:270
  51.9 1.3 %collective-permute-done.12.refs_41_ = bf16[4,2,2,32,128]{4,3,2,1,0:T(8,128)(2,1)S(1)} collective-permute-done((bf16[4,2,2,32,128]{4,3,2,1,0:T(8,128)(2,1)S(1)}, bf16[4,2,2,32,128]{4,3,2,1,0:T(8,128)(2,1)S(1)}, u32[]{:S(2)}, u32[]{:S(2)}) %collective-permute-start.12) | collective-permute-done | bytes 131104 | tf_op jit(solution)/shard_map/ppermute | solution.py:270
  53.2 1.5 %collective-permute-start.14 = (bf16[4,2,2,32,128]{4,3,2,1,0:T(8,128)(2,1)S(1)}, bf16[4,2,2,32,128]{4,3,2,1,0:T(8,128)(2,1)S(1)}, u32[]{:S(2)}, u32[]{:S(2)}) collective-permute-start(bf16[4,2,2,32,128]{4,3,2,1,0:T(8,128)(2,1)S(1)} %broadcast_select_fusion.28), channel_id=1, source_target_pairs={{0,8},{8,16},{16,24},{24,28},{28,20},{20,12},{12,4},{4,0},{1,9},{9... | collective-permute-start | bytes 393224 | tf_op jit(solution)/shard_map/ppermute | solution.py:270
  56.2 1.5 %collective-permute-start.15 = (bf16[4,2,2,32,128]{4,3,2,1,0:T(8,128)(2,1)S(1)}, bf16[4,2,2,32,128]{4,3,2,1,0:T(8,128)(2,1)S(1)}, u32[]{:S(2)}, u32[]{:S(2)}) collective-permute-start(bf16[4,2,2,32,128]{4,3,2,1,0:T(8,128)(2,1)S(1)} %broadcast_select_fusion.27), channel_id=1, source_target_pairs={{0,8},{8,16},{16,24},{24,28},{28,20},{20,12},{12,4},{4,0},{1,9},{9... | collective-permute-start | bytes 393224 | tf_op jit(solution)/shard_map/ppermute | solution.py:270
  57.7 1.9 %collective-permute-done.14.refs_43_ = bf16[4,2,2,32,128]{4,3,2,1,0:T(8,128)(2,1)S(1)} collective-permute-done((bf16[4,2,2,32,128]{4,3,2,1,0:T(8,128)(2,1)S(1)}, bf16[4,2,2,32,128]{4,3,2,1,0:T(8,128)(2,1)S(1)}, u32[]{:S(2)}, u32[]{:S(2)}) %collective-permute-start.14) | collective-permute-done | bytes 131104 | tf_op jit(solution)/shard_map/ppermute | solution.py:270
  59.7 1.5 %collective-permute-start.16 = (bf16[4,2,2,32,128]{4,3,2,1,0:T(8,128)(2,1)S(1)}, bf16[4,2,2,32,128]{4,3,2,1,0:T(8,128)(2,1)S(1)}, u32[]{:S(2)}, u32[]{:S(2)}) collective-permute-start(bf16[4,2,2,32,128]{4,3,2,1,0:T(8,128)(2,1)S(1)} %broadcast_select_fusion.26), channel_id=1, source_target_pairs={{0,8},{8,16},{16,24},{24,28},{28,20},{20,12},{12,4},{4,0},{1,9},{9... | collective-permute-start | bytes 393224 | tf_op jit(solution)/shard_map/ppermute | solution.py:270
  63.6 1.5 %collective-permute-start.17 = (bf16[4,2,2,32,128]{4,3,2,1,0:T(8,128)(2,1)S(1)}, bf16[4,2,2,32,128]{4,3,2,1,0:T(8,128)(2,1)S(1)}, u32[]{:S(2)}, u32[]{:S(2)}) collective-permute-start(bf16[4,2,2,32,128]{4,3,2,1,0:T(8,128)(2,1)S(1)} %broadcast_select_fusion.25), channel_id=1, source_target_pairs={{0,8},{8,16},{16,24},{24,28},{28,20},{20,12},{12,4},{4,0},{1,9},{9... | collective-permute-start | bytes 393224 | tf_op jit(solution)/shard_map/ppermute | solution.py:270
  65.8 1.5 %collective-permute-start.18 = (bf16[4,2,2,32,128]{4,3,2,1,0:T(8,128)(2,1)S(1)}, bf16[4,2,2,32,128]{4,3,2,1,0:T(8,128)(2,1)S(1)}, u32[]{:S(2)}, u32[]{:S(2)}) collective-permute-start(bf16[4,2,2,32,128]{4,3,2,1,0:T(8,128)(2,1)S(1)} %broadcast_select_fusion.24), channel_id=1, source_target_pairs={{0,8},{8,16},{16,24},{24,28},{28,20},{20,12},{12,4},{4,0},{1,9},{9... | collective-permute-start | bytes 393224 | tf_op jit(solution)/shard_map/ppermute | solution.py:270
  68.1 2.1 %collective-permute-done.41.refs_70_ = bf16[4,2,2,32,128]{4,3,2,1,0:T(8,128)(2,1)S(1)} collective-permute-done((bf16[4,2,2,32,128]{4,3,2,1,0:T(8,128)(2,1)S(1)}, bf16[4,2,2,32,128]{4,3,2,1,0:T(8,128)(2,1)S(1)}, u32[]{:S(2)}, u32[]{:S(2)}) %collective-permute-start.41) | collective-permute-done | bytes 131104 | tf_op jit(solution)/shard_map/ppermute | solution.py:270
  70.9 1.5 %collective-permute-start.19 = (bf16[4,2,2,32,128]{4,3,2,1,0:T(8,128)(2,1)S(1)}, bf16[4,2,2,32,128]{4,3,2,1,0:T(8,128)(2,1)S(1)}, u32[]{:S(2)}, u32[]{:S(2)}) collective-permute-start(bf16[4,2,2,32,128]{4,3,2,1,0:T(8,128)(2,1)S(1)} %broadcast_select_fusion.23), channel_id=1, source_target_pairs={{0,8},{8,16},{16,24},{24,28},{28,20},{20,12},{12,4},{4,0},{1,9},{9... | collective-permute-start | bytes 393224 | tf_op jit(solution)/shard_map/ppermute | solution.py:270
  72.8 1.5 %collective-permute-start.20 = (bf16[4,2,2,32,128]{4,3,2,1,0:T(8,128)(2,1)S(1)}, bf16[4,2,2,32,128]{4,3,2,1,0:T(8,128)(2,1)S(1)}, u32[]{:S(2)}, u32[]{:S(2)}) collective-permute-start(bf16[4,2,2,32,128]{4,3,2,1,0:T(8,128)(2,1)S(1)} %broadcast_select_fusion.22), channel_id=1, source_target_pairs={{0,8},{8,16},{16,24},{24,28},{28,20},{20,12},{12,4},{4,0},{1,9},{9... | collective-permute-start | bytes 393224 | tf_op jit(solution)/shard_map/ppermute | solution.py:270
  75.0 1.3 %collective-permute-done.43.refs_72_ = bf16[4,2,2,32,128]{4,3,2,1,0:T(8,128)(2,1)S(1)} collective-permute-done((bf16[4,2,2,32,128]{4,3,2,1,0:T(8,128)(2,1)S(1)}, bf16[4,2,2,32,128]{4,3,2,1,0:T(8,128)(2,1)S(1)}, u32[]{:S(2)}, u32[]{:S(2)}) %collective-permute-start.43) | collective-permute-done | bytes 131104 | tf_op jit(solution)/shard_map/ppermute | solution.py:270
  77.4 1.5 %collective-permute-start.21 = (bf16[4,2,2,32,128]{4,3,2,1,0:T(8,128)(2,1)S(1)}, bf16[4,2,2,32,128]{4,3,2,1,0:T(8,128)(2,1)S(1)}, u32[]{:S(2)}, u32[]{:S(2)}) collective-permute-start(bf16[4,2,2,32,128]{4,3,2,1,0:T(8,128)(2,1)S(1)} %broadcast_select_fusion.21), channel_id=1, source_target_pairs={{0,8},{8,16},{16,24},{24,28},{28,20},{20,12},{12,4},{4,0},{1,9},{9... | collective-permute-start | bytes 393224 | tf_op jit(solution)/shard_map/ppermute | solution.py:270
  79.5 1.5 %collective-permute-start.22 = (bf16[4,2,2,32,128]{4,3,2,1,0:T(8,128)(2,1)S(1)}, bf16[4,2,2,32,128]{4,3,2,1,0:T(8,128)(2,1)S(1)}, u32[]{:S(2)}, u32[]{:S(2)}) collective-permute-start(bf16[4,2,2,32,128]{4,3,2,1,0:T(8,128)(2,1)S(1)} %broadcast_select_fusion.20), channel_id=1, source_target_pairs={{0,8},{8,16},{16,24},{24,28},{28,20},{20,12},{12,4},{4,0},{1,9},{9... | collective-permute-start | bytes 393224 | tf_op jit(solution)/shard_map/ppermute | solution.py:270
  83.7 1.5 %collective-permute-start.23 = (bf16[4,2,2,32,128]{4,3,2,1,0:T(8,128)(2,1)S(1)}, bf16[4,2,2,32,128]{4,3,2,1,0:T(8,128)(2,1)S(1)}, u32[]{:S(2)}, u32[]{:S(2)}) collective-permute-start(bf16[4,2,2,32,128]{4,3,2,1,0:T(8,128)(2,1)S(1)} %broadcast_select_fusion.19), channel_id=1, source_target_pairs={{0,8},{8,16},{16,24},{24,28},{28,20},{20,12},{12,4},{4,0},{1,9},{9... | collective-permute-start | bytes 393224 | tf_op jit(solution)/shard_map/ppermute | solution.py:270
  85.8 1.5 %collective-permute-start.24 = (bf16[4,2,2,32,128]{4,3,2,1,0:T(8,128)(2,1)S(1)}, bf16[4,2,2,32,128]{4,3,2,1,0:T(8,128)(2,1)S(1)}, u32[]{:S(2)}, u32[]{:S(2)}) collective-permute-start(bf16[4,2,2,32,128]{4,3,2,1,0:T(8,128)(2,1)S(1)} %broadcast_select_fusion.18), channel_id=1, source_target_pairs={{0,8},{8,16},{16,24},{24,28},{28,20},{20,12},{12,4},{4,0},{1,9},{9... | collective-permute-start | bytes 393224 | tf_op jit(solution)/shard_map/ppermute | solution.py:270
  88.1 2.1 %collective-permute-done.47.refs_76_ = bf16[4,2,2,32,128]{4,3,2,1,0:T(8,128)(2,1)S(1)} collective-permute-done((bf16[4,2,2,32,128]{4,3,2,1,0:T(8,128)(2,1)S(1)}, bf16[4,2,2,32,128]{4,3,2,1,0:T(8,128)(2,1)S(1)}, u32[]{:S(2)}, u32[]{:S(2)}) %collective-permute-start.47) | collective-permute-done | bytes 131104 | tf_op jit(solution)/shard_map/ppermute | solution.py:270
  90.9 1.5 %collective-permute-start.25 = (bf16[4,2,2,32,128]{4,3,2,1,0:T(8,128)(2,1)S(1)}, bf16[4,2,2,32,128]{4,3,2,1,0:T(8,128)(2,1)S(1)}, u32[]{:S(2)}, u32[]{:S(2)}) collective-permute-start(bf16[4,2,2,32,128]{4,3,2,1,0:T(8,128)(2,1)S(1)} %broadcast_select_fusion.17), channel_id=1, source_target_pairs={{0,8},{8,16},{16,24},{24,28},{28,20},{20,12},{12,4},{4,0},{1,9},{9... | collective-permute-start | bytes 393224 | tf_op jit(solution)/shard_map/ppermute | solution.py:270
  93.8 1.4 %collective-permute-start.26 = (bf16[4,2,2,32,128]{4,3,2,1,0:T(8,128)(2,1)S(1)}, bf16[4,2,2,32,128]{4,3,2,1,0:T(8,128)(2,1)S(1)}, u32[]{:S(2)}, u32[]{:S(2)}) collective-permute-start(bf16[4,2,2,32,128]{4,3,2,1,0:T(8,128)(2,1)S(1)} %collective-permute-done.24.refs_53_), channel_id=1, source_target_pairs={{0,8},{8,16},{16,24},{24,28},{28,20},{20,12},{12,4},{4,0},{1,9},{9... | collective-permute-start | bytes 393224 | tf_op jit(solution)/shard_map/ppermute | solution.py:270
  95.3 1.4 %collective-permute-done.49.refs_78_ = bf16[4,2,2,32,128]{4,3,2,1,0:T(8,128)(2,1)S(1)} collective-permute-done((bf16[4,2,2,32,128]{4,3,2,1,0:T(8,128)(2,1)S(1)}, bf16[4,2,2,32,128]{4,3,2,1,0:T(8,128)(2,1)S(1)}, u32[]{:S(2)}, u32[]{:S(2)}) %collective-permute-start.49) | collective-permute-done | bytes 131104 | tf_op jit(solution)/shard_map/ppermute | solution.py:270
  97.3 1.4 %collective-permute-start.27 = (bf16[4,2,2,32,128]{4,3,2,1,0:T(8,128)(2,1)S(1)}, bf16[4,2,2,32,128]{4,3,2,1,0:T(8,128)(2,1)S(1)}, u32[]{:S(2)}, u32[]{:S(2)}) collective-permute-start(bf16[4,2,2,32,128]{4,3,2,1,0:T(8,128)(2,1)S(1)} %collective-permute-done.25.refs_54_), channel_id=1, source_target_pairs={{0,8},{8,16},{16,24},{24,28},{28,20},{20,12},{12,4},{4,0},{1,9},{9... | collective-permute-start | bytes 393224 | tf_op jit(solution)/shard_map/ppermute | solution.py:270
  100.2 1.4 %collective-permute-start.28 = (bf16[4,2,2,32,128]{4,3,2,1,0:T(8,128)(2,1)S(1)}, bf16[4,2,2,32,128]{4,3,2,1,0:T(8,128)(2,1)S(1)}, u32[]{:S(2)}, u32[]{:S(2)}) collective-permute-start(bf16[4,2,2,32,128]{4,3,2,1,0:T(8,128)(2,1)S(1)} %collective-permute-done.26.refs_55_), channel_id=1, source_target_pairs={{0,8},{8,16},{16,24},{24,28},{28,20},{20,12},{12,4},{4,0},{1,9},{9... | collective-permute-start | bytes 393224 | tf_op jit(solution)/shard_map/ppermute | solution.py:270
  103.2 1.4 %collective-permute-start.29 = (bf16[4,2,2,32,128]{4,3,2,1,0:T(8,128)(2,1)S(1)}, bf16[4,2,2,32,128]{4,3,2,1,0:T(8,128)(2,1)S(1)}, u32[]{:S(2)}, u32[]{:S(2)}) collective-permute-start(bf16[4,2,2,32,128]{4,3,2,1,0:T(8,128)(2,1)S(1)} %collective-permute-done.27.refs_56_), channel_id=1, source_target_pairs={{0,8},{8,16},{16,24},{24,28},{28,20},{20,12},{12,4},{4,0},{1,9},{9... | collective-permute-start | bytes 393224 | tf_op jit(solution)/shard_map/ppermute | solution.py:270
  105.9 1.4 %collective-permute-start.30 = (bf16[4,2,2,32,128]{4,3,2,1,0:T(8,128)(2,1)S(1)}, bf16[4,2,2,32,128]{4,3,2,1,0:T(8,128)(2,1)S(1)}, u32[]{:S(2)}, u32[]{:S(2)}) collective-permute-start(bf16[4,2,2,32,128]{4,3,2,1,0:T(8,128)(2,1)S(1)} %collective-permute-done.28.refs_57_), channel_id=1, source_target_pairs={{0,8},{8,16},{16,24},{24,28},{28,20},{20,12},{12,4},{4,0},{1,9},{9... | collective-permute-start | bytes 393224 | tf_op jit(solution)/shard_map/ppermute | solution.py:270
  108.2 1.4 %collective-permute-start.31 = (bf16[4,2,2,32,128]{4,3,2,1,0:T(8,128)(2,1)S(1)}, bf16[4,2,2,32,128]{4,3,2,1,0:T(8,128)(2,1)S(1)}, u32[]{:S(2)}, u32[]{:S(2)}) collective-permute-start(bf16[4,2,2,32,128]{4,3,2,1,0:T(8,128)(2,1)S(1)} %collective-permute-done.29.refs_58_), channel_id=1, source_target_pairs={{0,8},{8,16},{16,24},{24,28},{28,20},{20,12},{12,4},{4,0},{1,9},{9... | collective-permute-start | bytes 393224 | tf_op jit(solution)/shard_map/ppermute | solution.py:270
  110.9 1.7 %collective-permute-done.55.refs_84_ = bf16[4,2,2,32,128]{4,3,2,1,0:T(8,128)(2,1)S(1)} collective-permute-done((bf16[4,2,2,32,128]{4,3,2,1,0:T(8,128)(2,1)S(1)}, bf16[4,2,2,32,128]{4,3,2,1,0:T(8,128)(2,1)S(1)}, u32[]{:S(2)}, u32[]{:S(2)}) %collective-permute-start.55) | collective-permute-done | bytes 131104 | tf_op jit(solution)/shard_map/ppermute | solution.py:270
  113.1 2.1 %collective-permute-done.56.refs_85_ = bf16[4,2,2,32,128]{4,3,2,1,0:T(8,128)(2,1)S(1)} collective-permute-done((bf16[4,2,2,32,128]{4,3,2,1,0:T(8,128)(2,1)S(1)}, bf16[4,2,2,32,128]{4,3,2,1,0:T(8,128)(2,1)S(1)}, u32[]{:S(2)}, u32[]{:S(2)}) %collective-permute-start.56) | collective-permute-done | bytes 131104 | tf_op jit(solution)/shard_map/ppermute | solution.py:270
  115.2 7.1 %cross.1 = bf16[4,2,2,512,256]{4,3,2,1,0:T(8,128)(2,1)} custom-call(s32[4]{0:T(128)S(1)} %copy-done.2, bf16[2,2,512,128]{3,2,1,0:T(8,128)(2,1)S(1)} %get-tuple-element.143.refs_0_, bf16[2,2,512,128]{3,2,1,0:T(8,128)(2,1)S(1)} %get-tuple-element.144.refs_1_, bf16[2,2,512,128]{3,2,1,0:T(8,128)(2,1)S(1)} %get-tuple-element.145.refs_2_, ...), custom_call_target="tpu_custom_call" | custom-call | tf_op jit(solution)/shard_map/cross/pallas_call | solution.py:273
  (189 shorter events, 32.4 us)
Async XLA Ops:
  6.9 5.4 %collective-permute-start.2 = (f32[32,512]{1,0:T(8,128)S(1)}, f32[32,512]{1,0:T(8,128)S(1)}, u32[]{:S(2)}, u32[]{:S(2)}) collective-permute-start(f32[32,512]{1,0:T(8,128)S(1)} %slice_select_fusion.1), channel_id=1, source_target_pairs={{0,2},{1,3},{2,0},{3,1},{4,6},{5,7},{6,4},{7,5},{8,10},{9,11},{10,... | collective-permute-start | bytes 196616 | tf_op jit(solution)/shard_map/ppermute | solution.py:180
  9.9 5.7 %collective-permute-start.1 = (f32[288,128]{1,0:T(8,128)S(1)}, f32[288,128]{1,0:T(8,128)S(1)}, u32[]{:S(2)}, u32[]{:S(2)}) collective-permute-start(f32[288,128]{1,0:T(8,128)S(1)} %slice.26.p_ref), channel_id=1, source_target_pairs={{0,2},{1,3},{2,0},{3,1},{4,6},{5,7},{6,4},{7,5},{8,10},{9,11},{10,... | collective-permute-start | bytes 442376 | tf_op jit(solution)/shard_map/ppermute | solution.py:180
  21.1 7.2 %collective-permute-start.7 = (bf16[4,2,2,32,128]{4,3,2,1,0:T(8,128)(2,1)S(1)}, bf16[4,2,2,32,128]{4,3,2,1,0:T(8,128)(2,1)S(1)}, u32[]{:S(2)}, u32[]{:S(2)}) collective-permute-start(bf16[4,2,2,32,128]{4,3,2,1,0:T(8,128)(2,1)S(1)} %get-tuple-element.147.refs_4_), channel_id=1, source_target_pairs={{0,8},{8,16},{16,24},{24,28},{28,20},{20,12},{12,4},{4,0},{1,9},{9... | collective-permute-start | bytes 393224 | tf_op jit(solution)/shard_map/ppermute | solution.py:270
  24.1 12.5 %collective-permute-start.5 = (f32[288,384]{1,0:T(8,128)S(1)}, f32[288,384]{1,0:T(8,128)S(1)}, u32[]{:S(2)}, u32[]{:S(2)}) collective-permute-start(f32[288,384]{1,0:T(8,128)S(1)} %slice.29.p_ref), channel_id=1, source_target_pairs={{0,2},{1,3},{2,0},{3,1},{4,6},{5,7},{6,4},{7,5},{8,10},{9,11},{10,... | collective-permute-start | bytes 1327112 | tf_op jit(solution)/shard_map/ppermute | solution.py:180
  26.2 6.2 %collective-permute-start.8 = (bf16[4,2,2,32,128]{4,3,2,1,0:T(8,128)(2,1)S(1)}, bf16[4,2,2,32,128]{4,3,2,1,0:T(8,128)(2,1)S(1)}, u32[]{:S(2)}, u32[]{:S(2)}) collective-permute-start(bf16[4,2,2,32,128]{4,3,2,1,0:T(8,128)(2,1)S(1)} %get-tuple-element.148.refs_5_), channel_id=1, source_target_pairs={{0,8},{8,16},{16,24},{24,28},{28,20},{20,12},{12,4},{4,0},{1,9},{9... | collective-permute-start | bytes 393224 | tf_op jit(solution)/shard_map/ppermute | solution.py:270
  27.8 6.2 %collective-permute-start.32 = (bf16[4,2,2,32,128]{4,3,2,1,0:T(8,128)(2,1)S(1)}, bf16[4,2,2,32,128]{4,3,2,1,0:T(8,128)(2,1)S(1)}, u32[]{:S(2)}, u32[]{:S(2)}) collective-permute-start(bf16[4,2,2,32,128]{4,3,2,1,0:T(8,128)(2,1)S(1)} %get-tuple-element.163.refs_20_), channel_id=1, source_target_pairs={{0,4},{8,0},{16,8},{24,16},{28,24},{20,28},{12,20},{4,12},{1,5},{9... | collective-permute-start | bytes 393224 | tf_op jit(solution)/shard_map/ppermute | solution.py:270
  28.2 8.4 %collective-permute-start.33 = (bf16[4,2,2,32,128]{4,3,2,1,0:T(8,128)(2,1)S(1)}, bf16[4,2,2,32,128]{4,3,2,1,0:T(8,128)(2,1)S(1)}, u32[]{:S(2)}, u32[]{:S(2)}) collective-permute-start(bf16[4,2,2,32,128]{4,3,2,1,0:T(8,128)(2,1)S(1)} %get-tuple-element.164.refs_21_), channel_id=1, source_target_pairs={{0,4},{8,0},{16,8},{24,16},{28,24},{20,28},{12,20},{4,12},{1,5},{9... | collective-permute-start | bytes 393224 | tf_op jit(solution)/shard_map/ppermute | solution.py:270
  28.3 13.6 %collective-permute-start.9 = (bf16[4,2,2,32,128]{4,3,2,1,0:T(8,128)(2,1)S(1)}, bf16[4,2,2,32,128]{4,3,2,1,0:T(8,128)(2,1)S(1)}, u32[]{:S(2)}, u32[]{:S(2)}) collective-permute-start(bf16[4,2,2,32,128]{4,3,2,1,0:T(8,128)(2,1)S(1)} %broadcast_select_fusion.33), channel_id=1, source_target_pairs={{0,8},{8,16},{16,24},{24,28},{28,20},{20,12},{12,4},{4,0},{1,9},{9... | collective-permute-start | bytes 393224 | tf_op jit(solution)/shard_map/ppermute | solution.py:270
  32.4 9.4 %collective-permute-start.10 = (bf16[4,2,2,32,128]{4,3,2,1,0:T(8,128)(2,1)S(1)}, bf16[4,2,2,32,128]{4,3,2,1,0:T(8,128)(2,1)S(1)}, u32[]{:S(2)}, u32[]{:S(2)}) collective-permute-start(bf16[4,2,2,32,128]{4,3,2,1,0:T(8,128)(2,1)S(1)} %broadcast_select_fusion.32), channel_id=1, source_target_pairs={{0,8},{8,16},{16,24},{24,28},{28,20},{20,12},{12,4},{4,0},{1,9},{9... | collective-permute-start | bytes 393224 | tf_op jit(solution)/shard_map/ppermute | solution.py:270
  34.0 7.9 %collective-permute-start.34 = (bf16[4,2,2,32,128]{4,3,2,1,0:T(8,128)(2,1)S(1)}, bf16[4,2,2,32,128]{4,3,2,1,0:T(8,128)(2,1)S(1)}, u32[]{:S(2)}, u32[]{:S(2)}) collective-permute-start(bf16[4,2,2,32,128]{4,3,2,1,0:T(8,128)(2,1)S(1)} %broadcast_select_fusion.16), channel_id=1, source_target_pairs={{0,4},{8,0},{16,8},{24,16},{28,24},{20,28},{12,20},{4,12},{1,5},{9... | collective-permute-start | bytes 393224 | tf_op jit(solution)/shard_map/ppermute | solution.py:270
  38.0 5.9 %collective-permute-start.35 = (bf16[4,2,2,32,128]{4,3,2,1,0:T(8,128)(2,1)S(1)}, bf16[4,2,2,32,128]{4,3,2,1,0:T(8,128)(2,1)S(1)}, u32[]{:S(2)}, u32[]{:S(2)}) collective-permute-start(bf16[4,2,2,32,128]{4,3,2,1,0:T(8,128)(2,1)S(1)} %broadcast_select_fusion.15), channel_id=1, source_target_pairs={{0,4},{8,0},{16,8},{24,16},{28,24},{20,28},{12,20},{4,12},{1,5},{9... | collective-permute-start | bytes 393224 | tf_op jit(solution)/shard_map/ppermute | solution.py:270
  44.0 6.4 %collective-permute-start.11 = (bf16[4,2,2,32,128]{4,3,2,1,0:T(8,128)(2,1)S(1)}, bf16[4,2,2,32,128]{4,3,2,1,0:T(8,128)(2,1)S(1)}, u32[]{:S(2)}, u32[]{:S(2)}) collective-permute-start(bf16[4,2,2,32,128]{4,3,2,1,0:T(8,128)(2,1)S(1)} %broadcast_select_fusion.31), channel_id=1, source_target_pairs={{0,8},{8,16},{16,24},{24,28},{28,20},{20,12},{12,4},{4,0},{1,9},{9... | collective-permute-start | bytes 393224 | tf_op jit(solution)/shard_map/ppermute | solution.py:270
  45.5 7.7 %collective-permute-start.12 = (bf16[4,2,2,32,128]{4,3,2,1,0:T(8,128)(2,1)S(1)}, bf16[4,2,2,32,128]{4,3,2,1,0:T(8,128)(2,1)S(1)}, u32[]{:S(2)}, u32[]{:S(2)}) collective-permute-start(bf16[4,2,2,32,128]{4,3,2,1,0:T(8,128)(2,1)S(1)} %broadcast_select_fusion.30), channel_id=1, source_target_pairs={{0,8},{8,16},{16,24},{24,28},{28,20},{20,12},{12,4},{4,0},{1,9},{9... | collective-permute-start | bytes 393224 | tf_op jit(solution)/shard_map/ppermute | solution.py:270
  47.1 7.7 %collective-permute-start.36 = (bf16[4,2,2,32,128]{4,3,2,1,0:T(8,128)(2,1)S(1)}, bf16[4,2,2,32,128]{4,3,2,1,0:T(8,128)(2,1)S(1)}, u32[]{:S(2)}, u32[]{:S(2)}) collective-permute-start(bf16[4,2,2,32,128]{4,3,2,1,0:T(8,128)(2,1)S(1)} %broadcast_select_fusion.14), channel_id=1, source_target_pairs={{0,4},{8,0},{16,8},{24,16},{28,24},{20,28},{12,20},{4,12},{1,5},{9... | collective-permute-start | bytes 393224 | tf_op jit(solution)/shard_map/ppermute | solution.py:270
  47.6 7.8 %collective-permute-start.37 = (bf16[4,2,2,32,128]{4,3,2,1,0:T(8,128)(2,1)S(1)}, bf16[4,2,2,32,128]{4,3,2,1,0:T(8,128)(2,1)S(1)}, u32[]{:S(2)}, u32[]{:S(2)}) collective-permute-start(bf16[4,2,2,32,128]{4,3,2,1,0:T(8,128)(2,1)S(1)} %broadcast_select_fusion.13), channel_id=1, source_target_pairs={{0,4},{8,0},{16,8},{24,16},{28,24},{20,28},{12,20},{4,12},{1,5},{9... | collective-permute-start | bytes 393224 | tf_op jit(solution)/shard_map/ppermute | solution.py:270
  50.4 5.8 %collective-permute-start.13 = (bf16[4,2,2,32,128]{4,3,2,1,0:T(8,128)(2,1)S(1)}, bf16[4,2,2,32,128]{4,3,2,1,0:T(8,128)(2,1)S(1)}, u32[]{:S(2)}, u32[]{:S(2)}) collective-permute-start(bf16[4,2,2,32,128]{4,3,2,1,0:T(8,128)(2,1)S(1)} %broadcast_select_fusion.29), channel_id=1, source_target_pairs={{0,8},{8,16},{16,24},{24,28},{28,20},{20,12},{12,4},{4,0},{1,9},{9... | collective-permute-start | bytes 393224 | tf_op jit(solution)/shard_map/ppermute | solution.py:270
  53.2 6.4 %collective-permute-start.14 = (bf16[4,2,2,32,128]{4,3,2,1,0:T(8,128)(2,1)S(1)}, bf16[4,2,2,32,128]{4,3,2,1,0:T(8,128)(2,1)S(1)}, u32[]{:S(2)}, u32[]{:S(2)}) collective-permute-start(bf16[4,2,2,32,128]{4,3,2,1,0:T(8,128)(2,1)S(1)} %broadcast_select_fusion.28), channel_id=1, source_target_pairs={{0,8},{8,16},{16,24},{24,28},{28,20},{20,12},{12,4},{4,0},{1,9},{9... | collective-permute-start | bytes 393224 | tf_op jit(solution)/shard_map/ppermute | solution.py:270
  54.7 6.4 %collective-permute-start.38 = (bf16[4,2,2,32,128]{4,3,2,1,0:T(8,128)(2,1)S(1)}, bf16[4,2,2,32,128]{4,3,2,1,0:T(8,128)(2,1)S(1)}, u32[]{:S(2)}, u32[]{:S(2)}) collective-permute-start(bf16[4,2,2,32,128]{4,3,2,1,0:T(8,128)(2,1)S(1)} %broadcast_select_fusion.12), channel_id=1, source_target_pairs={{0,4},{8,0},{16,8},{24,16},{28,24},{20,28},{12,20},{4,12},{1,5},{9... | collective-permute-start | bytes 393224 | tf_op jit(solution)/shard_map/ppermute | solution.py:270
  55.4 7.5 %collective-permute-start.39 = (bf16[4,2,2,32,128]{4,3,2,1,0:T(8,128)(2,1)S(1)}, bf16[4,2,2,32,128]{4,3,2,1,0:T(8,128)(2,1)S(1)}, u32[]{:S(2)}, u32[]{:S(2)}) collective-permute-start(bf16[4,2,2,32,128]{4,3,2,1,0:T(8,128)(2,1)S(1)} %broadcast_select_fusion.11), channel_id=1, source_target_pairs={{0,4},{8,0},{16,8},{24,16},{28,24},{20,28},{12,20},{4,12},{1,5},{9... | collective-permute-start | bytes 393224 | tf_op jit(solution)/shard_map/ppermute | solution.py:270
  56.2 7.4 %collective-permute-start.15 = (bf16[4,2,2,32,128]{4,3,2,1,0:T(8,128)(2,1)S(1)}, bf16[4,2,2,32,128]{4,3,2,1,0:T(8,128)(2,1)S(1)}, u32[]{:S(2)}, u32[]{:S(2)}) collective-permute-start(bf16[4,2,2,32,128]{4,3,2,1,0:T(8,128)(2,1)S(1)} %broadcast_select_fusion.27), channel_id=1, source_target_pairs={{0,8},{8,16},{16,24},{24,28},{28,20},{20,12},{12,4},{4,0},{1,9},{9... | collective-permute-start | bytes 393224 | tf_op jit(solution)/shard_map/ppermute | solution.py:270
  59.7 6.1 %collective-permute-start.16 = (bf16[4,2,2,32,128]{4,3,2,1,0:T(8,128)(2,1)S(1)}, bf16[4,2,2,32,128]{4,3,2,1,0:T(8,128)(2,1)S(1)}, u32[]{:S(2)}, u32[]{:S(2)}) collective-permute-start(bf16[4,2,2,32,128]{4,3,2,1,0:T(8,128)(2,1)S(1)} %broadcast_select_fusion.26), channel_id=1, source_target_pairs={{0,8},{8,16},{16,24},{24,28},{28,20},{20,12},{12,4},{4,0},{1,9},{9... | collective-permute-start | bytes 393224 | tf_op jit(solution)/shard_map/ppermute | solution.py:270
  61.2 6.2 %collective-permute-start.40 = (bf16[4,2,2,32,128]{4,3,2,1,0:T(8,128)(2,1)S(1)}, bf16[4,2,2,32,128]{4,3,2,1,0:T(8,128)(2,1)S(1)}, u32[]{:S(2)}, u32[]{:S(2)}) collective-permute-start(bf16[4,2,2,32,128]{4,3,2,1,0:T(8,128)(2,1)S(1)} %broadcast_select_fusion.10), channel_id=1, source_target_pairs={{0,4},{8,0},{16,8},{24,16},{28,24},{20,28},{12,20},{4,12},{1,5},{9... | collective-permute-start | bytes 393224 | tf_op jit(solution)/shard_map/ppermute | solution.py:270
  62.9 7.3 %collective-permute-start.41 = (bf16[4,2,2,32,128]{4,3,2,1,0:T(8,128)(2,1)S(1)}, bf16[4,2,2,32,128]{4,3,2,1,0:T(8,128)(2,1)S(1)}, u32[]{:S(2)}, u32[]{:S(2)}) collective-permute-start(bf16[4,2,2,32,128]{4,3,2,1,0:T(8,128)(2,1)S(1)} %broadcast_select_fusion.9), channel_id=1, source_target_pairs={{0,4},{8,0},{16,8},{24,16},{28,24},{20,28},{12,20},{4,12},{1,5},{9... | collective-permute-start | bytes 393224 | tf_op jit(solution)/shard_map/ppermute | solution.py:270
  63.6 7.3 %collective-permute-start.17 = (bf16[4,2,2,32,128]{4,3,2,1,0:T(8,128)(2,1)S(1)}, bf16[4,2,2,32,128]{4,3,2,1,0:T(8,128)(2,1)S(1)}, u32[]{:S(2)}, u32[]{:S(2)}) collective-permute-start(bf16[4,2,2,32,128]{4,3,2,1,0:T(8,128)(2,1)S(1)} %broadcast_select_fusion.25), channel_id=1, source_target_pairs={{0,8},{8,16},{16,24},{24,28},{28,20},{20,12},{12,4},{4,0},{1,9},{9... | collective-permute-start | bytes 393224 | tf_op jit(solution)/shard_map/ppermute | solution.py:270
  65.8 7.0 %collective-permute-start.18 = (bf16[4,2,2,32,128]{4,3,2,1,0:T(8,128)(2,1)S(1)}, bf16[4,2,2,32,128]{4,3,2,1,0:T(8,128)(2,1)S(1)}, u32[]{:S(2)}, u32[]{:S(2)}) collective-permute-start(bf16[4,2,2,32,128]{4,3,2,1,0:T(8,128)(2,1)S(1)} %broadcast_select_fusion.24), channel_id=1, source_target_pairs={{0,8},{8,16},{16,24},{24,28},{28,20},{20,12},{12,4},{4,0},{1,9},{9... | collective-permute-start | bytes 393224 | tf_op jit(solution)/shard_map/ppermute | solution.py:270
  67.4 6.9 %collective-permute-start.42 = (bf16[4,2,2,32,128]{4,3,2,1,0:T(8,128)(2,1)S(1)}, bf16[4,2,2,32,128]{4,3,2,1,0:T(8,128)(2,1)S(1)}, u32[]{:S(2)}, u32[]{:S(2)}) collective-permute-start(bf16[4,2,2,32,128]{4,3,2,1,0:T(8,128)(2,1)S(1)} %broadcast_select_fusion.8), channel_id=1, source_target_pairs={{0,4},{8,0},{16,8},{24,16},{28,24},{20,28},{12,20},{4,12},{1,5},{9... | collective-permute-start | bytes 393224 | tf_op jit(solution)/shard_map/ppermute | solution.py:270
  70.2 6.0 %collective-permute-start.43 = (bf16[4,2,2,32,128]{4,3,2,1,0:T(8,128)(2,1)S(1)}, bf16[4,2,2,32,128]{4,3,2,1,0:T(8,128)(2,1)S(1)}, u32[]{:S(2)}, u32[]{:S(2)}) collective-permute-start(bf16[4,2,2,32,128]{4,3,2,1,0:T(8,128)(2,1)S(1)} %broadcast_select_fusion.7), channel_id=1, source_target_pairs={{0,4},{8,0},{16,8},{24,16},{28,24},{20,28},{12,20},{4,12},{1,5},{9... | collective-permute-start | bytes 393224 | tf_op jit(solution)/shard_map/ppermute | solution.py:270
  70.9 6.4 %collective-permute-start.19 = (bf16[4,2,2,32,128]{4,3,2,1,0:T(8,128)(2,1)S(1)}, bf16[4,2,2,32,128]{4,3,2,1,0:T(8,128)(2,1)S(1)}, u32[]{:S(2)}, u32[]{:S(2)}) collective-permute-start(bf16[4,2,2,32,128]{4,3,2,1,0:T(8,128)(2,1)S(1)} %broadcast_select_fusion.23), channel_id=1, source_target_pairs={{0,8},{8,16},{16,24},{24,28},{28,20},{20,12},{12,4},{4,0},{1,9},{9... | collective-permute-start | bytes 393224 | tf_op jit(solution)/shard_map/ppermute | solution.py:270
  72.8 6.6 %collective-permute-start.20 = (bf16[4,2,2,32,128]{4,3,2,1,0:T(8,128)(2,1)S(1)}, bf16[4,2,2,32,128]{4,3,2,1,0:T(8,128)(2,1)S(1)}, u32[]{:S(2)}, u32[]{:S(2)}) collective-permute-start(bf16[4,2,2,32,128]{4,3,2,1,0:T(8,128)(2,1)S(1)} %broadcast_select_fusion.22), channel_id=1, source_target_pairs={{0,8},{8,16},{16,24},{24,28},{28,20},{20,12},{12,4},{4,0},{1,9},{9... | collective-permute-start | bytes 393224 | tf_op jit(solution)/shard_map/ppermute | solution.py:270
  74.3 6.6 %collective-permute-start.44 = (bf16[4,2,2,32,128]{4,3,2,1,0:T(8,128)(2,1)S(1)}, bf16[4,2,2,32,128]{4,3,2,1,0:T(8,128)(2,1)S(1)}, u32[]{:S(2)}, u32[]{:S(2)}) collective-permute-start(bf16[4,2,2,32,128]{4,3,2,1,0:T(8,128)(2,1)S(1)} %broadcast_select_fusion.6), channel_id=1, source_target_pairs={{0,4},{8,0},{16,8},{24,16},{28,24},{20,28},{12,20},{4,12},{1,5},{9... | collective-permute-start | bytes 393224 | tf_op jit(solution)/shard_map/ppermute | solution.py:270
  76.3 6.1 %collective-permute-start.45 = (bf16[4,2,2,32,128]{4,3,2,1,0:T(8,128)(2,1)S(1)}, bf16[4,2,2,32,128]{4,3,2,1,0:T(8,128)(2,1)S(1)}, u32[]{:S(2)}, u32[]{:S(2)}) collective-permute-start(bf16[4,2,2,32,128]{4,3,2,1,0:T(8,128)(2,1)S(1)} %broadcast_select_fusion.5), channel_id=1, source_target_pairs={{0,4},{8,0},{16,8},{24,16},{28,24},{20,28},{12,20},{4,12},{1,5},{9... | collective-permute-start | bytes 393224 | tf_op jit(solution)/shard_map/ppermute | solution.py:270
  77.4 6.3 %collective-permute-start.21 = (bf16[4,2,2,32,128]{4,3,2,1,0:T(8,128)(2,1)S(1)}, bf16[4,2,2,32,128]{4,3,2,1,0:T(8,128)(2,1)S(1)}, u32[]{:S(2)}, u32[]{:S(2)}) collective-permute-start(bf16[4,2,2,32,128]{4,3,2,1,0:T(8,128)(2,1)S(1)} %broadcast_select_fusion.21), channel_id=1, source_target_pairs={{0,8},{8,16},{16,24},{24,28},{28,20},{20,12},{12,4},{4,0},{1,9},{9... | collective-permute-start | bytes 393224 | tf_op jit(solution)/shard_map/ppermute | solution.py:270
  79.5 6.3 %collective-permute-start.22 = (bf16[4,2,2,32,128]{4,3,2,1,0:T(8,128)(2,1)S(1)}, bf16[4,2,2,32,128]{4,3,2,1,0:T(8,128)(2,1)S(1)}, u32[]{:S(2)}, u32[]{:S(2)}) collective-permute-start(bf16[4,2,2,32,128]{4,3,2,1,0:T(8,128)(2,1)S(1)} %broadcast_select_fusion.20), channel_id=1, source_target_pairs={{0,8},{8,16},{16,24},{24,28},{28,20},{20,12},{12,4},{4,0},{1,9},{9... | collective-permute-start | bytes 393224 | tf_op jit(solution)/shard_map/ppermute | solution.py:270
  81.0 6.4 %collective-permute-start.46 = (bf16[4,2,2,32,128]{4,3,2,1,0:T(8,128)(2,1)S(1)}, bf16[4,2,2,32,128]{4,3,2,1,0:T(8,128)(2,1)S(1)}, u32[]{:S(2)}, u32[]{:S(2)}) collective-permute-start(bf16[4,2,2,32,128]{4,3,2,1,0:T(8,128)(2,1)S(1)} %broadcast_select_fusion.4), channel_id=1, source_target_pairs={{0,4},{8,0},{16,8},{24,16},{28,24},{20,28},{12,20},{4,12},{1,5},{9... | collective-permute-start | bytes 393224 | tf_op jit(solution)/shard_map/ppermute | solution.py:270
  82.4 7.8 %collective-permute-start.47 = (bf16[4,2,2,32,128]{4,3,2,1,0:T(8,128)(2,1)S(1)}, bf16[4,2,2,32,128]{4,3,2,1,0:T(8,128)(2,1)S(1)}, u32[]{:S(2)}, u32[]{:S(2)}) collective-permute-start(bf16[4,2,2,32,128]{4,3,2,1,0:T(8,128)(2,1)S(1)} %broadcast_select_fusion.3), channel_id=1, source_target_pairs={{0,4},{8,0},{16,8},{24,16},{28,24},{20,28},{12,20},{4,12},{1,5},{9... | collective-permute-start | bytes 393224 | tf_op jit(solution)/shard_map/ppermute | solution.py:270
  83.7 7.2 %collective-permute-start.23 = (bf16[4,2,2,32,128]{4,3,2,1,0:T(8,128)(2,1)S(1)}, bf16[4,2,2,32,128]{4,3,2,1,0:T(8,128)(2,1)S(1)}, u32[]{:S(2)}, u32[]{:S(2)}) collective-permute-start(bf16[4,2,2,32,128]{4,3,2,1,0:T(8,128)(2,1)S(1)} %broadcast_select_fusion.19), channel_id=1, source_target_pairs={{0,8},{8,16},{16,24},{24,28},{28,20},{20,12},{12,4},{4,0},{1,9},{9... | collective-permute-start | bytes 393224 | tf_op jit(solution)/shard_map/ppermute | solution.py:270
  85.8 8.0 %collective-permute-start.24 = (bf16[4,2,2,32,128]{4,3,2,1,0:T(8,128)(2,1)S(1)}, bf16[4,2,2,32,128]{4,3,2,1,0:T(8,128)(2,1)S(1)}, u32[]{:S(2)}, u32[]{:S(2)}) collective-permute-start(bf16[4,2,2,32,128]{4,3,2,1,0:T(8,128)(2,1)S(1)} %broadcast_select_fusion.18), channel_id=1, source_target_pairs={{0,8},{8,16},{16,24},{24,28},{28,20},{20,12},{12,4},{4,0},{1,9},{9... | collective-permute-start | bytes 393224 | tf_op jit(solution)/shard_map/ppermute | solution.py:270
  87.4 5.7 %collective-permute-start.48 = (bf16[4,2,2,32,128]{4,3,2,1,0:T(8,128)(2,1)S(1)}, bf16[4,2,2,32,128]{4,3,2,1,0:T(8,128)(2,1)S(1)}, u32[]{:S(2)}, u32[]{:S(2)}) collective-permute-start(bf16[4,2,2,32,128]{4,3,2,1,0:T(8,128)(2,1)S(1)} %broadcast_select_fusion.2), channel_id=1, source_target_pairs={{0,4},{8,0},{16,8},{24,16},{28,24},{20,28},{12,20},{4,12},{1,5},{9... | collective-permute-start | bytes 393224 | tf_op jit(solution)/shard_map/ppermute | solution.py:270
  90.3 6.4 %collective-permute-start.49 = (bf16[4,2,2,32,128]{4,3,2,1,0:T(8,128)(2,1)S(1)}, bf16[4,2,2,32,128]{4,3,2,1,0:T(8,128)(2,1)S(1)}, u32[]{:S(2)}, u32[]{:S(2)}) collective-permute-start(bf16[4,2,2,32,128]{4,3,2,1,0:T(8,128)(2,1)S(1)} %broadcast_select_fusion.1), channel_id=1, source_target_pairs={{0,4},{8,0},{16,8},{24,16},{28,24},{20,28},{12,20},{4,12},{1,5},{9... | collective-permute-start | bytes 393224 | tf_op jit(solution)/shard_map/ppermute | solution.py:270
  90.9 6.3 %collective-permute-start.25 = (bf16[4,2,2,32,128]{4,3,2,1,0:T(8,128)(2,1)S(1)}, bf16[4,2,2,32,128]{4,3,2,1,0:T(8,128)(2,1)S(1)}, u32[]{:S(2)}, u32[]{:S(2)}) collective-permute-start(bf16[4,2,2,32,128]{4,3,2,1,0:T(8,128)(2,1)S(1)} %broadcast_select_fusion.17), channel_id=1, source_target_pairs={{0,8},{8,16},{16,24},{24,28},{28,20},{20,12},{12,4},{4,0},{1,9},{9... | collective-permute-start | bytes 393224 | tf_op jit(solution)/shard_map/ppermute | solution.py:270
  93.2 6.4 %collective-permute-start.50 = (bf16[4,2,2,32,128]{4,3,2,1,0:T(8,128)(2,1)S(1)}, bf16[4,2,2,32,128]{4,3,2,1,0:T(8,128)(2,1)S(1)}, u32[]{:S(2)}, u32[]{:S(2)}) collective-permute-start(bf16[4,2,2,32,128]{4,3,2,1,0:T(8,128)(2,1)S(1)} %broadcast_select_fusion), channel_id=1, source_target_pairs={{0,4},{8,0},{16,8},{24,16},{28,24},{20,28},{12,20},{4,12},{1,5},{9... | collective-permute-start | bytes 393224 | tf_op jit(solution)/shard_map/ppermute | solution.py:270
  93.8 6.4 %collective-permute-start.26 = (bf16[4,2,2,32,128]{4,3,2,1,0:T(8,128)(2,1)S(1)}, bf16[4,2,2,32,128]{4,3,2,1,0:T(8,128)(2,1)S(1)}, u32[]{:S(2)}, u32[]{:S(2)}) collective-permute-start(bf16[4,2,2,32,128]{4,3,2,1,0:T(8,128)(2,1)S(1)} %collective-permute-done.24.refs_53_), channel_id=1, source_target_pairs={{0,8},{8,16},{16,24},{24,28},{28,20},{20,12},{12,4},{4,0},{1,9},{9... | collective-permute-start | bytes 393224 | tf_op jit(solution)/shard_map/ppermute | solution.py:270
  96.7 5.9 %collective-permute-start.51 = (bf16[4,2,2,32,128]{4,3,2,1,0:T(8,128)(2,1)S(1)}, bf16[4,2,2,32,128]{4,3,2,1,0:T(8,128)(2,1)S(1)}, u32[]{:S(2)}, u32[]{:S(2)}) collective-permute-start(bf16[4,2,2,32,128]{4,3,2,1,0:T(8,128)(2,1)S(1)} %collective-permute-done.49.refs_78_), channel_id=1, source_target_pairs={{0,4},{8,0},{16,8},{24,16},{28,24},{20,28},{12,20},{4,12},{1,5},{9... | collective-permute-start | bytes 393224 | tf_op jit(solution)/shard_map/ppermute | solution.py:270
  97.3 5.9 %collective-permute-start.27 = (bf16[4,2,2,32,128]{4,3,2,1,0:T(8,128)(2,1)S(1)}, bf16[4,2,2,32,128]{4,3,2,1,0:T(8,128)(2,1)S(1)}, u32[]{:S(2)}, u32[]{:S(2)}) collective-permute-start(bf16[4,2,2,32,128]{4,3,2,1,0:T(8,128)(2,1)S(1)} %collective-permute-done.25.refs_54_), channel_id=1, source_target_pairs={{0,8},{8,16},{16,24},{24,28},{28,20},{20,12},{12,4},{4,0},{1,9},{9... | collective-permute-start | bytes 393224 | tf_op jit(solution)/shard_map/ppermute | solution.py:270
  99.6 5.7 %collective-permute-start.52 = (bf16[4,2,2,32,128]{4,3,2,1,0:T(8,128)(2,1)S(1)}, bf16[4,2,2,32,128]{4,3,2,1,0:T(8,128)(2,1)S(1)}, u32[]{:S(2)}, u32[]{:S(2)}) collective-permute-start(bf16[4,2,2,32,128]{4,3,2,1,0:T(8,128)(2,1)S(1)} %collective-permute-done.50.refs_79_), channel_id=1, source_target_pairs={{0,4},{8,0},{16,8},{24,16},{28,24},{20,28},{12,20},{4,12},{1,5},{9... | collective-permute-start | bytes 393224 | tf_op jit(solution)/shard_map/ppermute | solution.py:270
  100.2 5.7 %collective-permute-start.28 = (bf16[4,2,2,32,128]{4,3,2,1,0:T(8,128)(2,1)S(1)}, bf16[4,2,2,32,128]{4,3,2,1,0:T(8,128)(2,1)S(1)}, u32[]{:S(2)}, u32[]{:S(2)}) collective-permute-start(bf16[4,2,2,32,128]{4,3,2,1,0:T(8,128)(2,1)S(1)} %collective-permute-done.26.refs_55_), channel_id=1, source_target_pairs={{0,8},{8,16},{16,24},{24,28},{28,20},{20,12},{12,4},{4,0},{1,9},{9... | collective-permute-start | bytes 393224 | tf_op jit(solution)/shard_map/ppermute | solution.py:270
  103.2 5.0 %collective-permute-start.29 = (bf16[4,2,2,32,128]{4,3,2,1,0:T(8,128)(2,1)S(1)}, bf16[4,2,2,32,128]{4,3,2,1,0:T(8,128)(2,1)S(1)}, u32[]{:S(2)}, u32[]{:S(2)}) collective-permute-start(bf16[4,2,2,32,128]{4,3,2,1,0:T(8,128)(2,1)S(1)} %collective-permute-done.27.refs_56_), channel_id=1, source_target_pairs={{0,8},{8,16},{16,24},{24,28},{28,20},{20,12},{12,4},{4,0},{1,9},{9... | collective-permute-start | bytes 393224 | tf_op jit(solution)/shard_map/ppermute | solution.py:270
  105.9 5.0 %collective-permute-start.30 = (bf16[4,2,2,32,128]{4,3,2,1,0:T(8,128)(2,1)S(1)}, bf16[4,2,2,32,128]{4,3,2,1,0:T(8,128)(2,1)S(1)}, u32[]{:S(2)}, u32[]{:S(2)}) collective-permute-start(bf16[4,2,2,32,128]{4,3,2,1,0:T(8,128)(2,1)S(1)} %collective-permute-done.28.refs_57_), channel_id=1, source_target_pairs={{0,8},{8,16},{16,24},{24,28},{28,20},{20,12},{12,4},{4,0},{1,9},{9... | collective-permute-start | bytes 393224 | tf_op jit(solution)/shard_map/ppermute | solution.py:270
  (13 other events, 92.3 us)

commit v2 on v1

--- a/solution.py
+++ b/solution.py
@@ -15,7 +15,7 @@
 LANES = 128
 LAG = 2
 SUBS = 4
-SPANS = (1, 3)
+SPANS = (1, 1, 2)
 
 
 def spans_of(groups):
@@ -188,21 +188,26 @@
         ]
         return lax.ppermute(block, ("chan", "band"), pairs)
 
-    power = jnp.sum(jnp.square(spectra.astype(jnp.float32)), axis=(0, 1))
+    def power_of(block):
+        return jnp.sum(jnp.square(block.astype(jnp.float32)), axis=(0, 1))
+
+    low, high = power_of(spectra[:, :, :HALO]), power_of(spectra[:, :, ch_dev - HALO :])
+    edge = jnp.where(near, low, high) + flip(jnp.where(near, high, low), 1)
+    power = power_of(spectra)
     first, second = power[:keep_rows], power[half_rows - HALO :]
     share = jnp.where(near, first, second) + flip(jnp.where(near, second, first), 1)
     bit = 2
     while bit * 2 < n_band:
+        edge = edge + flip(edge, bit)
         share = share + flip(share, bit)
         bit *= 2
+    edge = edge + flip(edge, bit)
+    halo = outward(edge)
     spans = spans_of(groups)
     shares = [share[:, base * LANES : (base + n) * LANES] for base, n in spans]
     theirs = []
     for i in range(len(spans)):
         theirs.append(flip(shares[i], bit))
-    edge = jnp.where(near, share[:HALO], share[keep_rows - HALO :])
-    edge = edge + flip(edge, bit)
-    halo = outward(edge)
     widths = half_width.reshape(1, windows)
 
     piece = (NPANEL, f_dev, parts, HALF // SUBS, LANES)

time: 123 us -> 125 us (1.016)
  starting transfers between devices: 62.9 us -> 69.3 us
  waiting for transfers between devices: 41.1 us -> 35.4 us
    ppermute x6 -> x9, starting transfers between devices: 8.48 us -> 14.8 us  [flip(): return lax.ppermute(block, 'band', [(b, b ^ bit) for b in range(n_band)])]
    ppermute x6 -> x9, waiting for transfers between devices: 8.6 us -> 3.32 us  [flip(): return lax.ppermute(block, 'band', [(b, b ^ bit) for b in range(n_band)])]
    reduce_sum x1 -> x2, other arithmetic: 2.29 us -> 3.19 us  [power_of(): return jnp.sum(jnp.square(block.astype(jnp.float32)), axis=(0, 1))]
    pallas_call x2 -> x3, Pallas kernels: 3.48 us -> 4.05 us  [local(): outs = norm(panel_offset, scale, other, spectra)]
  transfers between devices with their start and end apart: 57 -> 60, of which waited for: 35 -> 29; matrix products, arithmetic and copies ran while one was open for 1% -> 4% of each run, Pallas kernels for 3% -> 5%
where the time goes in v2:
time: 125 us; the launch traced here: 124 us
  starting transfers between devices  69.3 us (55%)
  waiting for transfers between devices  35.4 us (28%)
  Pallas kernels  12.7 us (10%)
  other arithmetic  6.46 us (5%)
    ppermute x50, starting transfers between devices, local(): got[half].append(lax.ppermute(value, 'chan', pairs))  53.9 us
    ppermute x50, waiting for transfers between devices, local(): got[half].append(lax.ppermute(value, 'chan', pairs))  32 us
    ppermute x9, starting transfers between devices, flip(): return lax.ppermute(block, 'band', [(b, b ^ bit) for b in range(n_band)])  14.8 us
    pallas_call x1, Pallas kernels, local(): pl.pallas_call(functools.partial(cross_kernel, groups, n_chan, n_chunks,...  7.07 us
    pallas_call x3, Pallas kernels, local(): outs = norm(panel_offset, scale, other, spectra)  4.05 us
    ppermute x9, waiting for transfers between devices, flip(): return lax.ppermute(block, 'band', [(b, b ^ bit) for b in range(n_band)])  3.32 us
    reduce_sum x2, other arithmetic, power_of(): return jnp.sum(jnp.square(block.astype(jnp.float32)), axis=(0, 1))  3.19 us
  transfers between devices with their start and end apart: 60, of which 29 were waited for; matrix products, arithmetic and copies ran while one was open for 4% of the time, Pallas kernels for 5%

profile of v2, /device:TPU:0, one launch (start us, length us, event | category | flops | bytes accessed | tf_op | source)
XLA Modules:
  0.0 124.5 jit_solution(16756044293402208327)
XLA Ops:
  0.0 1.0 multiply_reduce_fusion.2
  1.6 2.2 %multiply_reduce_fusion = f32[512,512]{1,0:T(8,128)S(1)} fusion(bf16[2,2,512,512]{3,2,1,0:T(8,128)(2,1)} %x_ref.5), kind=kLoop, calls=%fused_computation | loop fusion | flops 2883584 | bytes 3145728 | tf_op jit(solution)/shard_map/reduce_sum | solution.py:192
  5.2 3.1 %collective-permute-start.3 = (f32[32,512]{1,0:T(8,128)S(1)}, f32[32,512]{1,0:T(8,128)S(1)}, u32[]{:S(2)}, u32[]{:S(2)}) collective-permute-start(f32[32,512]{1,0:T(8,128)S(1)} %select_add_fusion.1), channel_id=1, source_target_pairs={{0,2},{1,3},{2,0},{3,1},{4,6},{5,7},{6,4},{7,5},{8,10},{9,11},{10,... | collective-permute-start | bytes 196616 | tf_op jit(solution)/shard_map/ppermute | solution.py:180
  8.2 2.3 %collective-permute-done.3 = f32[32,512]{1,0:T(8,128)S(1)} collective-permute-done((f32[32,512]{1,0:T(8,128)S(1)}, f32[32,512]{1,0:T(8,128)S(1)}, u32[]{:S(2)}, u32[]{:S(2)}) %collective-permute-start.3) | collective-permute-done | bytes 65568 | tf_op jit(solution)/shard_map/ppermute | solution.py:180
  11.2 1.2 select_add_fusion
  12.5 2.1 %collective-permute-start.1 = (f32[288,128]{1,0:T(8,128)S(1)}, f32[288,128]{1,0:T(8,128)S(1)}, u32[]{:S(2)}, u32[]{:S(2)}) collective-permute-start(f32[288,128]{1,0:T(8,128)S(1)} %get-tuple-element.286.p_ref), channel_id=1, source_target_pairs={{0,2},{1,3},{2,0},{3,1},{4,6},{5,7},{6,4},{7,5},{8,10},{9,11},{10,... | collective-permute-start | bytes 442376 | tf_op jit(solution)/shard_map/ppermute | solution.py:180
  14.7 2.0 %collective-permute-start.8 = (f32[288,256]{1,0:T(8,128)S(1)}, f32[288,256]{1,0:T(8,128)S(1)}, u32[]{:S(2)}, u32[]{:S(2)}) collective-permute-start(f32[288,256]{1,0:T(8,128)S(1)} %slice.32.p_ref), channel_id=1, source_target_pairs={{0,2},{1,3},{2,0},{3,1},{4,6},{5,7},{6,4},{7,5},{8,10},{9,11},{10,... | collective-permute-start | bytes 884744 | tf_op jit(solution)/shard_map/ppermute | solution.py:180
  18.0 4.1 %collective-permute-start.5 = (f32[256,128]{1,0:T(8,128)S(1)}, f32[256,128]{1,0:T(8,128)S(1)}, u32[]{:S(2)}, u32[]{:S(2)}) collective-permute-start(f32[256,128]{1,0:T(8,128)S(1)} %scale.3.mine_ref), channel_id=1, source_target_pairs={{0,1},{1,0},{2,3},{3,2},{4,5},{5,4},{6,7},{7,6},{8,9},{9,8},{10,11... | collective-permute-start | bytes 393224 | tf_op jit(solution)/shard_map/ppermute | solution.py:180
  22.5 2.8 %collective-permute-start.7 = (f32[256,128]{1,0:T(8,128)S(1)}, f32[256,128]{1,0:T(8,128)S(1)}, u32[]{:S(2)}, u32[]{:S(2)}) collective-permute-start(f32[256,128]{1,0:T(8,128)S(1)} %scale.4.mine_ref), channel_id=1, source_target_pairs={{0,1},{1,0},{2,3},{3,2},{4,5},{5,4},{6,7},{7,6},{8,9},{9,8},{10,11... | collective-permute-start | bytes 393224 | tf_op jit(solution)/shard_map/ppermute | solution.py:180
  25.3 1.3 %norm.3 = (bf16[2,2,512,128]{3,2,1,0:T(8,128)(2,1)S(1)}, bf16[4,2,2,32,128]{4,3,2,1,0:T(8,128)(2,1)S(1)}, bf16[4,2,2,32,128]{4,3,2,1,0:T(8,128)(2,1)S(1)}, bf16[...) custom-call(s32[4]{0:T(128)S(1)} %copy-done.2, ...), custom_call_target="tpu_custom_call" | custom-call | tf_op jit(solution)/shard_map/norm/pallas_call | solution.py:249
  26.6 1.6 %collective-permute-start.10 = (bf16[4,2,2,32,128]{4,3,2,1,0:T(8,128)(2,1)S(1)}, bf16[4,2,2,32,128]{4,3,2,1,0:T(8,128)(2,1)S(1)}, u32[]{:S(2)}, u32[]{:S(2)}) collective-permute-start(bf16[4,2,2,32,128]{4,3,2,1,0:T(8,128)(2,1)S(1)} %get-tuple-element.147.refs_4_), channel_id=1, source_target_pairs={{0,8},{8,16},{16,24},{24,28},{28,20},{20,12},{12,4},{4,0},{1,9},{9... | collective-permute-start | bytes 393224 | tf_op jit(solution)/shard_map/ppermute | solution.py:275
  28.3 1.6 %collective-permute-start.11 = (bf16[4,2,2,32,128]{4,3,2,1,0:T(8,128)(2,1)S(1)}, bf16[4,2,2,32,128]{4,3,2,1,0:T(8,128)(2,1)S(1)}, u32[]{:S(2)}, u32[]{:S(2)}) collective-permute-start(bf16[4,2,2,32,128]{4,3,2,1,0:T(8,128)(2,1)S(1)} %get-tuple-element.148.refs_5_), channel_id=1, source_target_pairs={{0,8},{8,16},{16,24},{24,28},{28,20},{20,12},{12,4},{4,0},{1,9},{9... | collective-permute-start | bytes 393224 | tf_op jit(solution)/shard_map/ppermute | solution.py:275
  30.8 1.3 %norm.4 = (bf16[2,2,512,128]{3,2,1,0:T(8,128)(2,1)S(1)}, bf16[4,2,2,32,128]{4,3,2,1,0:T(8,128)(2,1)S(1)}, bf16[4,2,2,32,128]{4,3,2,1,0:T(8,128)(2,1)S(1)}, bf16[...) custom-call(s32[4]{0:T(128)S(1)} %copy-done.2, ...), custom_call_target="tpu_custom_call" | custom-call | tf_op jit(solution)/shard_map/norm/pallas_call | solution.py:249
  33.1 1.6 %collective-permute-start.12 = (bf16[4,2,2,32,128]{4,3,2,1,0:T(8,128)(2,1)S(1)}, bf16[4,2,2,32,128]{4,3,2,1,0:T(8,128)(2,1)S(1)}, u32[]{:S(2)}, u32[]{:S(2)}) collective-permute-start(bf16[4,2,2,32,128]{4,3,2,1,0:T(8,128)(2,1)S(1)} %broadcast_select_fusion.33), channel_id=1, source_target_pairs={{0,8},{8,16},{16,24},{24,28},{28,20},{20,12},{12,4},{4,0},{1,9},{9... | collective-permute-start | bytes 393224 | tf_op jit(solution)/shard_map/ppermute | solution.py:275
  35.0 1.6 %collective-permute-start.13 = (bf16[4,2,2,32,128]{4,3,2,1,0:T(8,128)(2,1)S(1)}, bf16[4,2,2,32,128]{4,3,2,1,0:T(8,128)(2,1)S(1)}, u32[]{:S(2)}, u32[]{:S(2)}) collective-permute-start(bf16[4,2,2,32,128]{4,3,2,1,0:T(8,128)(2,1)S(1)} %broadcast_select_fusion.32), channel_id=1, source_target_pairs={{0,8},{8,16},{16,24},{24,28},{28,20},{20,12},{12,4},{4,0},{1,9},{9... | collective-permute-start | bytes 393224 | tf_op jit(solution)/shard_map/ppermute | solution.py:275
  37.6 1.2 collective-permute-start.38
  39.5 2.3 %collective-permute-done.13.refs_39_ = bf16[4,2,2,32,128]{4,3,2,1,0:T(8,128)(2,1)S(1)} collective-permute-done((bf16[4,2,2,32,128]{4,3,2,1,0:T(8,128)(2,1)S(1)}, bf16[4,2,2,32,128]{4,3,2,1,0:T(8,128)(2,1)S(1)}, u32[]{:S(2)}, u32[]{:S(2)}) %collective-permute-start.13) | collective-permute-done | bytes 131104 | tf_op jit(solution)/shard_map/ppermute | solution.py:275
  41.8 1.2 collective-permute-done.37.refs_63_
  43.1 1.5 %collective-permute-done.38.refs_64_ = bf16[4,2,2,32,128]{4,3,2,1,0:T(8,128)(2,1)S(1)} collective-permute-done((bf16[4,2,2,32,128]{4,3,2,1,0:T(8,128)(2,1)S(1)}, bf16[4,2,2,32,128]{4,3,2,1,0:T(8,128)(2,1)S(1)}, u32[]{:S(2)}, u32[]{:S(2)}) %collective-permute-start.38) | collective-permute-done | bytes 131104 | tf_op jit(solution)/shard_map/ppermute | solution.py:275
  44.6 1.6 %collective-permute-start.14 = (bf16[4,2,2,32,128]{4,3,2,1,0:T(8,128)(2,1)S(1)}, bf16[4,2,2,32,128]{4,3,2,1,0:T(8,128)(2,1)S(1)}, u32[]{:S(2)}, u32[]{:S(2)}) collective-permute-start(bf16[4,2,2,32,128]{4,3,2,1,0:T(8,128)(2,1)S(1)} %broadcast_select_fusion.31), channel_id=1, source_target_pairs={{0,8},{8,16},{16,24},{24,28},{28,20},{20,12},{12,4},{4,0},{1,9},{9... | collective-permute-start | bytes 393224 | tf_op jit(solution)/shard_map/ppermute | solution.py:275
  47.1 1.3 %collective-permute-start.39 = (bf16[4,2,2,32,128]{4,3,2,1,0:T(8,128)(2,1)S(1)}, bf16[4,2,2,32,128]{4,3,2,1,0:T(8,128)(2,1)S(1)}, u32[]{:S(2)}, u32[]{:S(2)}) collective-permute-start(bf16[4,2,2,32,128]{4,3,2,1,0:T(8,128)(2,1)S(1)} %broadcast_select_fusion.14), channel_id=1, source_target_pairs={{0,4},{8,0},{16,8},{24,16},{28,24},{20,28},{12,20},{4,12},{1,5},{9... | collective-permute-start | bytes 393224 | tf_op jit(solution)/shard_map/ppermute | solution.py:275
  49.0 1.4 %norm.5 = (bf16[2,2,512,128]{3,2,1,0:T(8,128)(2,1)S(1)}, bf16[2,2,512,128]{3,2,1,0:T(8,128)(2,1)S(1)}, bf16[4,2,2,32,128]{4,3,2,1,0:T(8,128)(2,1)S(1)}, bf16[4,2...) custom-call(s32[4]{0:T(128)S(1)} %copy-done.2, ...), custom_call_target="tpu_custom_call" | custom-call | tf_op jit(solution)/shard_map/norm/pallas_call | solution.py:249
  50.4 1.6 %collective-permute-start.16 = (bf16[4,2,2,32,128]{4,3,2,1,0:T(8,128)(2,1)S(1)}, bf16[4,2,2,32,128]{4,3,2,1,0:T(8,128)(2,1)S(1)}, u32[]{:S(2)}, u32[]{:S(2)}) collective-permute-start(bf16[4,2,2,32,128]{4,3,2,1,0:T(8,128)(2,1)S(1)} %broadcast_select_fusion.29), channel_id=1, source_target_pairs={{0,8},{8,16},{16,24},{24,28},{28,20},{20,12},{12,4},{4,0},{1,9},{9... | collective-permute-start | bytes 393224 | tf_op jit(solution)/shard_map/ppermute | solution.py:275
  52.7 1.6 %collective-permute-start.17 = (bf16[4,2,2,32,128]{4,3,2,1,0:T(8,128)(2,1)S(1)}, bf16[4,2,2,32,128]{4,3,2,1,0:T(8,128)(2,1)S(1)}, u32[]{:S(2)}, u32[]{:S(2)}) collective-permute-start(bf16[4,2,2,32,128]{4,3,2,1,0:T(8,128)(2,1)S(1)} %broadcast_select_fusion.28), channel_id=1, source_target_pairs={{0,8},{8,16},{16,24},{24,28},{28,20},{20,12},{12,4},{4,0},{1,9},{9... | collective-permute-start | bytes 393224 | tf_op jit(solution)/shard_map/ppermute | solution.py:275
  55.9 1.8 %collective-permute-done.17.refs_43_ = bf16[4,2,2,32,128]{4,3,2,1,0:T(8,128)(2,1)S(1)} collective-permute-done((bf16[4,2,2,32,128]{4,3,2,1,0:T(8,128)(2,1)S(1)}, bf16[4,2,2,32,128]{4,3,2,1,0:T(8,128)(2,1)S(1)}, u32[]{:S(2)}, u32[]{:S(2)}) %collective-permute-start.17) | collective-permute-done | bytes 131104 | tf_op jit(solution)/shard_map/ppermute | solution.py:275
  57.7 1.7 %collective-permute-done.41.refs_67_ = bf16[4,2,2,32,128]{4,3,2,1,0:T(8,128)(2,1)S(1)} collective-permute-done((bf16[4,2,2,32,128]{4,3,2,1,0:T(8,128)(2,1)S(1)}, bf16[4,2,2,32,128]{4,3,2,1,0:T(8,128)(2,1)S(1)}, u32[]{:S(2)}, u32[]{:S(2)}) %collective-permute-start.41) | collective-permute-done | bytes 131104 | tf_op jit(solution)/shard_map/ppermute | solution.py:275
  59.4 1.4 %collective-permute-done.42.refs_68_ = bf16[4,2,2,32,128]{4,3,2,1,0:T(8,128)(2,1)S(1)} collective-permute-done((bf16[4,2,2,32,128]{4,3,2,1,0:T(8,128)(2,1)S(1)}, bf16[4,2,2,32,128]{4,3,2,1,0:T(8,128)(2,1)S(1)}, u32[]{:S(2)}, u32[]{:S(2)}) %collective-permute-start.42) | collective-permute-done | bytes 131104 | tf_op jit(solution)/shard_map/ppermute | solution.py:275
  61.6 1.7 %collective-permute-start.19 = (bf16[4,2,2,32,128]{4,3,2,1,0:T(8,128)(2,1)S(1)}, bf16[4,2,2,32,128]{4,3,2,1,0:T(8,128)(2,1)S(1)}, u32[]{:S(2)}, u32[]{:S(2)}) collective-permute-start(bf16[4,2,2,32,128]{4,3,2,1,0:T(8,128)(2,1)S(1)} %broadcast_select_fusion.26), channel_id=1, source_target_pairs={{0,8},{8,16},{16,24},{24,28},{28,20},{20,12},{12,4},{4,0},{1,9},{9... | collective-permute-start | bytes 393224 | tf_op jit(solution)/shard_map/ppermute | solution.py:275
  63.8 1.3 %collective-permute-start.44 = (bf16[4,2,2,32,128]{4,3,2,1,0:T(8,128)(2,1)S(1)}, bf16[4,2,2,32,128]{4,3,2,1,0:T(8,128)(2,1)S(1)}, u32[]{:S(2)}, u32[]{:S(2)}) collective-permute-start(bf16[4,2,2,32,128]{4,3,2,1,0:T(8,128)(2,1)S(1)} %broadcast_select_fusion.9), channel_id=1, source_target_pairs={{0,4},{8,0},{16,8},{24,16},{28,24},{20,28},{12,20},{4,12},{1,5},{9... | collective-permute-start | bytes 393224 | tf_op jit(solution)/shard_map/ppermute | solution.py:275
  65.1 2.1 %collective-permute-done.18.refs_44_ = bf16[4,2,2,32,128]{4,3,2,1,0:T(8,128)(2,1)S(1)} collective-permute-done((bf16[4,2,2,32,128]{4,3,2,1,0:T(8,128)(2,1)S(1)}, bf16[4,2,2,32,128]{4,3,2,1,0:T(8,128)(2,1)S(1)}, u32[]{:S(2)}, u32[]{:S(2)}) %collective-permute-start.18) | collective-permute-done | bytes 131104 | tf_op jit(solution)/shard_map/ppermute | solution.py:275
  68.1 2.0 %collective-permute-done.19.refs_45_ = bf16[4,2,2,32,128]{4,3,2,1,0:T(8,128)(2,1)S(1)} collective-permute-done((bf16[4,2,2,32,128]{4,3,2,1,0:T(8,128)(2,1)S(1)}, bf16[4,2,2,32,128]{4,3,2,1,0:T(8,128)(2,1)S(1)}, u32[]{:S(2)}, u32[]{:S(2)}) %collective-permute-start.19) | collective-permute-done | bytes 131104 | tf_op jit(solution)/shard_map/ppermute | solution.py:275
  70.9 1.3 %collective-permute-start.45 = (bf16[4,2,2,32,128]{4,3,2,1,0:T(8,128)(2,1)S(1)}, bf16[4,2,2,32,128]{4,3,2,1,0:T(8,128)(2,1)S(1)}, u32[]{:S(2)}, u32[]{:S(2)}) collective-permute-start(bf16[4,2,2,32,128]{4,3,2,1,0:T(8,128)(2,1)S(1)} %broadcast_select_fusion.8), channel_id=1, source_target_pairs={{0,4},{8,0},{16,8},{24,16},{28,24},{20,28},{12,20},{4,12},{1,5},{9... | collective-permute-start | bytes 393224 | tf_op jit(solution)/shard_map/ppermute | solution.py:275
  74.4 1.8 %collective-permute-done.21.refs_47_ = bf16[4,2,2,32,128]{4,3,2,1,0:T(8,128)(2,1)S(1)} collective-permute-done((bf16[4,2,2,32,128]{4,3,2,1,0:T(8,128)(2,1)S(1)}, bf16[4,2,2,32,128]{4,3,2,1,0:T(8,128)(2,1)S(1)}, u32[]{:S(2)}, u32[]{:S(2)}) %collective-permute-start.21) | collective-permute-done | bytes 131104 | tf_op jit(solution)/shard_map/ppermute | solution.py:275
  77.2 1.3 %collective-permute-start.47 = (bf16[4,2,2,32,128]{4,3,2,1,0:T(8,128)(2,1)S(1)}, bf16[4,2,2,32,128]{4,3,2,1,0:T(8,128)(2,1)S(1)}, u32[]{:S(2)}, u32[]{:S(2)}) collective-permute-start(bf16[4,2,2,32,128]{4,3,2,1,0:T(8,128)(2,1)S(1)} %broadcast_select_fusion.6), channel_id=1, source_target_pairs={{0,4},{8,0},{16,8},{24,16},{28,24},{20,28},{12,20},{4,12},{1,5},{9... | collective-permute-start | bytes 393224 | tf_op jit(solution)/shard_map/ppermute | solution.py:275
  79.3 1.5 %collective-permute-start.24 = (bf16[4,2,2,32,128]{4,3,2,1,0:T(8,128)(2,1)S(1)}, bf16[4,2,2,32,128]{4,3,2,1,0:T(8,128)(2,1)S(1)}, u32[]{:S(2)}, u32[]{:S(2)}) collective-permute-start(bf16[4,2,2,32,128]{4,3,2,1,0:T(8,128)(2,1)S(1)} %broadcast_select_fusion.21), channel_id=1, source_target_pairs={{0,8},{8,16},{16,24},{24,28},{28,20},{20,12},{12,4},{4,0},{1,9},{9... | collective-permute-start | bytes 393224 | tf_op jit(solution)/shard_map/ppermute | solution.py:275
  80.8 1.9 %collective-permute-done.23.refs_49_ = bf16[4,2,2,32,128]{4,3,2,1,0:T(8,128)(2,1)S(1)} collective-permute-done((bf16[4,2,2,32,128]{4,3,2,1,0:T(8,128)(2,1)S(1)}, bf16[4,2,2,32,128]{4,3,2,1,0:T(8,128)(2,1)S(1)}, u32[]{:S(2)}, u32[]{:S(2)}) %collective-permute-start.23) | collective-permute-done | bytes 131104 | tf_op jit(solution)/shard_map/ppermute | solution.py:275
  83.6 1.3 %collective-permute-start.49 = (bf16[4,2,2,32,128]{4,3,2,1,0:T(8,128)(2,1)S(1)}, bf16[4,2,2,32,128]{4,3,2,1,0:T(8,128)(2,1)S(1)}, u32[]{:S(2)}, u32[]{:S(2)}) collective-permute-start(bf16[4,2,2,32,128]{4,3,2,1,0:T(8,128)(2,1)S(1)} %broadcast_select_fusion.4), channel_id=1, source_target_pairs={{0,4},{8,0},{16,8},{24,16},{28,24},{20,28},{12,20},{4,12},{1,5},{9... | collective-permute-start | bytes 393224 | tf_op jit(solution)/shard_map/ppermute | solution.py:275
  86.4 1.5 %collective-permute-start.26 = (bf16[4,2,2,32,128]{4,3,2,1,0:T(8,128)(2,1)S(1)}, bf16[4,2,2,32,128]{4,3,2,1,0:T(8,128)(2,1)S(1)}, u32[]{:S(2)}, u32[]{:S(2)}) collective-permute-start(bf16[4,2,2,32,128]{4,3,2,1,0:T(8,128)(2,1)S(1)} %broadcast_select_fusion.19), channel_id=1, source_target_pairs={{0,8},{8,16},{16,24},{24,28},{28,20},{20,12},{12,4},{4,0},{1,9},{9... | collective-permute-start | bytes 393224 | tf_op jit(solution)/shard_map/ppermute | solution.py:275
  88.0 2.1 %collective-permute-start.27 = (bf16[4,2,2,32,128]{4,3,2,1,0:T(8,128)(2,1)S(1)}, bf16[4,2,2,32,128]{4,3,2,1,0:T(8,128)(2,1)S(1)}, u32[]{:S(2)}, u32[]{:S(2)}) collective-permute-start(bf16[4,2,2,32,128]{4,3,2,1,0:T(8,128)(2,1)S(1)} %broadcast_select_fusion.18), channel_id=1, source_target_pairs={{0,8},{8,16},{16,24},{24,28},{28,20},{20,12},{12,4},{4,0},{1,9},{9... | collective-permute-start | bytes 393224 | tf_op jit(solution)/shard_map/ppermute | solution.py:275
  90.9 1.8 %collective-permute-done.50.refs_76_ = bf16[4,2,2,32,128]{4,3,2,1,0:T(8,128)(2,1)S(1)} collective-permute-done((bf16[4,2,2,32,128]{4,3,2,1,0:T(8,128)(2,1)S(1)}, bf16[4,2,2,32,128]{4,3,2,1,0:T(8,128)(2,1)S(1)}, u32[]{:S(2)}, u32[]{:S(2)}) %collective-permute-start.50) | collective-permute-done | bytes 131104 | tf_op jit(solution)/shard_map/ppermute | solution.py:275
  93.7 1.1 collective-permute-start.28
  94.8 1.2 collective-permute-done.51.refs_77_
  96.1 1.2 collective-permute-start.53
  100.1 1.1 collective-permute-start.30
  103.0 1.1 collective-permute-start.31
  104.0 1.4 %collective-permute-done.54.refs_80_ = bf16[4,2,2,32,128]{4,3,2,1,0:T(8,128)(2,1)S(1)} collective-permute-done((bf16[4,2,2,32,128]{4,3,2,1,0:T(8,128)(2,1)S(1)}, bf16[4,2,2,32,128]{4,3,2,1,0:T(8,128)(2,1)S(1)}, u32[]{:S(2)}, u32[]{:S(2)}) %collective-permute-start.54) | collective-permute-done | bytes 131104 | tf_op jit(solution)/shard_map/ppermute | solution.py:275
  113.5 1.9 %collective-permute-done.58.refs_84_ = bf16[4,2,2,32,128]{4,3,2,1,0:T(8,128)(2,1)S(1)} collective-permute-done((bf16[4,2,2,32,128]{4,3,2,1,0:T(8,128)(2,1)S(1)}, bf16[4,2,2,32,128]{4,3,2,1,0:T(8,128)(2,1)S(1)}, u32[]{:S(2)}, u32[]{:S(2)}) %collective-permute-start.58) | collective-permute-done | bytes 131104 | tf_op jit(solution)/shard_map/ppermute | solution.py:275
  117.4 7.1 %cross.1 = bf16[4,2,2,512,256]{4,3,2,1,0:T(8,128)(2,1)} custom-call(s32[4]{0:T(128)S(1)} %copy-done.3, bf16[2,2,512,128]{3,2,1,0:T(8,128)(2,1)S(1)} %get-tuple-element.143.refs_0_, bf16[2,2,512,128]{3,2,1,0:T(8,128)(2,1)S(1)} %get-tuple-element.144.refs_1_, bf16[2,2,512,128]{3,2,1,0:T(8,128)(2,1)S(1)} %get-tuple-element.145.refs_2_, ...), custom_call_target="tpu_custom_call" | custom-call | tf_op jit(solution)/shard_map/cross/pallas_call | solution.py:278
  (199 shorter events, 38.0 us)
Async XLA Ops:
  4.7 6.5 %collective-permute-start = (f32[288,512]{1,0:T(8,128)}, f32[288,512]{1,0:T(8,128)}, u32[]{:S(2)}, u32[]{:S(2)}) collective-permute-start(f32[288,512]{1,0:T(8,128)} %slice_select_fusion), channel_id=1, source_target_pairs={{0,1},{1,0},{2,3},{3,2},{4,5},{5,4},{6,7},{7,6},{8,9},{9,8},{10,11... | collective-permute-start | bytes 1769480 | tf_op jit(solution)/shard_map/ppermute | solution.py:180
  5.2 5.3 %collective-permute-start.3 = (f32[32,512]{1,0:T(8,128)S(1)}, f32[32,512]{1,0:T(8,128)S(1)}, u32[]{:S(2)}, u32[]{:S(2)}) collective-permute-start(f32[32,512]{1,0:T(8,128)S(1)} %select_add_fusion.1), channel_id=1, source_target_pairs={{0,2},{1,3},{2,0},{3,1},{4,6},{5,7},{6,4},{7,5},{8,10},{9,11},{10,... | collective-permute-start | bytes 196616 | tf_op jit(solution)/shard_map/ppermute | solution.py:180
  10.5 6.1 %collective-permute-start.4 = (f32[32,512]{1,0:T(8,128)S(1)}, f32[32,512]{1,0:T(8,128)S(1)}, u32[]{:S(2)}, u32[]{:S(2)}) collective-permute-start(f32[32,512]{1,0:T(8,128)S(1)} %add.23), channel_id=1, source_target_pairs={{1,4},{3,6},{4,1},{5,8},{6,3},{7,10},{8,5},{9,12},{10,7},{11,14},{... | collective-permute-start | bytes 196616 | tf_op jit(solution)/shard_map/ppermute | solution.py:189
  14.6 7.6 %collective-permute-start.6 = (f32[288,128]{1,0:T(8,128)S(1)}, f32[288,128]{1,0:T(8,128)S(1)}, u32[]{:S(2)}, u32[]{:S(2)}) collective-permute-start(f32[288,128]{1,0:T(8,128)S(1)} %get-tuple-element.285.p_ref), channel_id=1, source_target_pairs={{0,2},{1,3},{2,0},{3,1},{4,6},{5,7},{6,4},{7,5},{8,10},{9,11},{10,... | collective-permute-start | bytes 442376 | tf_op jit(solution)/shard_map/ppermute | solution.py:180
  14.7 17.4 %collective-permute-start.8 = (f32[288,256]{1,0:T(8,128)S(1)}, f32[288,256]{1,0:T(8,128)S(1)}, u32[]{:S(2)}, u32[]{:S(2)}) collective-permute-start(f32[288,256]{1,0:T(8,128)S(1)} %slice.32.p_ref), channel_id=1, source_target_pairs={{0,2},{1,3},{2,0},{3,1},{4,6},{5,7},{6,4},{7,5},{8,10},{9,11},{10,... | collective-permute-start | bytes 884744 | tf_op jit(solution)/shard_map/ppermute | solution.py:180
  18.0 7.3 %collective-permute-start.5 = (f32[256,128]{1,0:T(8,128)S(1)}, f32[256,128]{1,0:T(8,128)S(1)}, u32[]{:S(2)}, u32[]{:S(2)}) collective-permute-start(f32[256,128]{1,0:T(8,128)S(1)} %scale.3.mine_ref), channel_id=1, source_target_pairs={{0,1},{1,0},{2,3},{3,2},{4,5},{5,4},{6,7},{7,6},{8,9},{9,8},{10,11... | collective-permute-start | bytes 393224 | tf_op jit(solution)/shard_map/ppermute | solution.py:180
  22.5 7.8 %collective-permute-start.7 = (f32[256,128]{1,0:T(8,128)S(1)}, f32[256,128]{1,0:T(8,128)S(1)}, u32[]{:S(2)}, u32[]{:S(2)}) collective-permute-start(f32[256,128]{1,0:T(8,128)S(1)} %scale.4.mine_ref), channel_id=1, source_target_pairs={{0,1},{1,0},{2,3},{3,2},{4,5},{5,4},{6,7},{7,6},{8,9},{9,8},{10,11... | collective-permute-start | bytes 393224 | tf_op jit(solution)/shard_map/ppermute | solution.py:180
  26.6 6.4 %collective-permute-start.10 = (bf16[4,2,2,32,128]{4,3,2,1,0:T(8,128)(2,1)S(1)}, bf16[4,2,2,32,128]{4,3,2,1,0:T(8,128)(2,1)S(1)}, u32[]{:S(2)}, u32[]{:S(2)}) collective-permute-start(bf16[4,2,2,32,128]{4,3,2,1,0:T(8,128)(2,1)S(1)} %get-tuple-element.147.refs_4_), channel_id=1, source_target_pairs={{0,8},{8,16},{16,24},{24,28},{28,20},{20,12},{12,4},{4,0},{1,9},{9... | collective-permute-start | bytes 393224 | tf_op jit(solution)/shard_map/ppermute | solution.py:275
  28.3 6.7 %collective-permute-start.11 = (bf16[4,2,2,32,128]{4,3,2,1,0:T(8,128)(2,1)S(1)}, bf16[4,2,2,32,128]{4,3,2,1,0:T(8,128)(2,1)S(1)}, u32[]{:S(2)}, u32[]{:S(2)}) collective-permute-start(bf16[4,2,2,32,128]{4,3,2,1,0:T(8,128)(2,1)S(1)} %get-tuple-element.148.refs_5_), channel_id=1, source_target_pairs={{0,8},{8,16},{16,24},{24,28},{28,20},{20,12},{12,4},{4,0},{1,9},{9... | collective-permute-start | bytes 393224 | tf_op jit(solution)/shard_map/ppermute | solution.py:275
  29.9 6.8 %collective-permute-start.35 = (bf16[4,2,2,32,128]{4,3,2,1,0:T(8,128)(2,1)S(1)}, bf16[4,2,2,32,128]{4,3,2,1,0:T(8,128)(2,1)S(1)}, u32[]{:S(2)}, u32[]{:S(2)}) collective-permute-start(bf16[4,2,2,32,128]{4,3,2,1,0:T(8,128)(2,1)S(1)} %get-tuple-element.163.refs_20_), channel_id=1, source_target_pairs={{0,4},{8,0},{16,8},{24,16},{28,24},{20,28},{12,20},{4,12},{1,5},{9... | collective-permute-start | bytes 393224 | tf_op jit(solution)/shard_map/ppermute | solution.py:275
  30.3 7.2 %collective-permute-start.36 = (bf16[4,2,2,32,128]{4,3,2,1,0:T(8,128)(2,1)S(1)}, bf16[4,2,2,32,128]{4,3,2,1,0:T(8,128)(2,1)S(1)}, u32[]{:S(2)}, u32[]{:S(2)}) collective-permute-start(bf16[4,2,2,32,128]{4,3,2,1,0:T(8,128)(2,1)S(1)} %get-tuple-element.164.refs_21_), channel_id=1, source_target_pairs={{0,4},{8,0},{16,8},{24,16},{28,24},{20,28},{12,20},{4,12},{1,5},{9... | collective-permute-start | bytes 393224 | tf_op jit(solution)/shard_map/ppermute | solution.py:275
  33.0 16.0 %collective-permute-start.9 = (f32[256,256]{1,0:T(8,128)S(1)}, f32[256,256]{1,0:T(8,128)S(1)}, u32[]{:S(2)}, u32[]{:S(2)}) collective-permute-start(f32[256,256]{1,0:T(8,128)S(1)} %scale.5.mine_ref), channel_id=1, source_target_pairs={{0,1},{1,0},{2,3},{3,2},{4,5},{5,4},{6,7},{7,6},{8,9},{9,8},{10,11... | collective-permute-start | bytes 786440 | tf_op jit(solution)/shard_map/ppermute | solution.py:180
  33.1 6.4 %collective-permute-start.12 = (bf16[4,2,2,32,128]{4,3,2,1,0:T(8,128)(2,1)S(1)}, bf16[4,2,2,32,128]{4,3,2,1,0:T(8,128)(2,1)S(1)}, u32[]{:S(2)}, u32[]{:S(2)}) collective-permute-start(bf16[4,2,2,32,128]{4,3,2,1,0:T(8,128)(2,1)S(1)} %broadcast_select_fusion.33), channel_id=1, source_target_pairs={{0,8},{8,16},{16,24},{24,28},{28,20},{20,12},{12,4},{4,0},{1,9},{9... | collective-permute-start | bytes 393224 | tf_op jit(solution)/shard_map/ppermute | solution.py:275
  35.0 6.9 %collective-permute-start.13 = (bf16[4,2,2,32,128]{4,3,2,1,0:T(8,128)(2,1)S(1)}, bf16[4,2,2,32,128]{4,3,2,1,0:T(8,128)(2,1)S(1)}, u32[]{:S(2)}, u32[]{:S(2)}) collective-permute-start(bf16[4,2,2,32,128]{4,3,2,1,0:T(8,128)(2,1)S(1)} %broadcast_select_fusion.32), channel_id=1, source_target_pairs={{0,8},{8,16},{16,24},{24,28},{28,20},{20,12},{12,4},{4,0},{1,9},{9... | collective-permute-start | bytes 393224 | tf_op jit(solution)/shard_map/ppermute | solution.py:275
  36.6 6.4 %collective-permute-start.37 = (bf16[4,2,2,32,128]{4,3,2,1,0:T(8,128)(2,1)S(1)}, bf16[4,2,2,32,128]{4,3,2,1,0:T(8,128)(2,1)S(1)}, u32[]{:S(2)}, u32[]{:S(2)}) collective-permute-start(bf16[4,2,2,32,128]{4,3,2,1,0:T(8,128)(2,1)S(1)} %broadcast_select_fusion.16), channel_id=1, source_target_pairs={{0,4},{8,0},{16,8},{24,16},{28,24},{20,28},{12,20},{4,12},{1,5},{9... | collective-permute-start | bytes 393224 | tf_op jit(solution)/shard_map/ppermute | solution.py:275
  37.6 7.0 %collective-permute-start.38 = (bf16[4,2,2,32,128]{4,3,2,1,0:T(8,128)(2,1)S(1)}, bf16[4,2,2,32,128]{4,3,2,1,0:T(8,128)(2,1)S(1)}, u32[]{:S(2)}, u32[]{:S(2)}) collective-permute-start(bf16[4,2,2,32,128]{4,3,2,1,0:T(8,128)(2,1)S(1)} %broadcast_select_fusion.15), channel_id=1, source_target_pairs={{0,4},{8,0},{16,8},{24,16},{28,24},{20,28},{12,20},{4,12},{1,5},{9... | collective-permute-start | bytes 393224 | tf_op jit(solution)/shard_map/ppermute | solution.py:275
  44.6 5.8 %collective-permute-start.14 = (bf16[4,2,2,32,128]{4,3,2,1,0:T(8,128)(2,1)S(1)}, bf16[4,2,2,32,128]{4,3,2,1,0:T(8,128)(2,1)S(1)}, u32[]{:S(2)}, u32[]{:S(2)}) collective-permute-start(bf16[4,2,2,32,128]{4,3,2,1,0:T(8,128)(2,1)S(1)} %broadcast_select_fusion.31), channel_id=1, source_target_pairs={{0,8},{8,16},{16,24},{24,28},{28,20},{20,12},{12,4},{4,0},{1,9},{9... | collective-permute-start | bytes 393224 | tf_op jit(solution)/shard_map/ppermute | solution.py:275
  46.3 6.4 %collective-permute-start.15 = (bf16[4,2,2,32,128]{4,3,2,1,0:T(8,128)(2,1)S(1)}, bf16[4,2,2,32,128]{4,3,2,1,0:T(8,128)(2,1)S(1)}, u32[]{:S(2)}, u32[]{:S(2)}) collective-permute-start(bf16[4,2,2,32,128]{4,3,2,1,0:T(8,128)(2,1)S(1)} %broadcast_select_fusion.30), channel_id=1, source_target_pairs={{0,8},{8,16},{16,24},{24,28},{28,20},{20,12},{12,4},{4,0},{1,9},{9... | collective-permute-start | bytes 393224 | tf_op jit(solution)/shard_map/ppermute | solution.py:275
  47.1 7.2 %collective-permute-start.39 = (bf16[4,2,2,32,128]{4,3,2,1,0:T(8,128)(2,1)S(1)}, bf16[4,2,2,32,128]{4,3,2,1,0:T(8,128)(2,1)S(1)}, u32[]{:S(2)}, u32[]{:S(2)}) collective-permute-start(bf16[4,2,2,32,128]{4,3,2,1,0:T(8,128)(2,1)S(1)} %broadcast_select_fusion.14), channel_id=1, source_target_pairs={{0,4},{8,0},{16,8},{24,16},{28,24},{20,28},{12,20},{4,12},{1,5},{9... | collective-permute-start | bytes 393224 | tf_op jit(solution)/shard_map/ppermute | solution.py:275
  48.5 6.4 %collective-permute-start.40 = (bf16[4,2,2,32,128]{4,3,2,1,0:T(8,128)(2,1)S(1)}, bf16[4,2,2,32,128]{4,3,2,1,0:T(8,128)(2,1)S(1)}, u32[]{:S(2)}, u32[]{:S(2)}) collective-permute-start(bf16[4,2,2,32,128]{4,3,2,1,0:T(8,128)(2,1)S(1)} %broadcast_select_fusion.13), channel_id=1, source_target_pairs={{0,4},{8,0},{16,8},{24,16},{28,24},{20,28},{12,20},{4,12},{1,5},{9... | collective-permute-start | bytes 393224 | tf_op jit(solution)/shard_map/ppermute | solution.py:275
  50.4 5.5 %collective-permute-start.16 = (bf16[4,2,2,32,128]{4,3,2,1,0:T(8,128)(2,1)S(1)}, bf16[4,2,2,32,128]{4,3,2,1,0:T(8,128)(2,1)S(1)}, u32[]{:S(2)}, u32[]{:S(2)}) collective-permute-start(bf16[4,2,2,32,128]{4,3,2,1,0:T(8,128)(2,1)S(1)} %broadcast_select_fusion.29), channel_id=1, source_target_pairs={{0,8},{8,16},{16,24},{24,28},{28,20},{20,12},{12,4},{4,0},{1,9},{9... | collective-permute-start | bytes 393224 | tf_op jit(solution)/shard_map/ppermute | solution.py:275
  54.9 5.9 %collective-permute-start.42 = (bf16[4,2,2,32,128]{4,3,2,1,0:T(8,128)(2,1)S(1)}, bf16[4,2,2,32,128]{4,3,2,1,0:T(8,128)(2,1)S(1)}, u32[]{:S(2)}, u32[]{:S(2)}) collective-permute-start(bf16[4,2,2,32,128]{4,3,2,1,0:T(8,128)(2,1)S(1)} %broadcast_select_fusion.11), channel_id=1, source_target_pairs={{0,4},{8,0},{16,8},{24,16},{28,24},{20,28},{12,20},{4,12},{1,5},{9... | collective-permute-start | bytes 393224 | tf_op jit(solution)/shard_map/ppermute | solution.py:275
  60.8 6.4 %collective-permute-start.18 = (bf16[4,2,2,32,128]{4,3,2,1,0:T(8,128)(2,1)S(1)}, bf16[4,2,2,32,128]{4,3,2,1,0:T(8,128)(2,1)S(1)}, u32[]{:S(2)}, u32[]{:S(2)}) collective-permute-start(bf16[4,2,2,32,128]{4,3,2,1,0:T(8,128)(2,1)S(1)} %broadcast_select_fusion.27), channel_id=1, source_target_pairs={{0,8},{8,16},{16,24},{24,28},{28,20},{20,12},{12,4},{4,0},{1,9},{9... | collective-permute-start | bytes 393224 | tf_op jit(solution)/shard_map/ppermute | solution.py:275
  61.6 8.4 %collective-permute-start.19 = (bf16[4,2,2,32,128]{4,3,2,1,0:T(8,128)(2,1)S(1)}, bf16[4,2,2,32,128]{4,3,2,1,0:T(8,128)(2,1)S(1)}, u32[]{:S(2)}, u32[]{:S(2)}) collective-permute-start(bf16[4,2,2,32,128]{4,3,2,1,0:T(8,128)(2,1)S(1)} %broadcast_select_fusion.26), channel_id=1, source_target_pairs={{0,8},{8,16},{16,24},{24,28},{28,20},{20,12},{12,4},{4,0},{1,9},{9... | collective-permute-start | bytes 393224 | tf_op jit(solution)/shard_map/ppermute | solution.py:275
  63.4 7.5 %collective-permute-start.43 = (bf16[4,2,2,32,128]{4,3,2,1,0:T(8,128)(2,1)S(1)}, bf16[4,2,2,32,128]{4,3,2,1,0:T(8,128)(2,1)S(1)}, u32[]{:S(2)}, u32[]{:S(2)}) collective-permute-start(bf16[4,2,2,32,128]{4,3,2,1,0:T(8,128)(2,1)S(1)} %broadcast_select_fusion.10), channel_id=1, source_target_pairs={{0,4},{8,0},{16,8},{24,16},{28,24},{20,28},{12,20},{4,12},{1,5},{9... | collective-permute-start | bytes 393224 | tf_op jit(solution)/shard_map/ppermute | solution.py:275
  63.8 8.4 %collective-permute-start.44 = (bf16[4,2,2,32,128]{4,3,2,1,0:T(8,128)(2,1)S(1)}, bf16[4,2,2,32,128]{4,3,2,1,0:T(8,128)(2,1)S(1)}, u32[]{:S(2)}, u32[]{:S(2)}) collective-permute-start(bf16[4,2,2,32,128]{4,3,2,1,0:T(8,128)(2,1)S(1)} %broadcast_select_fusion.9), channel_id=1, source_target_pairs={{0,4},{8,0},{16,8},{24,16},{28,24},{20,28},{12,20},{4,12},{1,5},{9... | collective-permute-start | bytes 393224 | tf_op jit(solution)/shard_map/ppermute | solution.py:275
  67.3 6.2 %collective-permute-start.20 = (bf16[4,2,2,32,128]{4,3,2,1,0:T(8,128)(2,1)S(1)}, bf16[4,2,2,32,128]{4,3,2,1,0:T(8,128)(2,1)S(1)}, u32[]{:S(2)}, u32[]{:S(2)}) collective-permute-start(bf16[4,2,2,32,128]{4,3,2,1,0:T(8,128)(2,1)S(1)} %broadcast_select_fusion.25), channel_id=1, source_target_pairs={{0,8},{8,16},{16,24},{24,28},{28,20},{20,12},{12,4},{4,0},{1,9},{9... | collective-permute-start | bytes 393224 | tf_op jit(solution)/shard_map/ppermute | solution.py:275
  70.1 6.2 %collective-permute-start.21 = (bf16[4,2,2,32,128]{4,3,2,1,0:T(8,128)(2,1)S(1)}, bf16[4,2,2,32,128]{4,3,2,1,0:T(8,128)(2,1)S(1)}, u32[]{:S(2)}, u32[]{:S(2)}) collective-permute-start(bf16[4,2,2,32,128]{4,3,2,1,0:T(8,128)(2,1)S(1)} %broadcast_select_fusion.24), channel_id=1, source_target_pairs={{0,8},{8,16},{16,24},{24,28},{28,20},{20,12},{12,4},{4,0},{1,9},{9... | collective-permute-start | bytes 393224 | tf_op jit(solution)/shard_map/ppermute | solution.py:275
  70.9 6.3 %collective-permute-start.45 = (bf16[4,2,2,32,128]{4,3,2,1,0:T(8,128)(2,1)S(1)}, bf16[4,2,2,32,128]{4,3,2,1,0:T(8,128)(2,1)S(1)}, u32[]{:S(2)}, u32[]{:S(2)}) collective-permute-start(bf16[4,2,2,32,128]{4,3,2,1,0:T(8,128)(2,1)S(1)} %broadcast_select_fusion.8), channel_id=1, source_target_pairs={{0,4},{8,0},{16,8},{24,16},{28,24},{20,28},{12,20},{4,12},{1,5},{9... | collective-permute-start | bytes 393224 | tf_op jit(solution)/shard_map/ppermute | solution.py:275
  72.3 6.2 %collective-permute-start.46 = (bf16[4,2,2,32,128]{4,3,2,1,0:T(8,128)(2,1)S(1)}, bf16[4,2,2,32,128]{4,3,2,1,0:T(8,128)(2,1)S(1)}, u32[]{:S(2)}, u32[]{:S(2)}) collective-permute-start(bf16[4,2,2,32,128]{4,3,2,1,0:T(8,128)(2,1)S(1)} %broadcast_select_fusion.7), channel_id=1, source_target_pairs={{0,4},{8,0},{16,8},{24,16},{28,24},{20,28},{12,20},{4,12},{1,5},{9... | collective-permute-start | bytes 393224 | tf_op jit(solution)/shard_map/ppermute | solution.py:275
  73.5 5.9 %collective-permute-start.22 = (bf16[4,2,2,32,128]{4,3,2,1,0:T(8,128)(2,1)S(1)}, bf16[4,2,2,32,128]{4,3,2,1,0:T(8,128)(2,1)S(1)}, u32[]{:S(2)}, u32[]{:S(2)}) collective-permute-start(bf16[4,2,2,32,128]{4,3,2,1,0:T(8,128)(2,1)S(1)} %broadcast_select_fusion.23), channel_id=1, source_target_pairs={{0,8},{8,16},{16,24},{24,28},{28,20},{20,12},{12,4},{4,0},{1,9},{9... | collective-permute-start | bytes 393224 | tf_op jit(solution)/shard_map/ppermute | solution.py:275
  76.3 6.4 %collective-permute-start.23 = (bf16[4,2,2,32,128]{4,3,2,1,0:T(8,128)(2,1)S(1)}, bf16[4,2,2,32,128]{4,3,2,1,0:T(8,128)(2,1)S(1)}, u32[]{:S(2)}, u32[]{:S(2)}) collective-permute-start(bf16[4,2,2,32,128]{4,3,2,1,0:T(8,128)(2,1)S(1)} %broadcast_select_fusion.22), channel_id=1, source_target_pairs={{0,8},{8,16},{16,24},{24,28},{28,20},{20,12},{12,4},{4,0},{1,9},{9... | collective-permute-start | bytes 393224 | tf_op jit(solution)/shard_map/ppermute | solution.py:275
  77.2 6.4 %collective-permute-start.47 = (bf16[4,2,2,32,128]{4,3,2,1,0:T(8,128)(2,1)S(1)}, bf16[4,2,2,32,128]{4,3,2,1,0:T(8,128)(2,1)S(1)}, u32[]{:S(2)}, u32[]{:S(2)}) collective-permute-start(bf16[4,2,2,32,128]{4,3,2,1,0:T(8,128)(2,1)S(1)} %broadcast_select_fusion.6), channel_id=1, source_target_pairs={{0,4},{8,0},{16,8},{24,16},{28,24},{20,28},{12,20},{4,12},{1,5},{9... | collective-permute-start | bytes 393224 | tf_op jit(solution)/shard_map/ppermute | solution.py:275
  78.5 6.8 %collective-permute-start.48 = (bf16[4,2,2,32,128]{4,3,2,1,0:T(8,128)(2,1)S(1)}, bf16[4,2,2,32,128]{4,3,2,1,0:T(8,128)(2,1)S(1)}, u32[]{:S(2)}, u32[]{:S(2)}) collective-permute-start(bf16[4,2,2,32,128]{4,3,2,1,0:T(8,128)(2,1)S(1)} %broadcast_select_fusion.5), channel_id=1, source_target_pairs={{0,4},{8,0},{16,8},{24,16},{28,24},{20,28},{12,20},{4,12},{1,5},{9... | collective-permute-start | bytes 393224 | tf_op jit(solution)/shard_map/ppermute | solution.py:275
  79.3 7.1 %collective-permute-start.24 = (bf16[4,2,2,32,128]{4,3,2,1,0:T(8,128)(2,1)S(1)}, bf16[4,2,2,32,128]{4,3,2,1,0:T(8,128)(2,1)S(1)}, u32[]{:S(2)}, u32[]{:S(2)}) collective-permute-start(bf16[4,2,2,32,128]{4,3,2,1,0:T(8,128)(2,1)S(1)} %broadcast_select_fusion.21), channel_id=1, source_target_pairs={{0,8},{8,16},{16,24},{24,28},{28,20},{20,12},{12,4},{4,0},{1,9},{9... | collective-permute-start | bytes 393224 | tf_op jit(solution)/shard_map/ppermute | solution.py:275
  83.6 6.4 %collective-permute-start.49 = (bf16[4,2,2,32,128]{4,3,2,1,0:T(8,128)(2,1)S(1)}, bf16[4,2,2,32,128]{4,3,2,1,0:T(8,128)(2,1)S(1)}, u32[]{:S(2)}, u32[]{:S(2)}) collective-permute-start(bf16[4,2,2,32,128]{4,3,2,1,0:T(8,128)(2,1)S(1)} %broadcast_select_fusion.4), channel_id=1, source_target_pairs={{0,4},{8,0},{16,8},{24,16},{28,24},{20,28},{12,20},{4,12},{1,5},{9... | collective-permute-start | bytes 393224 | tf_op jit(solution)/shard_map/ppermute | solution.py:275
  85.4 7.3 %collective-permute-start.50 = (bf16[4,2,2,32,128]{4,3,2,1,0:T(8,128)(2,1)S(1)}, bf16[4,2,2,32,128]{4,3,2,1,0:T(8,128)(2,1)S(1)}, u32[]{:S(2)}, u32[]{:S(2)}) collective-permute-start(bf16[4,2,2,32,128]{4,3,2,1,0:T(8,128)(2,1)S(1)} %broadcast_select_fusion.3), channel_id=1, source_target_pairs={{0,4},{8,0},{16,8},{24,16},{28,24},{20,28},{12,20},{4,12},{1,5},{9... | collective-permute-start | bytes 393224 | tf_op jit(solution)/shard_map/ppermute | solution.py:275
  86.4 7.3 %collective-permute-start.26 = (bf16[4,2,2,32,128]{4,3,2,1,0:T(8,128)(2,1)S(1)}, bf16[4,2,2,32,128]{4,3,2,1,0:T(8,128)(2,1)S(1)}, u32[]{:S(2)}, u32[]{:S(2)}) collective-permute-start(bf16[4,2,2,32,128]{4,3,2,1,0:T(8,128)(2,1)S(1)} %broadcast_select_fusion.19), channel_id=1, source_target_pairs={{0,8},{8,16},{16,24},{24,28},{28,20},{20,12},{12,4},{4,0},{1,9},{9... | collective-permute-start | bytes 393224 | tf_op jit(solution)/shard_map/ppermute | solution.py:275
  88.0 9.3 %collective-permute-start.27 = (bf16[4,2,2,32,128]{4,3,2,1,0:T(8,128)(2,1)S(1)}, bf16[4,2,2,32,128]{4,3,2,1,0:T(8,128)(2,1)S(1)}, u32[]{:S(2)}, u32[]{:S(2)}) collective-permute-start(bf16[4,2,2,32,128]{4,3,2,1,0:T(8,128)(2,1)S(1)} %broadcast_select_fusion.18), channel_id=1, source_target_pairs={{0,8},{8,16},{16,24},{24,28},{28,20},{20,12},{12,4},{4,0},{1,9},{9... | collective-permute-start | bytes 393224 | tf_op jit(solution)/shard_map/ppermute | solution.py:275
  90.1 6.0 %collective-permute-start.51 = (bf16[4,2,2,32,128]{4,3,2,1,0:T(8,128)(2,1)S(1)}, bf16[4,2,2,32,128]{4,3,2,1,0:T(8,128)(2,1)S(1)}, u32[]{:S(2)}, u32[]{:S(2)}) collective-permute-start(bf16[4,2,2,32,128]{4,3,2,1,0:T(8,128)(2,1)S(1)} %broadcast_select_fusion.2), channel_id=1, source_target_pairs={{0,4},{8,0},{16,8},{24,16},{28,24},{20,28},{12,20},{4,12},{1,5},{9... | collective-permute-start | bytes 393224 | tf_op jit(solution)/shard_map/ppermute | solution.py:275
  92.7 6.4 %collective-permute-start.52 = (bf16[4,2,2,32,128]{4,3,2,1,0:T(8,128)(2,1)S(1)}, bf16[4,2,2,32,128]{4,3,2,1,0:T(8,128)(2,1)S(1)}, u32[]{:S(2)}, u32[]{:S(2)}) collective-permute-start(bf16[4,2,2,32,128]{4,3,2,1,0:T(8,128)(2,1)S(1)} %broadcast_select_fusion.1), channel_id=1, source_target_pairs={{0,4},{8,0},{16,8},{24,16},{28,24},{20,28},{12,20},{4,12},{1,5},{9... | collective-permute-start | bytes 393224 | tf_op jit(solution)/shard_map/ppermute | solution.py:275
  93.7 6.3 %collective-permute-start.28 = (bf16[4,2,2,32,128]{4,3,2,1,0:T(8,128)(2,1)S(1)}, bf16[4,2,2,32,128]{4,3,2,1,0:T(8,128)(2,1)S(1)}, u32[]{:S(2)}, u32[]{:S(2)}) collective-permute-start(bf16[4,2,2,32,128]{4,3,2,1,0:T(8,128)(2,1)S(1)} %broadcast_select_fusion.17), channel_id=1, source_target_pairs={{0,8},{8,16},{16,24},{24,28},{28,20},{20,12},{12,4},{4,0},{1,9},{9... | collective-permute-start | bytes 393224 | tf_op jit(solution)/shard_map/ppermute | solution.py:275
  96.1 5.9 %collective-permute-start.53 = (bf16[4,2,2,32,128]{4,3,2,1,0:T(8,128)(2,1)S(1)}, bf16[4,2,2,32,128]{4,3,2,1,0:T(8,128)(2,1)S(1)}, u32[]{:S(2)}, u32[]{:S(2)}) collective-permute-start(bf16[4,2,2,32,128]{4,3,2,1,0:T(8,128)(2,1)S(1)} %broadcast_select_fusion), channel_id=1, source_target_pairs={{0,4},{8,0},{16,8},{24,16},{28,24},{20,28},{12,20},{4,12},{1,5},{9... | collective-permute-start | bytes 393224 | tf_op jit(solution)/shard_map/ppermute | solution.py:275
  97.3 5.7 %collective-permute-start.29 = (bf16[4,2,2,32,128]{4,3,2,1,0:T(8,128)(2,1)S(1)}, bf16[4,2,2,32,128]{4,3,2,1,0:T(8,128)(2,1)S(1)}, u32[]{:S(2)}, u32[]{:S(2)}) collective-permute-start(bf16[4,2,2,32,128]{4,3,2,1,0:T(8,128)(2,1)S(1)} %collective-permute-done.27.refs_53_), channel_id=1, source_target_pairs={{0,8},{8,16},{16,24},{24,28},{28,20},{20,12},{12,4},{4,0},{1,9},{9... | collective-permute-start | bytes 393224 | tf_op jit(solution)/shard_map/ppermute | solution.py:275
  99.1 6.3 %collective-permute-start.54 = (bf16[4,2,2,32,128]{4,3,2,1,0:T(8,128)(2,1)S(1)}, bf16[4,2,2,32,128]{4,3,2,1,0:T(8,128)(2,1)S(1)}, u32[]{:S(2)}, u32[]{:S(2)}) collective-permute-start(bf16[4,2,2,32,128]{4,3,2,1,0:T(8,128)(2,1)S(1)} %collective-permute-done.52.refs_78_), channel_id=1, source_target_pairs={{0,4},{8,0},{16,8},{24,16},{28,24},{20,28},{12,20},{4,12},{1,5},{9... | collective-permute-start | bytes 393224 | tf_op jit(solution)/shard_map/ppermute | solution.py:275
  100.1 6.4 %collective-permute-start.30 = (bf16[4,2,2,32,128]{4,3,2,1,0:T(8,128)(2,1)S(1)}, bf16[4,2,2,32,128]{4,3,2,1,0:T(8,128)(2,1)S(1)}, u32[]{:S(2)}, u32[]{:S(2)}) collective-permute-start(bf16[4,2,2,32,128]{4,3,2,1,0:T(8,128)(2,1)S(1)} %collective-permute-done.28.refs_54_), channel_id=1, source_target_pairs={{0,8},{8,16},{16,24},{24,28},{28,20},{20,12},{12,4},{4,0},{1,9},{9... | collective-permute-start | bytes 393224 | tf_op jit(solution)/shard_map/ppermute | solution.py:275
  102.0 5.4 %collective-permute-start.55 = (bf16[4,2,2,32,128]{4,3,2,1,0:T(8,128)(2,1)S(1)}, bf16[4,2,2,32,128]{4,3,2,1,0:T(8,128)(2,1)S(1)}, u32[]{:S(2)}, u32[]{:S(2)}) collective-permute-start(bf16[4,2,2,32,128]{4,3,2,1,0:T(8,128)(2,1)S(1)} %collective-permute-done.53.refs_79_), channel_id=1, source_target_pairs={{0,4},{8,0},{16,8},{24,16},{28,24},{20,28},{12,20},{4,12},{1,5},{9... | collective-permute-start | bytes 393224 | tf_op jit(solution)/shard_map/ppermute | solution.py:275
  103.0 5.5 %collective-permute-start.31 = (bf16[4,2,2,32,128]{4,3,2,1,0:T(8,128)(2,1)S(1)}, bf16[4,2,2,32,128]{4,3,2,1,0:T(8,128)(2,1)S(1)}, u32[]{:S(2)}, u32[]{:S(2)}) collective-permute-start(bf16[4,2,2,32,128]{4,3,2,1,0:T(8,128)(2,1)S(1)} %collective-permute-done.29.refs_55_), channel_id=1, source_target_pairs={{0,8},{8,16},{16,24},{24,28},{28,20},{20,12},{12,4},{4,0},{1,9},{9... | collective-permute-start | bytes 393224 | tf_op jit(solution)/shard_map/ppermute | solution.py:275
  (16 other events, 123.7 us)

commit v3 on v2

--- a/solution.py
+++ b/solution.py
@@ -28,6 +28,12 @@
     single = n_chunks - both
     n_sends = single + 2 * both
     return single, n_sends, max(single + LAG * (n_chan - 2), n_sends + LAG * (n_chan // 2 - 1))
+
+
+def early_groups(n_chan, groups):
+    single, _, n_steps = plan(n_chan, groups * SUBS)
+    whole = min(single, n_steps - 2 - LAG * (n_chan - 2))
+    return min(max(whole, 0) // SUBS, groups - 1)
 
 
 def scale_kernel(channels, bins, p_ref, q_ref, edge_ref, w_ref, scale_ref, s_ref, t_ref):
@@ -109,15 +115,23 @@
                         own[g * per + i][p, f, k] = n_ref[f, k, at, :].astype(jnp.bfloat16)
 
 
-def cross_kernel(groups, n_chan, n_chunks, n_steps, single, scaling, block_ref, *refs):
+def cross_kernel(base, groups, n_chan, n_chunks, n_steps, single, scaling, block_ref, *refs):
     normed, refs = refs[:groups], refs[groups:]
     lists = []
     for size in (n_chunks, n_chunks, n_steps, n_steps):
         lists.append(refs[:size])
         refs = refs[size:]
-    (out_ref,) = refs
-    per = n_chunks // groups
+    out_ref = refs[-1]
+    per = SUBS
     panel = pl.program_id(0)
+
+    def store(f, part, value):
+        if scaling is None:
+            out_ref[panel, f, part] = value
+            return
+        if len(refs) > 1:
+            value = value + refs[0][panel, f, part]
+        out_ref[0, f, part] = (value * scaling).astype(jnp.bfloat16)
 
     def place(c):
         return jnp.where(lax.rem(c, 2) == 0, c // 2, n_chan - 1 - c // 2)
@@ -144,7 +158,7 @@
                 right = jnp.concatenate(
                     [
                         jnp.concatenate(
-                            [source(d, half, g * per + j)[panel, f, k] for half in range(2) for j in range(per)], axis=0
+                            [source(d, half, (base + g) * per + j)[panel, f, k] for half in range(2) for j in range(per)], axis=0
                         )
                         for k in range(2)
                         for g in range(groups)
@@ -152,9 +166,9 @@
                     axis=1,
                 )
                 real = dot(jnp.concatenate(left[0] + left[1], axis=1), right)
-                out_ref[0, f, 0] = (real * scaling).astype(jnp.bfloat16)
+                store(f, 0, real)
                 imag = dot(jnp.concatenate(left[1] + [-n for n in left[0]], axis=1), right)
-                out_ref[0, f, 1] = (imag * scaling).astype(jnp.bfloat16)
+                store(f, 1, imag)
 
 
 def local(spectra, half_width, panel_block, panel_offset):
@@ -255,6 +269,7 @@
 
     n_chunks = groups * SUBS
     single, n_sends, n_steps = plan(n_chan, n_chunks)
+    n_ready = early_groups(n_chan, groups) * SUBS + LAG * (n_chan - 2)
     got = [[], []]
     rest = [own[half][c] for c in range(single, n_chunks) for half in range(2)]
     sends = [own[half][:single] + rest for half in range(2)]
@@ -274,17 +289,32 @@
             pairs = [(ring[i], ring[(i + step) % n_chan]) for i in range(n_chan)]
             got[half].append(lax.ppermute(value, "chan", pairs))
 
-    block = (1, f_dev, parts, ch_dev, PANEL)
+    block = (f_dev, parts, ch_dev, PANEL)
+    messages = [*own[0], *own[1], *got[0], *got[1]]
+    ahead = early_groups(n_chan, groups)
+    sums = []
+    if ahead:
+        early = pl.pallas_call(
+            functools.partial(cross_kernel, 0, ahead, n_chan, n_chunks, n_ready, single, None),
+            grid=(NPANEL,),
+            out_shape=pltpu.VMEM((NPANEL, *block), jnp.float32),
+            in_specs=[pl.BlockSpec(memory_space=pltpu.SMEM)] + [vmem] * (ahead + 2 * n_chunks + 2 * n_ready),
+            out_specs=vmem,
+            compiler_params=pltpu.CompilerParams(vmem_limit_bytes=16 << 20),
+            name="early",
+        )
+        sums = [early(panel_block, *normed[:ahead], *own[0], *own[1], *got[0][:n_ready], *got[1][:n_ready])]
     return pl.pallas_call(
-        functools.partial(cross_kernel, groups, n_chan, n_chunks, n_steps, single, windows ** (-0.5)),
+        functools.partial(
+            cross_kernel, ahead, groups - ahead, n_chan, n_chunks, n_steps, single, windows ** (-0.5)
+        ),
         grid=(NPANEL,),
-        out_shape=jax.ShapeDtypeStruct((NPANEL, f_dev, parts, ch_dev, PANEL), jnp.bfloat16),
-        in_specs=[pl.BlockSpec(memory_space=pltpu.SMEM)]
-        + [vmem] * (groups + 2 * n_chunks + 2 * n_steps),
-        out_specs=pl.BlockSpec(block, lambda p: (p, 0, 0, 0, 0)),
+        out_shape=jax.ShapeDtypeStruct((NPANEL, *block), jnp.bfloat16),
+        in_specs=[pl.BlockSpec(memory_space=pltpu.SMEM)] + [vmem] * (groups - ahead + len(messages) + len(sums)),
+        out_specs=pl.BlockSpec((1, *block), lambda p: (p, 0, 0, 0, 0)),
         compiler_params=pltpu.CompilerParams(vmem_limit_bytes=20 << 20),
         name="cross",
-    )(panel_block, *normed, *own[0], *own[1], *got[0], *got[1])
+    )(panel_block, *normed[ahead:], *messages, *sums)
 
 
 def solution(mesh):

time: 125 us -> 123 us (0.984)
  waiting for transfers between devices: 35.4 us -> 31.7 us
  Pallas kernels: 12.7 us -> 14.5 us
    ppermute x50, waiting for transfers between devices: 32 us -> 28.4 us  [local(): got[half].append(lax.ppermute(value, 'chan', pairs))]
    pallas_call x1 -> x2, Pallas kernels: 7.07 us -> 8.87 us  [the longest x1 5.07 us: local(): pl.pallas_call(functools.partial(cross_kernel, ahead, groups - ahead, n_c...]
  transfers between devices with their start and end apart: 60 -> 60, of which waited for: 29 -> 27; matrix products, arithmetic and copies ran while one was open for 4% -> 4% of each run, Pallas kernels for 5% -> 8%
where the time goes in v3:
time: 123 us; the launch traced here: 122 us
  starting transfers between devices  69.2 us (56%)
  waiting for transfers between devices  31.7 us (26%)
  Pallas kernels  14.5 us (12%)
  other arithmetic  6.36 us (5%)
    ppermute x50, starting transfers between devices, local(): got[half].append(lax.ppermute(value, 'chan', pairs))  53.8 us
    ppermute x50, waiting for transfers between devices, local(): got[half].append(lax.ppermute(value, 'chan', pairs))  28.4 us
    ppermute x9, starting transfers between devices, flip(): return lax.ppermute(block, 'band', [(b, b ^ bit) for b in range(n_band)])  14.8 us
    pallas_call x1, Pallas kernels, local(): pl.pallas_call(functools.partial(cross_kernel, ahead, groups - ahead, n_c...  5.07 us
    pallas_call x3, Pallas kernels, local(): outs = norm(panel_offset, scale, other, spectra)  4.05 us
    pallas_call x1, Pallas kernels, local(): early(panel_block, *normed[:ahead], *own[0], *own[1], *got[0][:n_ready],...  3.8 us
    ppermute x9, waiting for transfers between devices, flip(): return lax.ppermute(block, 'band', [(b, b ^ bit) for b in range(n_band)])  3.32 us
    reduce_sum x2, other arithmetic, power_of(): return jnp.sum(jnp.square(block.astype(jnp.float32)), axis=(0, 1))  3.19 us
  transfers between devices with their start and end apart: 60, of which 27 were waited for; matrix products, arithmetic and copies ran while one was open for 4% of the time, Pallas kernels for 8%

profile of v3, /device:TPU:0, one launch (start us, length us, event | category | flops | bytes accessed | tf_op | source)
XLA Modules:
  0.0 122.5 jit_solution(16116868555191218169)
XLA Ops:
  1.6 2.2 %multiply_reduce_fusion = f32[512,512]{1,0:T(8,128)S(1)} fusion(bf16[2,2,512,512]{3,2,1,0:T(8,128)(2,1)} %x_ref.5), kind=kLoop, calls=%fused_computation | loop fusion | flops 2883584 | bytes 3145728 | tf_op jit(solution)/shard_map/reduce_sum | solution.py:206
  5.2 3.1 %collective-permute-start.3 = (f32[32,512]{1,0:T(8,128)S(1)}, f32[32,512]{1,0:T(8,128)S(1)}, u32[]{:S(2)}, u32[]{:S(2)}) collective-permute-start(f32[32,512]{1,0:T(8,128)S(1)} %select_add_fusion.1), channel_id=1, source_target_pairs={{0,2},{1,3},{2,0},{3,1},{4,6},{5,7},{6,4},{7,5},{8,10},{9,11},{10,... | collective-permute-start | bytes 196616 | tf_op jit(solution)/shard_map/ppermute | solution.py:194
  8.2 2.3 %collective-permute-done.3 = f32[32,512]{1,0:T(8,128)S(1)} collective-permute-done((f32[32,512]{1,0:T(8,128)S(1)}, f32[32,512]{1,0:T(8,128)S(1)}, u32[]{:S(2)}, u32[]{:S(2)}) %collective-permute-start.3) | collective-permute-done | bytes 65568 | tf_op jit(solution)/shard_map/ppermute | solution.py:194
  11.2 1.2 %select_add_fusion = f32[288,512]{1,0:T(8,128)S(1)} fusion(f32[288,512]{1,0:T(8,128)} %collective-permute-done, f32[512,512]{1,0:T(8,128)S(1)} %multiply_reduce_fusion, pred[]{:T(512)S(6)} %eq.11), kind=kLoop, calls=%fused_computation.1 | loop fusion | flops 294912 | bytes 2359297 | tf_op jit(solution)/shard_map/add | solution.py:212
  12.5 2.1 %collective-permute-start.6 = (f32[288,128]{1,0:T(8,128)S(1)}, f32[288,128]{1,0:T(8,128)S(1)}, u32[]{:S(2)}, u32[]{:S(2)}) collective-permute-start(f32[288,128]{1,0:T(8,128)S(1)} %get-tuple-element.286.p_ref), channel_id=1, source_target_pairs={{0,2},{1,3},{2,0},{3,1},{4,6},{5,7},{6,4},{7,5},{8,10},{9,11},{10,... | collective-permute-start | bytes 442376 | tf_op jit(solution)/shard_map/ppermute | solution.py:194
  14.7 2.0 %collective-permute-start.1 = (f32[288,256]{1,0:T(8,128)S(1)}, f32[288,256]{1,0:T(8,128)S(1)}, u32[]{:S(2)}, u32[]{:S(2)}) collective-permute-start(f32[288,256]{1,0:T(8,128)S(1)} %slice.30.p_ref), channel_id=1, source_target_pairs={{0,2},{1,3},{2,0},{3,1},{4,6},{5,7},{6,4},{7,5},{8,10},{9,11},{10,... | collective-permute-start | bytes 884744 | tf_op jit(solution)/shard_map/ppermute | solution.py:194
  18.0 4.1 %collective-permute-start.7 = (f32[256,128]{1,0:T(8,128)S(1)}, f32[256,128]{1,0:T(8,128)S(1)}, u32[]{:S(2)}, u32[]{:S(2)}) collective-permute-start(f32[256,128]{1,0:T(8,128)S(1)} %scale.4.mine_ref), channel_id=1, source_target_pairs={{0,1},{1,0},{2,3},{3,2},{4,5},{5,4},{6,7},{7,6},{8,9},{9,8},{10,11... | collective-permute-start | bytes 393224 | tf_op jit(solution)/shard_map/ppermute | solution.py:194
  22.5 2.8 %collective-permute-start.9 = (f32[256,128]{1,0:T(8,128)S(1)}, f32[256,128]{1,0:T(8,128)S(1)}, u32[]{:S(2)}, u32[]{:S(2)}) collective-permute-start(f32[256,128]{1,0:T(8,128)S(1)} %scale.5.mine_ref), channel_id=1, source_target_pairs={{0,1},{1,0},{2,3},{3,2},{4,5},{5,4},{6,7},{7,6},{8,9},{9,8},{10,11... | collective-permute-start | bytes 393224 | tf_op jit(solution)/shard_map/ppermute | solution.py:194
  25.3 1.3 %norm.4 = (bf16[2,2,512,128]{3,2,1,0:T(8,128)(2,1)S(1)}, bf16[4,2,2,32,128]{4,3,2,1,0:T(8,128)(2,1)S(1)}, bf16[4,2,2,32,128]{4,3,2,1,0:T(8,128)(2,1)S(1)}, bf16[...) custom-call(s32[4]{0:T(128)S(1)} %copy-done.3, ...), custom_call_target="tpu_custom_call" | custom-call | tf_op jit(solution)/shard_map/norm/pallas_call | solution.py:263
  26.6 1.6 %collective-permute-start.10 = (bf16[4,2,2,32,128]{4,3,2,1,0:T(8,128)(2,1)S(1)}, bf16[4,2,2,32,128]{4,3,2,1,0:T(8,128)(2,1)S(1)}, u32[]{:S(2)}, u32[]{:S(2)}) collective-permute-start(bf16[4,2,2,32,128]{4,3,2,1,0:T(8,128)(2,1)S(1)} %get-tuple-element.145.refs_2_), channel_id=1, source_target_pairs={{0,8},{8,16},{16,24},{24,28},{28,20},{20,12},{12,4},{4,0},{1,9},{9... | collective-permute-start | bytes 393224 | tf_op jit(solution)/shard_map/ppermute | solution.py:290
  28.3 1.6 %collective-permute-start.11 = (bf16[4,2,2,32,128]{4,3,2,1,0:T(8,128)(2,1)S(1)}, bf16[4,2,2,32,128]{4,3,2,1,0:T(8,128)(2,1)S(1)}, u32[]{:S(2)}, u32[]{:S(2)}) collective-permute-start(bf16[4,2,2,32,128]{4,3,2,1,0:T(8,128)(2,1)S(1)} %get-tuple-element.146.refs_3_), channel_id=1, source_target_pairs={{0,8},{8,16},{16,24},{24,28},{28,20},{20,12},{12,4},{4,0},{1,9},{9... | collective-permute-start | bytes 393224 | tf_op jit(solution)/shard_map/ppermute | solution.py:290
  30.8 1.3 %norm.5 = (bf16[2,2,512,128]{3,2,1,0:T(8,128)(2,1)S(1)}, bf16[4,2,2,32,128]{4,3,2,1,0:T(8,128)(2,1)S(1)}, bf16[4,2,2,32,128]{4,3,2,1,0:T(8,128)(2,1)S(1)}, bf16[...) custom-call(s32[4]{0:T(128)S(1)} %copy-done.3, ...), custom_call_target="tpu_custom_call" | custom-call | tf_op jit(solution)/shard_map/norm/pallas_call | solution.py:263
  33.1 1.6 %collective-permute-start.12 = (bf16[4,2,2,32,128]{4,3,2,1,0:T(8,128)(2,1)S(1)}, bf16[4,2,2,32,128]{4,3,2,1,0:T(8,128)(2,1)S(1)}, u32[]{:S(2)}, u32[]{:S(2)}) collective-permute-start(bf16[4,2,2,32,128]{4,3,2,1,0:T(8,128)(2,1)S(1)} %broadcast_select_fusion.33), channel_id=1, source_target_pairs={{0,8},{8,16},{16,24},{24,28},{28,20},{20,12},{12,4},{4,0},{1,9},{9... | collective-permute-start | bytes 393224 | tf_op jit(solution)/shard_map/ppermute | solution.py:290
  35.0 1.6 %collective-permute-start.13 = (bf16[4,2,2,32,128]{4,3,2,1,0:T(8,128)(2,1)S(1)}, bf16[4,2,2,32,128]{4,3,2,1,0:T(8,128)(2,1)S(1)}, u32[]{:S(2)}, u32[]{:S(2)}) collective-permute-start(bf16[4,2,2,32,128]{4,3,2,1,0:T(8,128)(2,1)S(1)} %broadcast_select_fusion.32), channel_id=1, source_target_pairs={{0,8},{8,16},{16,24},{24,28},{28,20},{20,12},{12,4},{4,0},{1,9},{9... | collective-permute-start | bytes 393224 | tf_op jit(solution)/shard_map/ppermute | solution.py:290
  37.6 1.2 collective-permute-start.38
  39.5 2.3 %collective-permute-done.13.refs_37_ = bf16[4,2,2,32,128]{4,3,2,1,0:T(8,128)(2,1)S(1)} collective-permute-done((bf16[4,2,2,32,128]{4,3,2,1,0:T(8,128)(2,1)S(1)}, bf16[4,2,2,32,128]{4,3,2,1,0:T(8,128)(2,1)S(1)}, u32[]{:S(2)}, u32[]{:S(2)}) %collective-permute-start.13) | collective-permute-done | bytes 131104 | tf_op jit(solution)/shard_map/ppermute | solution.py:290
  41.8 1.2 collective-permute-done.37.refs_56_.refs_61_
  43.1 1.5 %collective-permute-done.38.refs_57_.refs_62_ = bf16[4,2,2,32,128]{4,3,2,1,0:T(8,128)(2,1)S(1)} collective-permute-done((bf16[4,2,2,32,128]{4,3,2,1,0:T(8,128)(2,1)S(1)}, bf16[4,2,2,32,128]{4,3,2,1,0:T(8,128)(2,1)S(1)}, u32[]{:S(2)}, u32[]{:S(2)}) %collective-permute-start.38) | collective-permute-done | bytes 131104 | tf_op jit(solution)/shard_map/ppermute | solution.py:290
  44.6 1.6 %collective-permute-start.14 = (bf16[4,2,2,32,128]{4,3,2,1,0:T(8,128)(2,1)S(1)}, bf16[4,2,2,32,128]{4,3,2,1,0:T(8,128)(2,1)S(1)}, u32[]{:S(2)}, u32[]{:S(2)}) collective-permute-start(bf16[4,2,2,32,128]{4,3,2,1,0:T(8,128)(2,1)S(1)} %broadcast_select_fusion.31), channel_id=1, source_target_pairs={{0,8},{8,16},{16,24},{24,28},{28,20},{20,12},{12,4},{4,0},{1,9},{9... | collective-permute-start | bytes 393224 | tf_op jit(solution)/shard_map/ppermute | solution.py:290
  47.1 1.3 %collective-permute-start.39 = (bf16[4,2,2,32,128]{4,3,2,1,0:T(8,128)(2,1)S(1)}, bf16[4,2,2,32,128]{4,3,2,1,0:T(8,128)(2,1)S(1)}, u32[]{:S(2)}, u32[]{:S(2)}) collective-permute-start(bf16[4,2,2,32,128]{4,3,2,1,0:T(8,128)(2,1)S(1)} %broadcast_select_fusion.14), channel_id=1, source_target_pairs={{0,4},{8,0},{16,8},{24,16},{28,24},{20,28},{12,20},{4,12},{1,5},{9... | collective-permute-start | bytes 393224 | tf_op jit(solution)/shard_map/ppermute | solution.py:290
  48.9 1.4 %norm.3 = (bf16[2,2,512,128]{3,2,1,0:T(8,128)(2,1)S(1)}, bf16[2,2,512,128]{3,2,1,0:T(8,128)(2,1)S(1)}, bf16[4,2,2,32,128]{4,3,2,1,0:T(8,128)(2,1)S(1)}, bf16[4,2...) custom-call(s32[4]{0:T(128)S(1)} %copy-done.3, ...), custom_call_target="tpu_custom_call" | custom-call | tf_op jit(solution)/shard_map/norm/pallas_call | solution.py:263
  50.4 1.6 %collective-permute-start.16 = (bf16[4,2,2,32,128]{4,3,2,1,0:T(8,128)(2,1)S(1)}, bf16[4,2,2,32,128]{4,3,2,1,0:T(8,128)(2,1)S(1)}, u32[]{:S(2)}, u32[]{:S(2)}) collective-permute-start(bf16[4,2,2,32,128]{4,3,2,1,0:T(8,128)(2,1)S(1)} %broadcast_select_fusion.29), channel_id=1, source_target_pairs={{0,8},{8,16},{16,24},{24,28},{28,20},{20,12},{12,4},{4,0},{1,9},{9... | collective-permute-start | bytes 393224 | tf_op jit(solution)/shard_map/ppermute | solution.py:290
  52.7 1.6 %collective-permute-start.17 = (bf16[4,2,2,32,128]{4,3,2,1,0:T(8,128)(2,1)S(1)}, bf16[4,2,2,32,128]{4,3,2,1,0:T(8,128)(2,1)S(1)}, u32[]{:S(2)}, u32[]{:S(2)}) collective-permute-start(bf16[4,2,2,32,128]{4,3,2,1,0:T(8,128)(2,1)S(1)} %broadcast_select_fusion.28), channel_id=1, source_target_pairs={{0,8},{8,16},{16,24},{24,28},{28,20},{20,12},{12,4},{4,0},{1,9},{9... | collective-permute-start | bytes 393224 | tf_op jit(solution)/shard_map/ppermute | solution.py:290
  55.9 1.8 %collective-permute-done.17.refs_41_ = bf16[4,2,2,32,128]{4,3,2,1,0:T(8,128)(2,1)S(1)} collective-permute-done((bf16[4,2,2,32,128]{4,3,2,1,0:T(8,128)(2,1)S(1)}, bf16[4,2,2,32,128]{4,3,2,1,0:T(8,128)(2,1)S(1)}, u32[]{:S(2)}, u32[]{:S(2)}) %collective-permute-start.17) | collective-permute-done | bytes 131104 | tf_op jit(solution)/shard_map/ppermute | solution.py:290
  57.7 1.7 %collective-permute-done.41.refs_60_.refs_65_ = bf16[4,2,2,32,128]{4,3,2,1,0:T(8,128)(2,1)S(1)} collective-permute-done((bf16[4,2,2,32,128]{4,3,2,1,0:T(8,128)(2,1)S(1)}, bf16[4,2,2,32,128]{4,3,2,1,0:T(8,128)(2,1)S(1)}, u32[]{:S(2)}, u32[]{:S(2)}) %collective-permute-start.41) | collective-permute-done | bytes 131104 | tf_op jit(solution)/shard_map/ppermute | solution.py:290
  59.4 1.4 %collective-permute-done.42.refs_61_.refs_66_ = bf16[4,2,2,32,128]{4,3,2,1,0:T(8,128)(2,1)S(1)} collective-permute-done((bf16[4,2,2,32,128]{4,3,2,1,0:T(8,128)(2,1)S(1)}, bf16[4,2,2,32,128]{4,3,2,1,0:T(8,128)(2,1)S(1)}, u32[]{:S(2)}, u32[]{:S(2)}) %collective-permute-start.42) | collective-permute-done | bytes 131104 | tf_op jit(solution)/shard_map/ppermute | solution.py:290
  61.6 1.7 %collective-permute-start.19 = (bf16[4,2,2,32,128]{4,3,2,1,0:T(8,128)(2,1)S(1)}, bf16[4,2,2,32,128]{4,3,2,1,0:T(8,128)(2,1)S(1)}, u32[]{:S(2)}, u32[]{:S(2)}) collective-permute-start(bf16[4,2,2,32,128]{4,3,2,1,0:T(8,128)(2,1)S(1)} %broadcast_select_fusion.26), channel_id=1, source_target_pairs={{0,8},{8,16},{16,24},{24,28},{28,20},{20,12},{12,4},{4,0},{1,9},{9... | collective-permute-start | bytes 393224 | tf_op jit(solution)/shard_map/ppermute | solution.py:290
  63.8 1.3 %collective-permute-start.44 = (bf16[4,2,2,32,128]{4,3,2,1,0:T(8,128)(2,1)S(1)}, bf16[4,2,2,32,128]{4,3,2,1,0:T(8,128)(2,1)S(1)}, u32[]{:S(2)}, u32[]{:S(2)}) collective-permute-start(bf16[4,2,2,32,128]{4,3,2,1,0:T(8,128)(2,1)S(1)} %broadcast_select_fusion.9), channel_id=1, source_target_pairs={{0,4},{8,0},{16,8},{24,16},{28,24},{20,28},{12,20},{4,12},{1,5},{9... | collective-permute-start | bytes 393224 | tf_op jit(solution)/shard_map/ppermute | solution.py:290
  65.1 2.1 %collective-permute-done.18.refs_42_ = bf16[4,2,2,32,128]{4,3,2,1,0:T(8,128)(2,1)S(1)} collective-permute-done((bf16[4,2,2,32,128]{4,3,2,1,0:T(8,128)(2,1)S(1)}, bf16[4,2,2,32,128]{4,3,2,1,0:T(8,128)(2,1)S(1)}, u32[]{:S(2)}, u32[]{:S(2)}) %collective-permute-start.18) | collective-permute-done | bytes 131104 | tf_op jit(solution)/shard_map/ppermute | solution.py:290
  68.1 2.0 %collective-permute-done.19.refs_43_ = bf16[4,2,2,32,128]{4,3,2,1,0:T(8,128)(2,1)S(1)} collective-permute-done((bf16[4,2,2,32,128]{4,3,2,1,0:T(8,128)(2,1)S(1)}, bf16[4,2,2,32,128]{4,3,2,1,0:T(8,128)(2,1)S(1)}, u32[]{:S(2)}, u32[]{:S(2)}) %collective-permute-start.19) | collective-permute-done | bytes 131104 | tf_op jit(solution)/shard_map/ppermute | solution.py:290
  70.9 1.3 %collective-permute-start.45 = (bf16[4,2,2,32,128]{4,3,2,1,0:T(8,128)(2,1)S(1)}, bf16[4,2,2,32,128]{4,3,2,1,0:T(8,128)(2,1)S(1)}, u32[]{:S(2)}, u32[]{:S(2)}) collective-permute-start(bf16[4,2,2,32,128]{4,3,2,1,0:T(8,128)(2,1)S(1)} %broadcast_select_fusion.8), channel_id=1, source_target_pairs={{0,4},{8,0},{16,8},{24,16},{28,24},{20,28},{12,20},{4,12},{1,5},{9... | collective-permute-start | bytes 393224 | tf_op jit(solution)/shard_map/ppermute | solution.py:290
  74.4 1.9 %collective-permute-done.21.refs_45_ = bf16[4,2,2,32,128]{4,3,2,1,0:T(8,128)(2,1)S(1)} collective-permute-done((bf16[4,2,2,32,128]{4,3,2,1,0:T(8,128)(2,1)S(1)}, bf16[4,2,2,32,128]{4,3,2,1,0:T(8,128)(2,1)S(1)}, u32[]{:S(2)}, u32[]{:S(2)}) %collective-permute-start.21) | collective-permute-done | bytes 131104 | tf_op jit(solution)/shard_map/ppermute | solution.py:290
  77.2 1.3 %collective-permute-start.47 = (bf16[4,2,2,32,128]{4,3,2,1,0:T(8,128)(2,1)S(1)}, bf16[4,2,2,32,128]{4,3,2,1,0:T(8,128)(2,1)S(1)}, u32[]{:S(2)}, u32[]{:S(2)}) collective-permute-start(bf16[4,2,2,32,128]{4,3,2,1,0:T(8,128)(2,1)S(1)} %broadcast_select_fusion.6), channel_id=1, source_target_pairs={{0,4},{8,0},{16,8},{24,16},{28,24},{20,28},{12,20},{4,12},{1,5},{9... | collective-permute-start | bytes 393224 | tf_op jit(solution)/shard_map/ppermute | solution.py:290
  79.3 1.5 %collective-permute-start.24 = (bf16[4,2,2,32,128]{4,3,2,1,0:T(8,128)(2,1)S(1)}, bf16[4,2,2,32,128]{4,3,2,1,0:T(8,128)(2,1)S(1)}, u32[]{:S(2)}, u32[]{:S(2)}) collective-permute-start(bf16[4,2,2,32,128]{4,3,2,1,0:T(8,128)(2,1)S(1)} %broadcast_select_fusion.21), channel_id=1, source_target_pairs={{0,8},{8,16},{16,24},{24,28},{28,20},{20,12},{12,4},{4,0},{1,9},{9... | collective-permute-start | bytes 393224 | tf_op jit(solution)/shard_map/ppermute | solution.py:290
  80.9 1.8 %collective-permute-done.23.refs_47_ = bf16[4,2,2,32,128]{4,3,2,1,0:T(8,128)(2,1)S(1)} collective-permute-done((bf16[4,2,2,32,128]{4,3,2,1,0:T(8,128)(2,1)S(1)}, bf16[4,2,2,32,128]{4,3,2,1,0:T(8,128)(2,1)S(1)}, u32[]{:S(2)}, u32[]{:S(2)}) %collective-permute-start.23) | collective-permute-done | bytes 131104 | tf_op jit(solution)/shard_map/ppermute | solution.py:290
  83.7 1.2 %collective-permute-start.49 = (bf16[4,2,2,32,128]{4,3,2,1,0:T(8,128)(2,1)S(1)}, bf16[4,2,2,32,128]{4,3,2,1,0:T(8,128)(2,1)S(1)}, u32[]{:S(2)}, u32[]{:S(2)}) collective-permute-start(bf16[4,2,2,32,128]{4,3,2,1,0:T(8,128)(2,1)S(1)} %broadcast_select_fusion.4), channel_id=1, source_target_pairs={{0,4},{8,0},{16,8},{24,16},{28,24},{20,28},{12,20},{4,12},{1,5},{9... | collective-permute-start | bytes 393224 | tf_op jit(solution)/shard_map/ppermute | solution.py:290
  85.4 1.1 collective-permute-start.50
  86.5 1.5 %collective-permute-start.26 = (bf16[4,2,2,32,128]{4,3,2,1,0:T(8,128)(2,1)S(1)}, bf16[4,2,2,32,128]{4,3,2,1,0:T(8,128)(2,1)S(1)}, u32[]{:S(2)}, u32[]{:S(2)}) collective-permute-start(bf16[4,2,2,32,128]{4,3,2,1,0:T(8,128)(2,1)S(1)} %broadcast_select_fusion.19), channel_id=1, source_target_pairs={{0,8},{8,16},{16,24},{24,28},{28,20},{20,12},{12,4},{4,0},{1,9},{9... | collective-permute-start | bytes 393224 | tf_op jit(solution)/shard_map/ppermute | solution.py:290
  88.0 2.0 %collective-permute-start.27 = (bf16[4,2,2,32,128]{4,3,2,1,0:T(8,128)(2,1)S(1)}, bf16[4,2,2,32,128]{4,3,2,1,0:T(8,128)(2,1)S(1)}, u32[]{:S(2)}, u32[]{:S(2)}) collective-permute-start(bf16[4,2,2,32,128]{4,3,2,1,0:T(8,128)(2,1)S(1)} %broadcast_select_fusion.18), channel_id=1, source_target_pairs={{0,8},{8,16},{16,24},{24,28},{28,20},{20,12},{12,4},{4,0},{1,9},{9... | collective-permute-start | bytes 393224 | tf_op jit(solution)/shard_map/ppermute | solution.py:290
  90.9 1.8 %collective-permute-done.50.refs_69_.refs_74_ = bf16[4,2,2,32,128]{4,3,2,1,0:T(8,128)(2,1)S(1)} collective-permute-done((bf16[4,2,2,32,128]{4,3,2,1,0:T(8,128)(2,1)S(1)}, bf16[4,2,2,32,128]{4,3,2,1,0:T(8,128)(2,1)S(1)}, u32[]{:S(2)}, u32[]{:S(2)}) %collective-permute-start.50) | collective-permute-done | bytes 131104 | tf_op jit(solution)/shard_map/ppermute | solution.py:290
  93.8 1.1 collective-permute-start.28
  94.9 1.2 collective-permute-done.51.refs_70_.refs_75_
  96.1 1.3 %collective-permute-start.53 = (bf16[4,2,2,32,128]{4,3,2,1,0:T(8,128)(2,1)S(1)}, bf16[4,2,2,32,128]{4,3,2,1,0:T(8,128)(2,1)S(1)}, u32[]{:S(2)}, u32[]{:S(2)}) collective-permute-start(bf16[4,2,2,32,128]{4,3,2,1,0:T(8,128)(2,1)S(1)} %broadcast_select_fusion), channel_id=1, source_target_pairs={{0,4},{8,0},{16,8},{24,16},{28,24},{20,28},{12,20},{4,12},{1,5},{9... | collective-permute-start | bytes 393224 | tf_op jit(solution)/shard_map/ppermute | solution.py:290
  100.1 1.1 collective-permute-start.30
  103.0 1.1 collective-permute-start.31
  104.1 1.4 %collective-permute-done.54.refs_73_.refs_78_ = bf16[4,2,2,32,128]{4,3,2,1,0:T(8,128)(2,1)S(1)} collective-permute-done((bf16[4,2,2,32,128]{4,3,2,1,0:T(8,128)(2,1)S(1)}, bf16[4,2,2,32,128]{4,3,2,1,0:T(8,128)(2,1)S(1)}, u32[]{:S(2)}, u32[]{:S(2)}) %collective-permute-start.54) | collective-permute-done | bytes 131104 | tf_op jit(solution)/shard_map/ppermute | solution.py:290
  113.5 3.8 %early.1.refs_84_ = f32[4,2,2,512,256]{4,3,2,1,0:T(8,128)S(1)} custom-call(s32[4]{0:T(128)S(1)} %copy-done.2, bf16[2,2,512,128]{3,2,1,0:T(8,128)(2,1)S(1)} %get-tuple-element.279.refs_0_, bf16[2,2,512,128]{3,2,1,0:T(8,128)(2,1)S(1)} %get-tuple-element.280.refs_1_, bf16[4,2,2,32,128]{4,3,2,1,0:T(8,128)(2,1)S(1)} %get-tuple-element.145.refs_2_, ...), custom_call_target="tpu_custom_call" | custom-call | tf_op jit(solution)/shard_map/early/pallas_call | solution.py:306
  117.4 5.1 %cross.1 = bf16[4,2,2,512,256]{4,3,2,1,0:T(8,128)(2,1)} custom-call(s32[4]{0:T(128)S(1)} %copy-done.2, bf16[2,2,512,128]{3,2,1,0:T(8,128)(2,1)S(1)} %get-tuple-element.143.refs_0_, bf16[2,2,512,128]{3,2,1,0:T(8,128)(2,1)S(1)} %get-tuple-element.144.refs_1_, bf16[4,2,2,32,128]{4,3,2,1,0:T(8,128)(2,1)S(1)} %get-tuple-element.145.refs_2_, ...), custom_call_target="tpu_custom_call" | custom-call | tf_op jit(solution)/shard_map/cross/pallas_call | solution.py:307
  (200 shorter events, 36.0 us)
Async XLA Ops:
  4.7 6.5 %collective-permute-start = (f32[288,512]{1,0:T(8,128)}, f32[288,512]{1,0:T(8,128)}, u32[]{:S(2)}, u32[]{:S(2)}) collective-permute-start(f32[288,512]{1,0:T(8,128)} %slice_select_fusion), channel_id=1, source_target_pairs={{0,1},{1,0},{2,3},{3,2},{4,5},{5,4},{6,7},{7,6},{8,9},{9,8},{10,11... | collective-permute-start | bytes 1769480 | tf_op jit(solution)/shard_map/ppermute | solution.py:194
  10.5 6.1 %collective-permute-start.4 = (f32[32,512]{1,0:T(8,128)S(1)}, f32[32,512]{1,0:T(8,128)S(1)}, u32[]{:S(2)}, u32[]{:S(2)}) collective-permute-start(f32[32,512]{1,0:T(8,128)S(1)} %add.23), channel_id=1, source_target_pairs={{1,4},{3,6},{4,1},{5,8},{6,3},{7,10},{8,5},{9,12},{10,7},{11,14},{... | collective-permute-start | bytes 196616 | tf_op jit(solution)/shard_map/ppermute | solution.py:203
  14.6 7.6 %collective-permute-start.8 = (f32[288,128]{1,0:T(8,128)S(1)}, f32[288,128]{1,0:T(8,128)S(1)}, u32[]{:S(2)}, u32[]{:S(2)}) collective-permute-start(f32[288,128]{1,0:T(8,128)S(1)} %get-tuple-element.285.p_ref), channel_id=1, source_target_pairs={{0,2},{1,3},{2,0},{3,1},{4,6},{5,7},{6,4},{7,5},{8,10},{9,11},{10,... | collective-permute-start | bytes 442376 | tf_op jit(solution)/shard_map/ppermute | solution.py:194
  14.7 17.4 %collective-permute-start.1 = (f32[288,256]{1,0:T(8,128)S(1)}, f32[288,256]{1,0:T(8,128)S(1)}, u32[]{:S(2)}, u32[]{:S(2)}) collective-permute-start(f32[288,256]{1,0:T(8,128)S(1)} %slice.30.p_ref), channel_id=1, source_target_pairs={{0,2},{1,3},{2,0},{3,1},{4,6},{5,7},{6,4},{7,5},{8,10},{9,11},{10,... | collective-permute-start | bytes 884744 | tf_op jit(solution)/shard_map/ppermute | solution.py:194
  18.0 7.3 %collective-permute-start.7 = (f32[256,128]{1,0:T(8,128)S(1)}, f32[256,128]{1,0:T(8,128)S(1)}, u32[]{:S(2)}, u32[]{:S(2)}) collective-permute-start(f32[256,128]{1,0:T(8,128)S(1)} %scale.4.mine_ref), channel_id=1, source_target_pairs={{0,1},{1,0},{2,3},{3,2},{4,5},{5,4},{6,7},{7,6},{8,9},{9,8},{10,11... | collective-permute-start | bytes 393224 | tf_op jit(solution)/shard_map/ppermute | solution.py:194
  22.5 7.8 %collective-permute-start.9 = (f32[256,128]{1,0:T(8,128)S(1)}, f32[256,128]{1,0:T(8,128)S(1)}, u32[]{:S(2)}, u32[]{:S(2)}) collective-permute-start(f32[256,128]{1,0:T(8,128)S(1)} %scale.5.mine_ref), channel_id=1, source_target_pairs={{0,1},{1,0},{2,3},{3,2},{4,5},{5,4},{6,7},{7,6},{8,9},{9,8},{10,11... | collective-permute-start | bytes 393224 | tf_op jit(solution)/shard_map/ppermute | solution.py:194
  26.6 6.4 %collective-permute-start.10 = (bf16[4,2,2,32,128]{4,3,2,1,0:T(8,128)(2,1)S(1)}, bf16[4,2,2,32,128]{4,3,2,1,0:T(8,128)(2,1)S(1)}, u32[]{:S(2)}, u32[]{:S(2)}) collective-permute-start(bf16[4,2,2,32,128]{4,3,2,1,0:T(8,128)(2,1)S(1)} %get-tuple-element.145.refs_2_), channel_id=1, source_target_pairs={{0,8},{8,16},{16,24},{24,28},{28,20},{20,12},{12,4},{4,0},{1,9},{9... | collective-permute-start | bytes 393224 | tf_op jit(solution)/shard_map/ppermute | solution.py:290
  28.3 6.7 %collective-permute-start.11 = (bf16[4,2,2,32,128]{4,3,2,1,0:T(8,128)(2,1)S(1)}, bf16[4,2,2,32,128]{4,3,2,1,0:T(8,128)(2,1)S(1)}, u32[]{:S(2)}, u32[]{:S(2)}) collective-permute-start(bf16[4,2,2,32,128]{4,3,2,1,0:T(8,128)(2,1)S(1)} %get-tuple-element.146.refs_3_), channel_id=1, source_target_pairs={{0,8},{8,16},{16,24},{24,28},{28,20},{20,12},{12,4},{4,0},{1,9},{9... | collective-permute-start | bytes 393224 | tf_op jit(solution)/shard_map/ppermute | solution.py:290
  29.9 6.7 %collective-permute-start.35 = (bf16[4,2,2,32,128]{4,3,2,1,0:T(8,128)(2,1)S(1)}, bf16[4,2,2,32,128]{4,3,2,1,0:T(8,128)(2,1)S(1)}, u32[]{:S(2)}, u32[]{:S(2)}) collective-permute-start(bf16[4,2,2,32,128]{4,3,2,1,0:T(8,128)(2,1)S(1)} %get-tuple-element.161.refs_18_), channel_id=1, source_target_pairs={{0,4},{8,0},{16,8},{24,16},{28,24},{20,28},{12,20},{4,12},{1,5},{9... | collective-permute-start | bytes 393224 | tf_op jit(solution)/shard_map/ppermute | solution.py:290
  30.3 7.2 %collective-permute-start.36 = (bf16[4,2,2,32,128]{4,3,2,1,0:T(8,128)(2,1)S(1)}, bf16[4,2,2,32,128]{4,3,2,1,0:T(8,128)(2,1)S(1)}, u32[]{:S(2)}, u32[]{:S(2)}) collective-permute-start(bf16[4,2,2,32,128]{4,3,2,1,0:T(8,128)(2,1)S(1)} %get-tuple-element.162.refs_19_), channel_id=1, source_target_pairs={{0,4},{8,0},{16,8},{24,16},{28,24},{20,28},{12,20},{4,12},{1,5},{9... | collective-permute-start | bytes 393224 | tf_op jit(solution)/shard_map/ppermute | solution.py:290
  33.0 16.0 %collective-permute-start.5 = (f32[256,256]{1,0:T(8,128)S(1)}, f32[256,256]{1,0:T(8,128)S(1)}, u32[]{:S(2)}, u32[]{:S(2)}) collective-permute-start(f32[256,256]{1,0:T(8,128)S(1)} %scale.3.mine_ref), channel_id=1, source_target_pairs={{0,1},{1,0},{2,3},{3,2},{4,5},{5,4},{6,7},{7,6},{8,9},{9,8},{10,11... | collective-permute-start | bytes 786440 | tf_op jit(solution)/shard_map/ppermute | solution.py:194
  33.1 6.4 %collective-permute-start.12 = (bf16[4,2,2,32,128]{4,3,2,1,0:T(8,128)(2,1)S(1)}, bf16[4,2,2,32,128]{4,3,2,1,0:T(8,128)(2,1)S(1)}, u32[]{:S(2)}, u32[]{:S(2)}) collective-permute-start(bf16[4,2,2,32,128]{4,3,2,1,0:T(8,128)(2,1)S(1)} %broadcast_select_fusion.33), channel_id=1, source_target_pairs={{0,8},{8,16},{16,24},{24,28},{28,20},{20,12},{12,4},{4,0},{1,9},{9... | collective-permute-start | bytes 393224 | tf_op jit(solution)/shard_map/ppermute | solution.py:290
  35.0 6.9 %collective-permute-start.13 = (bf16[4,2,2,32,128]{4,3,2,1,0:T(8,128)(2,1)S(1)}, bf16[4,2,2,32,128]{4,3,2,1,0:T(8,128)(2,1)S(1)}, u32[]{:S(2)}, u32[]{:S(2)}) collective-permute-start(bf16[4,2,2,32,128]{4,3,2,1,0:T(8,128)(2,1)S(1)} %broadcast_select_fusion.32), channel_id=1, source_target_pairs={{0,8},{8,16},{16,24},{24,28},{28,20},{20,12},{12,4},{4,0},{1,9},{9... | collective-permute-start | bytes 393224 | tf_op jit(solution)/shard_map/ppermute | solution.py:290
  36.6 6.4 %collective-permute-start.37 = (bf16[4,2,2,32,128]{4,3,2,1,0:T(8,128)(2,1)S(1)}, bf16[4,2,2,32,128]{4,3,2,1,0:T(8,128)(2,1)S(1)}, u32[]{:S(2)}, u32[]{:S(2)}) collective-permute-start(bf16[4,2,2,32,128]{4,3,2,1,0:T(8,128)(2,1)S(1)} %broadcast_select_fusion.16), channel_id=1, source_target_pairs={{0,4},{8,0},{16,8},{24,16},{28,24},{20,28},{12,20},{4,12},{1,5},{9... | collective-permute-start | bytes 393224 | tf_op jit(solution)/shard_map/ppermute | solution.py:290
  37.6 7.0 %collective-permute-start.38 = (bf16[4,2,2,32,128]{4,3,2,1,0:T(8,128)(2,1)S(1)}, bf16[4,2,2,32,128]{4,3,2,1,0:T(8,128)(2,1)S(1)}, u32[]{:S(2)}, u32[]{:S(2)}) collective-permute-start(bf16[4,2,2,32,128]{4,3,2,1,0:T(8,128)(2,1)S(1)} %broadcast_select_fusion.15), channel_id=1, source_target_pairs={{0,4},{8,0},{16,8},{24,16},{28,24},{20,28},{12,20},{4,12},{1,5},{9... | collective-permute-start | bytes 393224 | tf_op jit(solution)/shard_map/ppermute | solution.py:290
  44.6 5.8 %collective-permute-start.14 = (bf16[4,2,2,32,128]{4,3,2,1,0:T(8,128)(2,1)S(1)}, bf16[4,2,2,32,128]{4,3,2,1,0:T(8,128)(2,1)S(1)}, u32[]{:S(2)}, u32[]{:S(2)}) collective-permute-start(bf16[4,2,2,32,128]{4,3,2,1,0:T(8,128)(2,1)S(1)} %broadcast_select_fusion.31), channel_id=1, source_target_pairs={{0,8},{8,16},{16,24},{24,28},{28,20},{20,12},{12,4},{4,0},{1,9},{9... | collective-permute-start | bytes 393224 | tf_op jit(solution)/shard_map/ppermute | solution.py:290
  46.3 6.4 %collective-permute-start.15 = (bf16[4,2,2,32,128]{4,3,2,1,0:T(8,128)(2,1)S(1)}, bf16[4,2,2,32,128]{4,3,2,1,0:T(8,128)(2,1)S(1)}, u32[]{:S(2)}, u32[]{:S(2)}) collective-permute-start(bf16[4,2,2,32,128]{4,3,2,1,0:T(8,128)(2,1)S(1)} %broadcast_select_fusion.30), channel_id=1, source_target_pairs={{0,8},{8,16},{16,24},{24,28},{28,20},{20,12},{12,4},{4,0},{1,9},{9... | collective-permute-start | bytes 393224 | tf_op jit(solution)/shard_map/ppermute | solution.py:290
  47.1 7.2 %collective-permute-start.39 = (bf16[4,2,2,32,128]{4,3,2,1,0:T(8,128)(2,1)S(1)}, bf16[4,2,2,32,128]{4,3,2,1,0:T(8,128)(2,1)S(1)}, u32[]{:S(2)}, u32[]{:S(2)}) collective-permute-start(bf16[4,2,2,32,128]{4,3,2,1,0:T(8,128)(2,1)S(1)} %broadcast_select_fusion.14), channel_id=1, source_target_pairs={{0,4},{8,0},{16,8},{24,16},{28,24},{20,28},{12,20},{4,12},{1,5},{9... | collective-permute-start | bytes 393224 | tf_op jit(solution)/shard_map/ppermute | solution.py:290
  48.4 6.4 %collective-permute-start.40 = (bf16[4,2,2,32,128]{4,3,2,1,0:T(8,128)(2,1)S(1)}, bf16[4,2,2,32,128]{4,3,2,1,0:T(8,128)(2,1)S(1)}, u32[]{:S(2)}, u32[]{:S(2)}) collective-permute-start(bf16[4,2,2,32,128]{4,3,2,1,0:T(8,128)(2,1)S(1)} %broadcast_select_fusion.13), channel_id=1, source_target_pairs={{0,4},{8,0},{16,8},{24,16},{28,24},{20,28},{12,20},{4,12},{1,5},{9... | collective-permute-start | bytes 393224 | tf_op jit(solution)/shard_map/ppermute | solution.py:290
  50.4 5.5 %collective-permute-start.16 = (bf16[4,2,2,32,128]{4,3,2,1,0:T(8,128)(2,1)S(1)}, bf16[4,2,2,32,128]{4,3,2,1,0:T(8,128)(2,1)S(1)}, u32[]{:S(2)}, u32[]{:S(2)}) collective-permute-start(bf16[4,2,2,32,128]{4,3,2,1,0:T(8,128)(2,1)S(1)} %broadcast_select_fusion.29), channel_id=1, source_target_pairs={{0,8},{8,16},{16,24},{24,28},{28,20},{20,12},{12,4},{4,0},{1,9},{9... | collective-permute-start | bytes 393224 | tf_op jit(solution)/shard_map/ppermute | solution.py:290
  54.9 5.9 %collective-permute-start.42 = (bf16[4,2,2,32,128]{4,3,2,1,0:T(8,128)(2,1)S(1)}, bf16[4,2,2,32,128]{4,3,2,1,0:T(8,128)(2,1)S(1)}, u32[]{:S(2)}, u32[]{:S(2)}) collective-permute-start(bf16[4,2,2,32,128]{4,3,2,1,0:T(8,128)(2,1)S(1)} %broadcast_select_fusion.11), channel_id=1, source_target_pairs={{0,4},{8,0},{16,8},{24,16},{28,24},{20,28},{12,20},{4,12},{1,5},{9... | collective-permute-start | bytes 393224 | tf_op jit(solution)/shard_map/ppermute | solution.py:290
  60.8 6.4 %collective-permute-start.18 = (bf16[4,2,2,32,128]{4,3,2,1,0:T(8,128)(2,1)S(1)}, bf16[4,2,2,32,128]{4,3,2,1,0:T(8,128)(2,1)S(1)}, u32[]{:S(2)}, u32[]{:S(2)}) collective-permute-start(bf16[4,2,2,32,128]{4,3,2,1,0:T(8,128)(2,1)S(1)} %broadcast_select_fusion.27), channel_id=1, source_target_pairs={{0,8},{8,16},{16,24},{24,28},{28,20},{20,12},{12,4},{4,0},{1,9},{9... | collective-permute-start | bytes 393224 | tf_op jit(solution)/shard_map/ppermute | solution.py:290
  61.6 8.4 %collective-permute-start.19 = (bf16[4,2,2,32,128]{4,3,2,1,0:T(8,128)(2,1)S(1)}, bf16[4,2,2,32,128]{4,3,2,1,0:T(8,128)(2,1)S(1)}, u32[]{:S(2)}, u32[]{:S(2)}) collective-permute-start(bf16[4,2,2,32,128]{4,3,2,1,0:T(8,128)(2,1)S(1)} %broadcast_select_fusion.26), channel_id=1, source_target_pairs={{0,8},{8,16},{16,24},{24,28},{28,20},{20,12},{12,4},{4,0},{1,9},{9... | collective-permute-start | bytes 393224 | tf_op jit(solution)/shard_map/ppermute | solution.py:290
  63.4 7.5 %collective-permute-start.43 = (bf16[4,2,2,32,128]{4,3,2,1,0:T(8,128)(2,1)S(1)}, bf16[4,2,2,32,128]{4,3,2,1,0:T(8,128)(2,1)S(1)}, u32[]{:S(2)}, u32[]{:S(2)}) collective-permute-start(bf16[4,2,2,32,128]{4,3,2,1,0:T(8,128)(2,1)S(1)} %broadcast_select_fusion.10), channel_id=1, source_target_pairs={{0,4},{8,0},{16,8},{24,16},{28,24},{20,28},{12,20},{4,12},{1,5},{9... | collective-permute-start | bytes 393224 | tf_op jit(solution)/shard_map/ppermute | solution.py:290
  63.8 8.4 %collective-permute-start.44 = (bf16[4,2,2,32,128]{4,3,2,1,0:T(8,128)(2,1)S(1)}, bf16[4,2,2,32,128]{4,3,2,1,0:T(8,128)(2,1)S(1)}, u32[]{:S(2)}, u32[]{:S(2)}) collective-permute-start(bf16[4,2,2,32,128]{4,3,2,1,0:T(8,128)(2,1)S(1)} %broadcast_select_fusion.9), channel_id=1, source_target_pairs={{0,4},{8,0},{16,8},{24,16},{28,24},{20,28},{12,20},{4,12},{1,5},{9... | collective-permute-start | bytes 393224 | tf_op jit(solution)/shard_map/ppermute | solution.py:290
  67.3 6.2 %collective-permute-start.20 = (bf16[4,2,2,32,128]{4,3,2,1,0:T(8,128)(2,1)S(1)}, bf16[4,2,2,32,128]{4,3,2,1,0:T(8,128)(2,1)S(1)}, u32[]{:S(2)}, u32[]{:S(2)}) collective-permute-start(bf16[4,2,2,32,128]{4,3,2,1,0:T(8,128)(2,1)S(1)} %broadcast_select_fusion.25), channel_id=1, source_target_pairs={{0,8},{8,16},{16,24},{24,28},{28,20},{20,12},{12,4},{4,0},{1,9},{9... | collective-permute-start | bytes 393224 | tf_op jit(solution)/shard_map/ppermute | solution.py:290
  70.1 6.2 %collective-permute-start.21 = (bf16[4,2,2,32,128]{4,3,2,1,0:T(8,128)(2,1)S(1)}, bf16[4,2,2,32,128]{4,3,2,1,0:T(8,128)(2,1)S(1)}, u32[]{:S(2)}, u32[]{:S(2)}) collective-permute-start(bf16[4,2,2,32,128]{4,3,2,1,0:T(8,128)(2,1)S(1)} %broadcast_select_fusion.24), channel_id=1, source_target_pairs={{0,8},{8,16},{16,24},{24,28},{28,20},{20,12},{12,4},{4,0},{1,9},{9... | collective-permute-start | bytes 393224 | tf_op jit(solution)/shard_map/ppermute | solution.py:290
  70.9 6.3 %collective-permute-start.45 = (bf16[4,2,2,32,128]{4,3,2,1,0:T(8,128)(2,1)S(1)}, bf16[4,2,2,32,128]{4,3,2,1,0:T(8,128)(2,1)S(1)}, u32[]{:S(2)}, u32[]{:S(2)}) collective-permute-start(bf16[4,2,2,32,128]{4,3,2,1,0:T(8,128)(2,1)S(1)} %broadcast_select_fusion.8), channel_id=1, source_target_pairs={{0,4},{8,0},{16,8},{24,16},{28,24},{20,28},{12,20},{4,12},{1,5},{9... | collective-permute-start | bytes 393224 | tf_op jit(solution)/shard_map/ppermute | solution.py:290
  72.3 6.2 %collective-permute-start.46 = (bf16[4,2,2,32,128]{4,3,2,1,0:T(8,128)(2,1)S(1)}, bf16[4,2,2,32,128]{4,3,2,1,0:T(8,128)(2,1)S(1)}, u32[]{:S(2)}, u32[]{:S(2)}) collective-permute-start(bf16[4,2,2,32,128]{4,3,2,1,0:T(8,128)(2,1)S(1)} %broadcast_select_fusion.7), channel_id=1, source_target_pairs={{0,4},{8,0},{16,8},{24,16},{28,24},{20,28},{12,20},{4,12},{1,5},{9... | collective-permute-start | bytes 393224 | tf_op jit(solution)/shard_map/ppermute | solution.py:290
  73.5 5.9 %collective-permute-start.22 = (bf16[4,2,2,32,128]{4,3,2,1,0:T(8,128)(2,1)S(1)}, bf16[4,2,2,32,128]{4,3,2,1,0:T(8,128)(2,1)S(1)}, u32[]{:S(2)}, u32[]{:S(2)}) collective-permute-start(bf16[4,2,2,32,128]{4,3,2,1,0:T(8,128)(2,1)S(1)} %broadcast_select_fusion.23), channel_id=1, source_target_pairs={{0,8},{8,16},{16,24},{24,28},{28,20},{20,12},{12,4},{4,0},{1,9},{9... | collective-permute-start | bytes 393224 | tf_op jit(solution)/shard_map/ppermute | solution.py:290
  76.3 6.4 %collective-permute-start.23 = (bf16[4,2,2,32,128]{4,3,2,1,0:T(8,128)(2,1)S(1)}, bf16[4,2,2,32,128]{4,3,2,1,0:T(8,128)(2,1)S(1)}, u32[]{:S(2)}, u32[]{:S(2)}) collective-permute-start(bf16[4,2,2,32,128]{4,3,2,1,0:T(8,128)(2,1)S(1)} %broadcast_select_fusion.22), channel_id=1, source_target_pairs={{0,8},{8,16},{16,24},{24,28},{28,20},{20,12},{12,4},{4,0},{1,9},{9... | collective-permute-start | bytes 393224 | tf_op jit(solution)/shard_map/ppermute | solution.py:290
  77.2 6.4 %collective-permute-start.47 = (bf16[4,2,2,32,128]{4,3,2,1,0:T(8,128)(2,1)S(1)}, bf16[4,2,2,32,128]{4,3,2,1,0:T(8,128)(2,1)S(1)}, u32[]{:S(2)}, u32[]{:S(2)}) collective-permute-start(bf16[4,2,2,32,128]{4,3,2,1,0:T(8,128)(2,1)S(1)} %broadcast_select_fusion.6), channel_id=1, source_target_pairs={{0,4},{8,0},{16,8},{24,16},{28,24},{20,28},{12,20},{4,12},{1,5},{9... | collective-permute-start | bytes 393224 | tf_op jit(solution)/shard_map/ppermute | solution.py:290
  78.5 6.8 %collective-permute-start.48 = (bf16[4,2,2,32,128]{4,3,2,1,0:T(8,128)(2,1)S(1)}, bf16[4,2,2,32,128]{4,3,2,1,0:T(8,128)(2,1)S(1)}, u32[]{:S(2)}, u32[]{:S(2)}) collective-permute-start(bf16[4,2,2,32,128]{4,3,2,1,0:T(8,128)(2,1)S(1)} %broadcast_select_fusion.5), channel_id=1, source_target_pairs={{0,4},{8,0},{16,8},{24,16},{28,24},{20,28},{12,20},{4,12},{1,5},{9... | collective-permute-start | bytes 393224 | tf_op jit(solution)/shard_map/ppermute | solution.py:290
  79.3 7.2 %collective-permute-start.24 = (bf16[4,2,2,32,128]{4,3,2,1,0:T(8,128)(2,1)S(1)}, bf16[4,2,2,32,128]{4,3,2,1,0:T(8,128)(2,1)S(1)}, u32[]{:S(2)}, u32[]{:S(2)}) collective-permute-start(bf16[4,2,2,32,128]{4,3,2,1,0:T(8,128)(2,1)S(1)} %broadcast_select_fusion.21), channel_id=1, source_target_pairs={{0,8},{8,16},{16,24},{24,28},{28,20},{20,12},{12,4},{4,0},{1,9},{9... | collective-permute-start | bytes 393224 | tf_op jit(solution)/shard_map/ppermute | solution.py:290
  83.7 6.4 %collective-permute-start.49 = (bf16[4,2,2,32,128]{4,3,2,1,0:T(8,128)(2,1)S(1)}, bf16[4,2,2,32,128]{4,3,2,1,0:T(8,128)(2,1)S(1)}, u32[]{:S(2)}, u32[]{:S(2)}) collective-permute-start(bf16[4,2,2,32,128]{4,3,2,1,0:T(8,128)(2,1)S(1)} %broadcast_select_fusion.4), channel_id=1, source_target_pairs={{0,4},{8,0},{16,8},{24,16},{28,24},{20,28},{12,20},{4,12},{1,5},{9... | collective-permute-start | bytes 393224 | tf_op jit(solution)/shard_map/ppermute | solution.py:290
  85.4 7.3 %collective-permute-start.50 = (bf16[4,2,2,32,128]{4,3,2,1,0:T(8,128)(2,1)S(1)}, bf16[4,2,2,32,128]{4,3,2,1,0:T(8,128)(2,1)S(1)}, u32[]{:S(2)}, u32[]{:S(2)}) collective-permute-start(bf16[4,2,2,32,128]{4,3,2,1,0:T(8,128)(2,1)S(1)} %broadcast_select_fusion.3), channel_id=1, source_target_pairs={{0,4},{8,0},{16,8},{24,16},{28,24},{20,28},{12,20},{4,12},{1,5},{9... | collective-permute-start | bytes 393224 | tf_op jit(solution)/shard_map/ppermute | solution.py:290
  86.5 7.2 %collective-permute-start.26 = (bf16[4,2,2,32,128]{4,3,2,1,0:T(8,128)(2,1)S(1)}, bf16[4,2,2,32,128]{4,3,2,1,0:T(8,128)(2,1)S(1)}, u32[]{:S(2)}, u32[]{:S(2)}) collective-permute-start(bf16[4,2,2,32,128]{4,3,2,1,0:T(8,128)(2,1)S(1)} %broadcast_select_fusion.19), channel_id=1, source_target_pairs={{0,8},{8,16},{16,24},{24,28},{28,20},{20,12},{12,4},{4,0},{1,9},{9... | collective-permute-start | bytes 393224 | tf_op jit(solution)/shard_map/ppermute | solution.py:290
  88.0 9.3 %collective-permute-start.27 = (bf16[4,2,2,32,128]{4,3,2,1,0:T(8,128)(2,1)S(1)}, bf16[4,2,2,32,128]{4,3,2,1,0:T(8,128)(2,1)S(1)}, u32[]{:S(2)}, u32[]{:S(2)}) collective-permute-start(bf16[4,2,2,32,128]{4,3,2,1,0:T(8,128)(2,1)S(1)} %broadcast_select_fusion.18), channel_id=1, source_target_pairs={{0,8},{8,16},{16,24},{24,28},{28,20},{20,12},{12,4},{4,0},{1,9},{9... | collective-permute-start | bytes 393224 | tf_op jit(solution)/shard_map/ppermute | solution.py:290
  90.1 6.0 %collective-permute-start.51 = (bf16[4,2,2,32,128]{4,3,2,1,0:T(8,128)(2,1)S(1)}, bf16[4,2,2,32,128]{4,3,2,1,0:T(8,128)(2,1)S(1)}, u32[]{:S(2)}, u32[]{:S(2)}) collective-permute-start(bf16[4,2,2,32,128]{4,3,2,1,0:T(8,128)(2,1)S(1)} %broadcast_select_fusion.2), channel_id=1, source_target_pairs={{0,4},{8,0},{16,8},{24,16},{28,24},{20,28},{12,20},{4,12},{1,5},{9... | collective-permute-start | bytes 393224 | tf_op jit(solution)/shard_map/ppermute | solution.py:290
  92.7 6.4 %collective-permute-start.52 = (bf16[4,2,2,32,128]{4,3,2,1,0:T(8,128)(2,1)S(1)}, bf16[4,2,2,32,128]{4,3,2,1,0:T(8,128)(2,1)S(1)}, u32[]{:S(2)}, u32[]{:S(2)}) collective-permute-start(bf16[4,2,2,32,128]{4,3,2,1,0:T(8,128)(2,1)S(1)} %broadcast_select_fusion.1), channel_id=1, source_target_pairs={{0,4},{8,0},{16,8},{24,16},{28,24},{20,28},{12,20},{4,12},{1,5},{9... | collective-permute-start | bytes 393224 | tf_op jit(solution)/shard_map/ppermute | solution.py:290
  93.8 6.3 %collective-permute-start.28 = (bf16[4,2,2,32,128]{4,3,2,1,0:T(8,128)(2,1)S(1)}, bf16[4,2,2,32,128]{4,3,2,1,0:T(8,128)(2,1)S(1)}, u32[]{:S(2)}, u32[]{:S(2)}) collective-permute-start(bf16[4,2,2,32,128]{4,3,2,1,0:T(8,128)(2,1)S(1)} %broadcast_select_fusion.17), channel_id=1, source_target_pairs={{0,8},{8,16},{16,24},{24,28},{28,20},{20,12},{12,4},{4,0},{1,9},{9... | collective-permute-start | bytes 393224 | tf_op jit(solution)/shard_map/ppermute | solution.py:290
  96.1 5.9 %collective-permute-start.53 = (bf16[4,2,2,32,128]{4,3,2,1,0:T(8,128)(2,1)S(1)}, bf16[4,2,2,32,128]{4,3,2,1,0:T(8,128)(2,1)S(1)}, u32[]{:S(2)}, u32[]{:S(2)}) collective-permute-start(bf16[4,2,2,32,128]{4,3,2,1,0:T(8,128)(2,1)S(1)} %broadcast_select_fusion), channel_id=1, source_target_pairs={{0,4},{8,0},{16,8},{24,16},{28,24},{20,28},{12,20},{4,12},{1,5},{9... | collective-permute-start | bytes 393224 | tf_op jit(solution)/shard_map/ppermute | solution.py:290
  97.4 5.6 %collective-permute-start.29 = (bf16[4,2,2,32,128]{4,3,2,1,0:T(8,128)(2,1)S(1)}, bf16[4,2,2,32,128]{4,3,2,1,0:T(8,128)(2,1)S(1)}, u32[]{:S(2)}, u32[]{:S(2)}) collective-permute-start(bf16[4,2,2,32,128]{4,3,2,1,0:T(8,128)(2,1)S(1)} %collective-permute-done.27.refs_51_), channel_id=1, source_target_pairs={{0,8},{8,16},{16,24},{24,28},{28,20},{20,12},{12,4},{4,0},{1,9},{9... | collective-permute-start | bytes 393224 | tf_op jit(solution)/shard_map/ppermute | solution.py:290
  99.1 6.3 %collective-permute-start.54 = (bf16[4,2,2,32,128]{4,3,2,1,0:T(8,128)(2,1)S(1)}, bf16[4,2,2,32,128]{4,3,2,1,0:T(8,128)(2,1)S(1)}, u32[]{:S(2)}, u32[]{:S(2)}) collective-permute-start(bf16[4,2,2,32,128]{4,3,2,1,0:T(8,128)(2,1)S(1)} %collective-permute-done.52.refs_71_.refs_76_), channel_id=1, source_target_pairs={{0,4},{8,0},{16,8},{24,16},{28,24},{20,28},{12,20},{4,12},{1,5},{9... | collective-permute-start | bytes 393224 | tf_op jit(solution)/shard_map/ppermute | solution.py:290
  100.1 6.4 %collective-permute-start.30 = (bf16[4,2,2,32,128]{4,3,2,1,0:T(8,128)(2,1)S(1)}, bf16[4,2,2,32,128]{4,3,2,1,0:T(8,128)(2,1)S(1)}, u32[]{:S(2)}, u32[]{:S(2)}) collective-permute-start(bf16[4,2,2,32,128]{4,3,2,1,0:T(8,128)(2,1)S(1)} %collective-permute-done.28.refs_52_), channel_id=1, source_target_pairs={{0,8},{8,16},{16,24},{24,28},{28,20},{20,12},{12,4},{4,0},{1,9},{9... | collective-permute-start | bytes 393224 | tf_op jit(solution)/shard_map/ppermute | solution.py:290
  108.5 8.8 %collective-permute-start.33 = (bf16[4,2,2,32,128]{4,3,2,1,0:T(8,128)(2,1)S(1)}, bf16[4,2,2,32,128]{4,3,2,1,0:T(8,128)(2,1)S(1)}, u32[]{:S(2)}, u32[]{:S(2)}) collective-permute-start(bf16[4,2,2,32,128]{4,3,2,1,0:T(8,128)(2,1)S(1)} %collective-permute-done.31.refs_55_), channel_id=1, source_target_pairs={{0,8},{8,16},{16,24},{24,28},{28,20},{20,12},{12,4},{4,0},{1,9},{9... | collective-permute-start | bytes 393224 | tf_op jit(solution)/shard_map/ppermute | solution.py:290
  110.4 6.9 %collective-permute-start.58 = (bf16[4,2,2,32,128]{4,3,2,1,0:T(8,128)(2,1)S(1)}, bf16[4,2,2,32,128]{4,3,2,1,0:T(8,128)(2,1)S(1)}, u32[]{:S(2)}, u32[]{:S(2)}) collective-permute-start(bf16[4,2,2,32,128]{4,3,2,1,0:T(8,128)(2,1)S(1)} %collective-permute-done.56.refs_80_), channel_id=1, source_target_pairs={{0,4},{8,0},{16,8},{24,16},{28,24},{20,28},{12,20},{4,12},{1,5},{9... | collective-permute-start | bytes 393224 | tf_op jit(solution)/shard_map/ppermute | solution.py:290
  111.4 5.9 %collective-permute-start.34 = (bf16[4,2,2,32,128]{4,3,2,1,0:T(8,128)(2,1)S(1)}, bf16[4,2,2,32,128]{4,3,2,1,0:T(8,128)(2,1)S(1)}, u32[]{:S(2)}, u32[]{:S(2)}) collective-permute-start(bf16[4,2,2,32,128]{4,3,2,1,0:T(8,128)(2,1)S(1)} %collective-permute-done.32.refs_56_), channel_id=1, source_target_pairs={{0,8},{8,16},{16,24},{24,28},{28,20},{20,12},{12,4},{4,0},{1,9},{9... | collective-permute-start | bytes 393224 | tf_op jit(solution)/shard_map/ppermute | solution.py:290
  (16 other events, 125.0 us)

commit v4 on v3

--- a/solution.py
+++ b/solution.py
@@ -15,7 +15,7 @@
 LANES = 128
 LAG = 2
 SUBS = 4
-SPANS = (1, 1, 2)
+SPANS = (1, 1, 1, 1)
 
 
 def spans_of(groups):
@@ -77,18 +77,13 @@
     scale_ref[...] = lax.rsqrt(total / (count.astype(jnp.float32) * bins) + 1e-06)
 
 
-def norm_kernel(base, groups, subs, starts_ref, mine_ref, other_ref, x_ref, *rest):
+def norm_kernel(groups, subs, starts_ref, mine_ref, other_ref, x_ref, *rest):
     per = 2 * subs
     normed, own = rest[:groups], rest[groups : groups * (1 + per)]
-    x_buf, scale_buf, n_ref, in_sem, scale_sem = rest[groups * (1 + per) :]
-    _, f_dev, parts, rows, _ = x_buf.shape
+    scale_buf, n_ref, scale_sem = rest[groups * (1 + per) :]
+    f_dev, parts, rows, _ = x_ref.shape
     half_rows = rows // 2
     far = lax.rem(lax.axis_index("band"), 2)
-    reads = []
-    for g in range(groups):
-        lanes = pl.ds((base + g) * LANES, LANES)
-        reads.append(pltpu.make_async_copy(x_ref.at[:, :, :, lanes], x_buf.at[g], in_sem.at[g]))
-        reads[g].start()
     shares = []
     for i, ref in enumerate((mine_ref, other_ref)):
         at = far * half_rows if i == 0 else (1 - far) * half_rows
@@ -99,11 +94,11 @@
         copy.wait()
     size = HALF // subs
     for g in range(groups):
-        reads[g].wait()
-        scale = scale_buf[:, g * LANES : (g + 1) * LANES]
+        lanes = slice(g * LANES, (g + 1) * LANES)
+        scale = scale_buf[:, lanes]
         for f in range(f_dev):
             for k in range(parts):
-                value = (x_buf[g, f, k].astype(jnp.float32) * scale).astype(jnp.bfloat16)
+                value = (x_ref[f, k, :, lanes].astype(jnp.float32) * scale).astype(jnp.bfloat16)
                 normed[g][f, k] = value
                 n_ref[f, k] = value.astype(jnp.float32)
         for p in range(NPANEL):
@@ -244,23 +239,22 @@
         )
         scale = scale(shares[i], theirs[i], halo, widths)
         norm = pl.pallas_call(
-            functools.partial(norm_kernel, base, n_groups, SUBS),
+            functools.partial(norm_kernel, n_groups, SUBS),
             out_shape=[pltpu.VMEM(block, jnp.bfloat16)] * n_groups
             + [pltpu.VMEM(piece, jnp.bfloat16)] * (n_groups * cuts),
-            in_specs=[pl.BlockSpec(memory_space=pltpu.SMEM)] + [hbm] * 3,
+            in_specs=[pl.BlockSpec(memory_space=pltpu.SMEM)] + [hbm] * 2 + [vmem],
             out_specs=[vmem] * (n_groups * (1 + cuts)),
             scratch_shapes=[
-                pltpu.VMEM((n_groups, *block), jnp.bfloat16),
                 pltpu.VMEM((ch_dev, span), jnp.float32),
                 pltpu.VMEM(block, jnp.float32),
-                pltpu.SemaphoreType.DMA((n_groups,)),
                 pltpu.SemaphoreType.DMA((2,)),
             ],
             compiler_params=pltpu.CompilerParams(vmem_limit_bytes=16 << 20),
             name="norm",
         )
+        cut = spectra[..., base * LANES : (base + n_groups) * LANES]
         other = flip(scale, 1)
-        outs = norm(panel_offset, scale, other, spectra)
+        outs = norm(panel_offset, scale, other, cut)
         normed += outs[:n_groups]
         outs = outs[n_groups:]
         for g in range(n_groups):

time: 123 us -> 123 us (level)
  waiting for transfers between devices: 31.7 us -> 26.4 us
  starting transfers between devices: 69.2 us -> 73.4 us
    ppermute x50, waiting for transfers between devices: 28.4 us -> 23.1 us  [local(): got[half].append(lax.ppermute(value, 'chan', pairs))]
    ppermute x9 -> x11, starting transfers between devices: 14.8 us -> 18.1 us  [flip(): return lax.ppermute(block, 'band', [(b, b ^ bit) for b in range(n_band)])]
    pallas_call x3 -> x4, Pallas kernels: 4.05 us -> 4.82 us  [local(): outs = norm(panel_offset, scale, other, cut)]
    ppermute x9 -> x11, waiting for transfers between devices: 3.32 us -> 3.32 us  [flip(): return lax.ppermute(block, 'band', [(b, b ^ bit) for b in range(n_band)])]
  transfers between devices with their start and end apart: 60 -> 62, of which waited for: 27 -> 25; matrix products, arithmetic and copies ran while one was open for 4% -> 5% of each run, Pallas kernels for 8% -> 8%
where the time goes in v4:
time: 123 us
  starting transfers between devices  73.4 us (60%)
  waiting for transfers between devices  26.4 us (21%)
  Pallas kernels  15.1 us (12%)
  other arithmetic  6.53 us (5%)
    ppermute x50, starting transfers between devices, local(): got[half].append(lax.ppermute(value, 'chan', pairs))  54.6 us
    ppermute x50, waiting for transfers between devices, local(): got[half].append(lax.ppermute(value, 'chan', pairs))  23.1 us
    ppermute x11, starting transfers between devices, flip(): return lax.ppermute(block, 'band', [(b, b ^ bit) for b in range(n_band)])  18.1 us
    pallas_call x1, Pallas kernels, local(): pl.pallas_call(functools.partial(cross_kernel, ahead, groups - ahead, n_c...  5.02 us
    pallas_call x4, Pallas kernels, local(): outs = norm(panel_offset, scale, other, cut)  4.82 us
    pallas_call x1, Pallas kernels, local(): early(panel_block, *normed[:ahead], *own[0], *own[1], *got[0][:n_ready],...  3.8 us
    reduce_sum x2, other arithmetic, power_of(): return jnp.sum(jnp.square(block.astype(jnp.float32)), axis=(0, 1))  3.33 us
    ppermute x11, waiting for transfers between devices, flip(): return lax.ppermute(block, 'band', [(b, b ^ bit) for b in range(n_band)])  3.32 us
  transfers between devices with their start and end apart: 62, of which 25 were waited for; matrix products, arithmetic and copies ran while one was open for 5% of the time, Pallas kernels for 8%

profile of v4, /device:TPU:0, one launch (start us, length us, event | category | flops | bytes accessed | tf_op | source)
XLA Modules:
  0.0 122.6 jit_solution(9932013406233403900)
XLA Ops:
  1.8 2.2 %multiply_reduce_fusion = f32[512,512]{1,0:T(8,128)S(1)} fusion(bf16[2,2,512,512]{3,2,1,0:T(8,128)(2,1)} %param.4), kind=kLoop, calls=%fused_computation | loop fusion | flops 2883584 | bytes 3145728 | tf_op jit(solution)/shard_map/reduce_sum | solution.py:201
  5.8 3.1 %collective-permute-start.3 = (f32[32,512]{1,0:T(8,128)S(1)}, f32[32,512]{1,0:T(8,128)S(1)}, u32[]{:S(2)}, u32[]{:S(2)}) collective-permute-start(f32[32,512]{1,0:T(8,128)S(1)} %select_add_fusion.1), channel_id=1, source_target_pairs={{0,2},{1,3},{2,0},{3,1},{4,6},{5,7},{6,4},{7,5},{8,10},{9,11},{10,... | collective-permute-start | bytes 196616 | tf_op jit(solution)/shard_map/ppermute | solution.py:189
  8.9 2.3 %collective-permute-done.3 = f32[32,512]{1,0:T(8,128)S(1)} collective-permute-done((f32[32,512]{1,0:T(8,128)S(1)}, f32[32,512]{1,0:T(8,128)S(1)}, u32[]{:S(2)}, u32[]{:S(2)}) %collective-permute-start.3) | collective-permute-done | bytes 65568 | tf_op jit(solution)/shard_map/ppermute | solution.py:189
  11.8 1.2 %select_add_fusion = f32[288,512]{1,0:T(8,128)S(1)} fusion(f32[288,512]{1,0:T(8,128)} %collective-permute-done, f32[512,512]{1,0:T(8,128)S(1)} %multiply_reduce_fusion, pred[]{:T(512)S(6)} %eq.11), kind=kLoop, calls=%fused_computation.1 | loop fusion | flops 294912 | bytes 2359297 | tf_op jit(solution)/shard_map/add | solution.py:207
  13.1 2.1 %collective-permute-start.8 = (f32[288,128]{1,0:T(8,128)S(1)}, f32[288,128]{1,0:T(8,128)S(1)}, u32[]{:S(2)}, u32[]{:S(2)}) collective-permute-start(f32[288,128]{1,0:T(8,128)S(1)} %get-tuple-element.290.p_ref), channel_id=1, source_target_pairs={{0,2},{1,3},{2,0},{3,1},{4,6},{5,7},{6,4},{7,5},{8,10},{9,11},{10,... | collective-permute-start | bytes 442376 | tf_op jit(solution)/shard_map/ppermute | solution.py:189
  15.3 1.9 %collective-permute-start.6 = (f32[288,128]{1,0:T(8,128)S(1)}, f32[288,128]{1,0:T(8,128)S(1)}, u32[]{:S(2)}, u32[]{:S(2)}) collective-permute-start(f32[288,128]{1,0:T(8,128)S(1)} %get-tuple-element.291.p_ref), channel_id=1, source_target_pairs={{0,2},{1,3},{2,0},{3,1},{4,6},{5,7},{6,4},{7,5},{8,10},{9,11},{10,... | collective-permute-start | bytes 442376 | tf_op jit(solution)/shard_map/ppermute | solution.py:189
  18.7 4.1 %collective-permute-start.9 = (f32[256,128]{1,0:T(8,128)S(1)}, f32[256,128]{1,0:T(8,128)S(1)}, u32[]{:S(2)}, u32[]{:S(2)}) collective-permute-start(f32[256,128]{1,0:T(8,128)S(1)} %scale.6.mine_ref), channel_id=1, source_target_pairs={{0,1},{1,0},{2,3},{3,2},{4,5},{5,4},{6,7},{7,6},{8,9},{9,8},{10,11... | collective-permute-start | bytes 393224 | tf_op jit(solution)/shard_map/ppermute | solution.py:189
  23.2 2.8 %collective-permute-start.11 = (f32[256,128]{1,0:T(8,128)S(1)}, f32[256,128]{1,0:T(8,128)S(1)}, u32[]{:S(2)}, u32[]{:S(2)}) collective-permute-start(f32[256,128]{1,0:T(8,128)S(1)} %scale.7.mine_ref), channel_id=1, source_target_pairs={{0,1},{1,0},{2,3},{3,2},{4,5},{5,4},{6,7},{7,6},{8,9},{9,8},{10,11... | collective-permute-start | bytes 393224 | tf_op jit(solution)/shard_map/ppermute | solution.py:189
  26.3 2.1 %collective-permute-start.7 = (f32[256,128]{1,0:T(8,128)S(1)}, f32[256,128]{1,0:T(8,128)S(1)}, u32[]{:S(2)}, u32[]{:S(2)}) collective-permute-start(f32[256,128]{1,0:T(8,128)S(1)} %scale.5.mine_ref), channel_id=1, source_target_pairs={{0,1},{1,0},{2,3},{3,2},{4,5},{5,4},{6,7},{7,6},{8,9},{9,8},{10,11... | collective-permute-start | bytes 393224 | tf_op jit(solution)/shard_map/ppermute | solution.py:189
  28.9 1.2 collective-permute-start.5
  30.1 1.2 norm.6
  31.3 2.9 %collective-permute-start.12 = (bf16[4,2,2,32,128]{4,3,2,1,0:T(8,128)(2,1)S(1)}, bf16[4,2,2,32,128]{4,3,2,1,0:T(8,128)(2,1)S(1)}, u32[]{:S(2)}, u32[]{:S(2)}) collective-permute-start(bf16[4,2,2,32,128]{4,3,2,1,0:T(8,128)(2,1)S(1)} %get-tuple-element.145.refs_2_), channel_id=1, source_target_pairs={{0,8},{8,16},{16,24},{24,28},{28,20},{20,12},{12,4},{4,0},{1,9},{9... | collective-permute-start | bytes 393224 | tf_op jit(solution)/shard_map/ppermute | solution.py:284
  34.2 1.6 %collective-permute-start.13 = (bf16[4,2,2,32,128]{4,3,2,1,0:T(8,128)(2,1)S(1)}, bf16[4,2,2,32,128]{4,3,2,1,0:T(8,128)(2,1)S(1)}, u32[]{:S(2)}, u32[]{:S(2)}) collective-permute-start(bf16[4,2,2,32,128]{4,3,2,1,0:T(8,128)(2,1)S(1)} %get-tuple-element.146.refs_3_), channel_id=1, source_target_pairs={{0,8},{8,16},{16,24},{24,28},{28,20},{20,12},{12,4},{4,0},{1,9},{9... | collective-permute-start | bytes 393224 | tf_op jit(solution)/shard_map/ppermute | solution.py:284
  37.5 1.2 norm.4
  38.8 1.2 norm.5
  40.0 2.1 %collective-permute-start.14 = (bf16[4,2,2,32,128]{4,3,2,1,0:T(8,128)(2,1)S(1)}, bf16[4,2,2,32,128]{4,3,2,1,0:T(8,128)(2,1)S(1)}, u32[]{:S(2)}, u32[]{:S(2)}) collective-permute-start(bf16[4,2,2,32,128]{4,3,2,1,0:T(8,128)(2,1)S(1)} %broadcast_select_fusion.33), channel_id=1, source_target_pairs={{0,8},{8,16},{16,24},{24,28},{28,20},{20,12},{12,4},{4,0},{1,9},{9... | collective-permute-start | bytes 393224 | tf_op jit(solution)/shard_map/ppermute | solution.py:284
  42.1 1.6 %collective-permute-start.15 = (bf16[4,2,2,32,128]{4,3,2,1,0:T(8,128)(2,1)S(1)}, bf16[4,2,2,32,128]{4,3,2,1,0:T(8,128)(2,1)S(1)}, u32[]{:S(2)}, u32[]{:S(2)}) collective-permute-start(bf16[4,2,2,32,128]{4,3,2,1,0:T(8,128)(2,1)S(1)} %broadcast_select_fusion.32), channel_id=1, source_target_pairs={{0,8},{8,16},{16,24},{24,28},{28,20},{20,12},{12,4},{4,0},{1,9},{9... | collective-permute-start | bytes 393224 | tf_op jit(solution)/shard_map/ppermute | solution.py:284
  44.7 1.7 %collective-permute-done.14.refs_36_ = bf16[4,2,2,32,128]{4,3,2,1,0:T(8,128)(2,1)S(1)} collective-permute-done((bf16[4,2,2,32,128]{4,3,2,1,0:T(8,128)(2,1)S(1)}, bf16[4,2,2,32,128]{4,3,2,1,0:T(8,128)(2,1)S(1)}, u32[]{:S(2)}, u32[]{:S(2)}) %collective-permute-start.14) | collective-permute-done | bytes 131104 | tf_op jit(solution)/shard_map/ppermute | solution.py:284
  46.4 1.5 %collective-permute-start.16 = (bf16[4,2,2,32,128]{4,3,2,1,0:T(8,128)(2,1)S(1)}, bf16[4,2,2,32,128]{4,3,2,1,0:T(8,128)(2,1)S(1)}, u32[]{:S(2)}, u32[]{:S(2)}) collective-permute-start(bf16[4,2,2,32,128]{4,3,2,1,0:T(8,128)(2,1)S(1)} %broadcast_select_fusion.31), channel_id=1, source_target_pairs={{0,8},{8,16},{16,24},{24,28},{28,20},{20,12},{12,4},{4,0},{1,9},{9... | collective-permute-start | bytes 393224 | tf_op jit(solution)/shard_map/ppermute | solution.py:284
  47.9 1.3 %collective-permute-done.15.refs_37_ = bf16[4,2,2,32,128]{4,3,2,1,0:T(8,128)(2,1)S(1)} collective-permute-done((bf16[4,2,2,32,128]{4,3,2,1,0:T(8,128)(2,1)S(1)}, bf16[4,2,2,32,128]{4,3,2,1,0:T(8,128)(2,1)S(1)}, u32[]{:S(2)}, u32[]{:S(2)}) %collective-permute-start.15) | collective-permute-done | bytes 131104 | tf_op jit(solution)/shard_map/ppermute | solution.py:284
  49.2 1.5 %collective-permute-start.17 = (bf16[4,2,2,32,128]{4,3,2,1,0:T(8,128)(2,1)S(1)}, bf16[4,2,2,32,128]{4,3,2,1,0:T(8,128)(2,1)S(1)}, u32[]{:S(2)}, u32[]{:S(2)}) collective-permute-start(bf16[4,2,2,32,128]{4,3,2,1,0:T(8,128)(2,1)S(1)} %broadcast_select_fusion.30), channel_id=1, source_target_pairs={{0,8},{8,16},{16,24},{24,28},{28,20},{20,12},{12,4},{4,0},{1,9},{9... | collective-permute-start | bytes 393224 | tf_op jit(solution)/shard_map/ppermute | solution.py:284
  51.4 1.7 %collective-permute-start.42 = (bf16[4,2,2,32,128]{4,3,2,1,0:T(8,128)(2,1)S(1)}, bf16[4,2,2,32,128]{4,3,2,1,0:T(8,128)(2,1)S(1)}, u32[]{:S(2)}, u32[]{:S(2)}) collective-permute-start(bf16[4,2,2,32,128]{4,3,2,1,0:T(8,128)(2,1)S(1)} %broadcast_select_fusion.13), channel_id=1, source_target_pairs={{0,4},{8,0},{16,8},{24,16},{28,24},{20,28},{12,20},{4,12},{1,5},{9... | collective-permute-start | bytes 393224 | tf_op jit(solution)/shard_map/ppermute | solution.py:284
  53.6 2.1 %collective-permute-done.17.refs_39_ = bf16[4,2,2,32,128]{4,3,2,1,0:T(8,128)(2,1)S(1)} collective-permute-done((bf16[4,2,2,32,128]{4,3,2,1,0:T(8,128)(2,1)S(1)}, bf16[4,2,2,32,128]{4,3,2,1,0:T(8,128)(2,1)S(1)}, u32[]{:S(2)}, u32[]{:S(2)}) %collective-permute-start.17) | collective-permute-done | bytes 131104 | tf_op jit(solution)/shard_map/ppermute | solution.py:284
  55.7 1.5 %collective-permute-start.19 = (bf16[4,2,2,32,128]{4,3,2,1,0:T(8,128)(2,1)S(1)}, bf16[4,2,2,32,128]{4,3,2,1,0:T(8,128)(2,1)S(1)}, u32[]{:S(2)}, u32[]{:S(2)}) collective-permute-start(bf16[4,2,2,32,128]{4,3,2,1,0:T(8,128)(2,1)S(1)} %broadcast_select_fusion.28), channel_id=1, source_target_pairs={{0,8},{8,16},{16,24},{24,28},{28,20},{20,12},{12,4},{4,0},{1,9},{9... | collective-permute-start | bytes 393224 | tf_op jit(solution)/shard_map/ppermute | solution.py:284
  57.8 1.4 %collective-permute-done.42.refs_59_.refs_64_ = bf16[4,2,2,32,128]{4,3,2,1,0:T(8,128)(2,1)S(1)} collective-permute-done((bf16[4,2,2,32,128]{4,3,2,1,0:T(8,128)(2,1)S(1)}, bf16[4,2,2,32,128]{4,3,2,1,0:T(8,128)(2,1)S(1)}, u32[]{:S(2)}, u32[]{:S(2)}) %collective-permute-start.42) | collective-permute-done | bytes 131104 | tf_op jit(solution)/shard_map/ppermute | solution.py:284
  60.1 1.7 %collective-permute-start.20 = (bf16[4,2,2,32,128]{4,3,2,1,0:T(8,128)(2,1)S(1)}, bf16[4,2,2,32,128]{4,3,2,1,0:T(8,128)(2,1)S(1)}, u32[]{:S(2)}, u32[]{:S(2)}) collective-permute-start(bf16[4,2,2,32,128]{4,3,2,1,0:T(8,128)(2,1)S(1)} %broadcast_select_fusion.27), channel_id=1, source_target_pairs={{0,8},{8,16},{16,24},{24,28},{28,20},{20,12},{12,4},{4,0},{1,9},{9... | collective-permute-start | bytes 393224 | tf_op jit(solution)/shard_map/ppermute | solution.py:284
  62.1 1.8 %collective-permute-start.21 = (bf16[4,2,2,32,128]{4,3,2,1,0:T(8,128)(2,1)S(1)}, bf16[4,2,2,32,128]{4,3,2,1,0:T(8,128)(2,1)S(1)}, u32[]{:S(2)}, u32[]{:S(2)}) collective-permute-start(bf16[4,2,2,32,128]{4,3,2,1,0:T(8,128)(2,1)S(1)} %broadcast_select_fusion.26), channel_id=1, source_target_pairs={{0,8},{8,16},{16,24},{24,28},{28,20},{20,12},{12,4},{4,0},{1,9},{9... | collective-permute-start | bytes 393224 | tf_op jit(solution)/shard_map/ppermute | solution.py:284
  64.3 2.2 %collective-permute-done.44.refs_61_.refs_66_ = bf16[4,2,2,32,128]{4,3,2,1,0:T(8,128)(2,1)S(1)} collective-permute-done((bf16[4,2,2,32,128]{4,3,2,1,0:T(8,128)(2,1)S(1)}, bf16[4,2,2,32,128]{4,3,2,1,0:T(8,128)(2,1)S(1)}, u32[]{:S(2)}, u32[]{:S(2)}) %collective-permute-start.44) | collective-permute-done | bytes 131104 | tf_op jit(solution)/shard_map/ppermute | solution.py:284
  66.9 1.7 %collective-permute-start.22 = (bf16[4,2,2,32,128]{4,3,2,1,0:T(8,128)(2,1)S(1)}, bf16[4,2,2,32,128]{4,3,2,1,0:T(8,128)(2,1)S(1)}, u32[]{:S(2)}, u32[]{:S(2)}) collective-permute-start(bf16[4,2,2,32,128]{4,3,2,1,0:T(8,128)(2,1)S(1)} %broadcast_select_fusion.25), channel_id=1, source_target_pairs={{0,8},{8,16},{16,24},{24,28},{28,20},{20,12},{12,4},{4,0},{1,9},{9... | collective-permute-start | bytes 393224 | tf_op jit(solution)/shard_map/ppermute | solution.py:284
  68.8 1.7 %collective-permute-start.23 = (bf16[4,2,2,32,128]{4,3,2,1,0:T(8,128)(2,1)S(1)}, bf16[4,2,2,32,128]{4,3,2,1,0:T(8,128)(2,1)S(1)}, u32[]{:S(2)}, u32[]{:S(2)}) collective-permute-start(bf16[4,2,2,32,128]{4,3,2,1,0:T(8,128)(2,1)S(1)} %broadcast_select_fusion.24), channel_id=1, source_target_pairs={{0,8},{8,16},{16,24},{24,28},{28,20},{20,12},{12,4},{4,0},{1,9},{9... | collective-permute-start | bytes 393224 | tf_op jit(solution)/shard_map/ppermute | solution.py:284
  73.2 1.9 %collective-permute-start.24 = (bf16[4,2,2,32,128]{4,3,2,1,0:T(8,128)(2,1)S(1)}, bf16[4,2,2,32,128]{4,3,2,1,0:T(8,128)(2,1)S(1)}, u32[]{:S(2)}, u32[]{:S(2)}) collective-permute-start(bf16[4,2,2,32,128]{4,3,2,1,0:T(8,128)(2,1)S(1)} %broadcast_select_fusion.23), channel_id=1, source_target_pairs={{0,8},{8,16},{16,24},{24,28},{28,20},{20,12},{12,4},{4,0},{1,9},{9... | collective-permute-start | bytes 393224 | tf_op jit(solution)/shard_map/ppermute | solution.py:284
  75.7 1.8 %collective-permute-start.25 = (bf16[4,2,2,32,128]{4,3,2,1,0:T(8,128)(2,1)S(1)}, bf16[4,2,2,32,128]{4,3,2,1,0:T(8,128)(2,1)S(1)}, u32[]{:S(2)}, u32[]{:S(2)}) collective-permute-start(bf16[4,2,2,32,128]{4,3,2,1,0:T(8,128)(2,1)S(1)} %broadcast_select_fusion.22), channel_id=1, source_target_pairs={{0,8},{8,16},{16,24},{24,28},{28,20},{20,12},{12,4},{4,0},{1,9},{9... | collective-permute-start | bytes 393224 | tf_op jit(solution)/shard_map/ppermute | solution.py:284
  78.3 1.5 %collective-permute-start.50 = (bf16[4,2,2,32,128]{4,3,2,1,0:T(8,128)(2,1)S(1)}, bf16[4,2,2,32,128]{4,3,2,1,0:T(8,128)(2,1)S(1)}, u32[]{:S(2)}, u32[]{:S(2)}) collective-permute-start(bf16[4,2,2,32,128]{4,3,2,1,0:T(8,128)(2,1)S(1)} %broadcast_select_fusion.5), channel_id=1, source_target_pairs={{0,4},{8,0},{16,8},{24,16},{28,24},{20,28},{12,20},{4,12},{1,5},{9... | collective-permute-start | bytes 393224 | tf_op jit(solution)/shard_map/ppermute | solution.py:284
  82.2 1.7 %collective-permute-start.27 = (bf16[4,2,2,32,128]{4,3,2,1,0:T(8,128)(2,1)S(1)}, bf16[4,2,2,32,128]{4,3,2,1,0:T(8,128)(2,1)S(1)}, u32[]{:S(2)}, u32[]{:S(2)}) collective-permute-start(bf16[4,2,2,32,128]{4,3,2,1,0:T(8,128)(2,1)S(1)} %broadcast_select_fusion.20), channel_id=1, source_target_pairs={{0,8},{8,16},{16,24},{24,28},{28,20},{20,12},{12,4},{4,0},{1,9},{9... | collective-permute-start | bytes 393224 | tf_op jit(solution)/shard_map/ppermute | solution.py:284
  84.9 1.4 %collective-permute-start.52 = (bf16[4,2,2,32,128]{4,3,2,1,0:T(8,128)(2,1)S(1)}, bf16[4,2,2,32,128]{4,3,2,1,0:T(8,128)(2,1)S(1)}, u32[]{:S(2)}, u32[]{:S(2)}) collective-permute-start(bf16[4,2,2,32,128]{4,3,2,1,0:T(8,128)(2,1)S(1)} %broadcast_select_fusion.3), channel_id=1, source_target_pairs={{0,4},{8,0},{16,8},{24,16},{28,24},{20,28},{12,20},{4,12},{1,5},{9... | collective-permute-start | bytes 393224 | tf_op jit(solution)/shard_map/ppermute | solution.py:284
  87.9 1.7 %collective-permute-start.29 = (bf16[4,2,2,32,128]{4,3,2,1,0:T(8,128)(2,1)S(1)}, bf16[4,2,2,32,128]{4,3,2,1,0:T(8,128)(2,1)S(1)}, u32[]{:S(2)}, u32[]{:S(2)}) collective-permute-start(bf16[4,2,2,32,128]{4,3,2,1,0:T(8,128)(2,1)S(1)} %broadcast_select_fusion.18), channel_id=1, source_target_pairs={{0,8},{8,16},{16,24},{24,28},{28,20},{20,12},{12,4},{4,0},{1,9},{9... | collective-permute-start | bytes 393224 | tf_op jit(solution)/shard_map/ppermute | solution.py:284
  90.1 2.7 %collective-permute-done.52.refs_69_.refs_74_ = bf16[4,2,2,32,128]{4,3,2,1,0:T(8,128)(2,1)S(1)} collective-permute-done((bf16[4,2,2,32,128]{4,3,2,1,0:T(8,128)(2,1)S(1)}, bf16[4,2,2,32,128]{4,3,2,1,0:T(8,128)(2,1)S(1)}, u32[]{:S(2)}, u32[]{:S(2)}) %collective-permute-start.52) | collective-permute-done | bytes 131104 | tf_op jit(solution)/shard_map/ppermute | solution.py:284
  93.0 2.0 %collective-permute-start.30 = (bf16[4,2,2,32,128]{4,3,2,1,0:T(8,128)(2,1)S(1)}, bf16[4,2,2,32,128]{4,3,2,1,0:T(8,128)(2,1)S(1)}, u32[]{:S(2)}, u32[]{:S(2)}) collective-permute-start(bf16[4,2,2,32,128]{4,3,2,1,0:T(8,128)(2,1)S(1)} %broadcast_select_fusion.17), channel_id=1, source_target_pairs={{0,8},{8,16},{16,24},{24,28},{28,20},{20,12},{12,4},{4,0},{1,9},{9... | collective-permute-start | bytes 393224 | tf_op jit(solution)/shard_map/ppermute | solution.py:284
  95.0 1.5 %collective-permute-done.53.refs_70_.refs_75_ = bf16[4,2,2,32,128]{4,3,2,1,0:T(8,128)(2,1)S(1)} collective-permute-done((bf16[4,2,2,32,128]{4,3,2,1,0:T(8,128)(2,1)S(1)}, bf16[4,2,2,32,128]{4,3,2,1,0:T(8,128)(2,1)S(1)}, u32[]{:S(2)}, u32[]{:S(2)}) %collective-permute-start.53) | collective-permute-done | bytes 131104 | tf_op jit(solution)/shard_map/ppermute | solution.py:284
  96.6 2.0 %collective-permute-start.31 = (bf16[4,2,2,32,128]{4,3,2,1,0:T(8,128)(2,1)S(1)}, bf16[4,2,2,32,128]{4,3,2,1,0:T(8,128)(2,1)S(1)}, u32[]{:S(2)}, u32[]{:S(2)}) collective-permute-start(bf16[4,2,2,32,128]{4,3,2,1,0:T(8,128)(2,1)S(1)} %collective-permute-done.29.refs_51_), channel_id=1, source_target_pairs={{0,8},{8,16},{16,24},{24,28},{28,20},{20,12},{12,4},{4,0},{1,9},{9... | collective-permute-start | bytes 393224 | tf_op jit(solution)/shard_map/ppermute | solution.py:284
  99.3 2.0 %collective-permute-start.32 = (bf16[4,2,2,32,128]{4,3,2,1,0:T(8,128)(2,1)S(1)}, bf16[4,2,2,32,128]{4,3,2,1,0:T(8,128)(2,1)S(1)}, u32[]{:S(2)}, u32[]{:S(2)}) collective-permute-start(bf16[4,2,2,32,128]{4,3,2,1,0:T(8,128)(2,1)S(1)} %collective-permute-done.30.refs_52_), channel_id=1, source_target_pairs={{0,8},{8,16},{16,24},{24,28},{28,20},{20,12},{12,4},{4,0},{1,9},{9... | collective-permute-start | bytes 393224 | tf_op jit(solution)/shard_map/ppermute | solution.py:284
  102.2 2.0 %collective-permute-start.33 = (bf16[4,2,2,32,128]{4,3,2,1,0:T(8,128)(2,1)S(1)}, bf16[4,2,2,32,128]{4,3,2,1,0:T(8,128)(2,1)S(1)}, u32[]{:S(2)}, u32[]{:S(2)}) collective-permute-start(bf16[4,2,2,32,128]{4,3,2,1,0:T(8,128)(2,1)S(1)} %collective-permute-done.31.refs_53_), channel_id=1, source_target_pairs={{0,8},{8,16},{16,24},{24,28},{28,20},{20,12},{12,4},{4,0},{1,9},{9... | collective-permute-start | bytes 393224 | tf_op jit(solution)/shard_map/ppermute | solution.py:284
  104.2 1.4 %collective-permute-done.56.refs_73_.refs_78_ = bf16[4,2,2,32,128]{4,3,2,1,0:T(8,128)(2,1)S(1)} collective-permute-done((bf16[4,2,2,32,128]{4,3,2,1,0:T(8,128)(2,1)S(1)}, bf16[4,2,2,32,128]{4,3,2,1,0:T(8,128)(2,1)S(1)}, u32[]{:S(2)}, u32[]{:S(2)}) %collective-permute-start.56) | collective-permute-done | bytes 131104 | tf_op jit(solution)/shard_map/ppermute | solution.py:284
  105.6 2.0 %collective-permute-start.34 = (bf16[4,2,2,32,128]{4,3,2,1,0:T(8,128)(2,1)S(1)}, bf16[4,2,2,32,128]{4,3,2,1,0:T(8,128)(2,1)S(1)}, u32[]{:S(2)}, u32[]{:S(2)}) collective-permute-start(bf16[4,2,2,32,128]{4,3,2,1,0:T(8,128)(2,1)S(1)} %collective-permute-done.32.refs_54_), channel_id=1, source_target_pairs={{0,8},{8,16},{16,24},{24,28},{28,20},{20,12},{12,4},{4,0},{1,9},{9... | collective-permute-start | bytes 393224 | tf_op jit(solution)/shard_map/ppermute | solution.py:284
  107.8 1.9 %collective-permute-start.35 = (bf16[4,2,2,32,128]{4,3,2,1,0:T(8,128)(2,1)S(1)}, bf16[4,2,2,32,128]{4,3,2,1,0:T(8,128)(2,1)S(1)}, u32[]{:S(2)}, u32[]{:S(2)}) collective-permute-start(bf16[4,2,2,32,128]{4,3,2,1,0:T(8,128)(2,1)S(1)} %collective-permute-done.33.refs_55_), channel_id=1, source_target_pairs={{0,8},{8,16},{16,24},{24,28},{28,20},{20,12},{12,4},{4,0},{1,9},{9... | collective-permute-start | bytes 393224 | tf_op jit(solution)/shard_map/ppermute | solution.py:284
  110.7 1.9 %collective-permute-start.36 = (bf16[4,2,2,32,128]{4,3,2,1,0:T(8,128)(2,1)S(1)}, bf16[4,2,2,32,128]{4,3,2,1,0:T(8,128)(2,1)S(1)}, u32[]{:S(2)}, u32[]{:S(2)}) collective-permute-start(bf16[4,2,2,32,128]{4,3,2,1,0:T(8,128)(2,1)S(1)} %collective-permute-done.34.refs_56_), channel_id=1, source_target_pairs={{0,8},{8,16},{16,24},{24,28},{28,20},{20,12},{12,4},{4,0},{1,9},{9... | collective-permute-start | bytes 393224 | tf_op jit(solution)/shard_map/ppermute | solution.py:284
  113.0 3.8 %early.1.refs_84_ = f32[4,2,2,512,256]{4,3,2,1,0:T(8,128)S(1)} custom-call(s32[4]{0:T(128)S(1)} %copy-done.2, bf16[2,2,512,128]{3,2,1,0:T(8,128)(2,1)S(1)} %get-tuple-element.279.refs_0_, bf16[2,2,512,128]{3,2,1,0:T(8,128)(2,1)S(1)} %get-tuple-element.280.refs_1_, bf16[4,2,2,32,128]{4,3,2,1,0:T(8,128)(2,1)S(1)} %get-tuple-element.145.refs_2_, ...), custom_call_target="tpu_custom_call" | custom-call | tf_op jit(solution)/shard_map/early/pallas_call | solution.py:300
  117.6 5.0 %cross.1 = bf16[4,2,2,512,256]{4,3,2,1,0:T(8,128)(2,1)} custom-call(s32[4]{0:T(128)S(1)} %copy-done.2, bf16[2,2,512,128]{3,2,1,0:T(8,128)(2,1)S(1)} %get-tuple-element.143.refs_0_, bf16[2,2,512,128]{3,2,1,0:T(8,128)(2,1)S(1)} %get-tuple-element.144.refs_1_, bf16[4,2,2,32,128]{4,3,2,1,0:T(8,128)(2,1)S(1)} %get-tuple-element.145.refs_2_, ...), custom_call_target="tpu_custom_call" | custom-call | tf_op jit(solution)/shard_map/cross/pallas_call | solution.py:301
  (206 shorter events, 27.2 us)
Async XLA Ops:
  4.8 7.0 %collective-permute-start = (f32[288,512]{1,0:T(8,128)}, f32[288,512]{1,0:T(8,128)}, u32[]{:S(2)}, u32[]{:S(2)}) collective-permute-start(f32[288,512]{1,0:T(8,128)} %slice_select_fusion), channel_id=1, source_target_pairs={{0,1},{1,0},{2,3},{3,2},{4,5},{5,4},{6,7},{7,6},{8,9},{9,8},{10,11... | collective-permute-start | bytes 1769480 | tf_op jit(solution)/shard_map/ppermute | solution.py:189
  11.2 6.2 %collective-permute-start.4 = (f32[32,512]{1,0:T(8,128)S(1)}, f32[32,512]{1,0:T(8,128)S(1)}, u32[]{:S(2)}, u32[]{:S(2)}) collective-permute-start(f32[32,512]{1,0:T(8,128)S(1)} %add.23), channel_id=1, source_target_pairs={{1,4},{3,6},{4,1},{5,8},{6,3},{7,10},{8,5},{9,12},{10,7},{11,14},{... | collective-permute-start | bytes 196616 | tf_op jit(solution)/shard_map/ppermute | solution.py:198
  15.2 7.6 %collective-permute-start.10 = (f32[288,128]{1,0:T(8,128)S(1)}, f32[288,128]{1,0:T(8,128)S(1)}, u32[]{:S(2)}, u32[]{:S(2)}) collective-permute-start(f32[288,128]{1,0:T(8,128)S(1)} %get-tuple-element.289.p_ref), channel_id=1, source_target_pairs={{0,2},{1,3},{2,0},{3,1},{4,6},{5,7},{6,4},{7,5},{8,10},{9,11},{10,... | collective-permute-start | bytes 442376 | tf_op jit(solution)/shard_map/ppermute | solution.py:189
  15.3 10.7 %collective-permute-start.6 = (f32[288,128]{1,0:T(8,128)S(1)}, f32[288,128]{1,0:T(8,128)S(1)}, u32[]{:S(2)}, u32[]{:S(2)}) collective-permute-start(f32[288,128]{1,0:T(8,128)S(1)} %get-tuple-element.291.p_ref), channel_id=1, source_target_pairs={{0,2},{1,3},{2,0},{3,1},{4,6},{5,7},{6,4},{7,5},{8,10},{9,11},{10,... | collective-permute-start | bytes 442376 | tf_op jit(solution)/shard_map/ppermute | solution.py:189
  17.2 11.3 %collective-permute-start.1 = (f32[288,128]{1,0:T(8,128)S(1)}, f32[288,128]{1,0:T(8,128)S(1)}, u32[]{:S(2)}, u32[]{:S(2)}) collective-permute-start(f32[288,128]{1,0:T(8,128)S(1)} %get-tuple-element.292.p_ref), channel_id=1, source_target_pairs={{0,2},{1,3},{2,0},{3,1},{4,6},{5,7},{6,4},{7,5},{8,10},{9,11},{10,... | collective-permute-start | bytes 442376 | tf_op jit(solution)/shard_map/ppermute | solution.py:189
  18.7 11.4 %collective-permute-start.9 = (f32[256,128]{1,0:T(8,128)S(1)}, f32[256,128]{1,0:T(8,128)S(1)}, u32[]{:S(2)}, u32[]{:S(2)}) collective-permute-start(f32[256,128]{1,0:T(8,128)S(1)} %scale.6.mine_ref), channel_id=1, source_target_pairs={{0,1},{1,0},{2,3},{3,2},{4,5},{5,4},{6,7},{7,6},{8,9},{9,8},{10,11... | collective-permute-start | bytes 393224 | tf_op jit(solution)/shard_map/ppermute | solution.py:189
  23.2 12.6 %collective-permute-start.11 = (f32[256,128]{1,0:T(8,128)S(1)}, f32[256,128]{1,0:T(8,128)S(1)}, u32[]{:S(2)}, u32[]{:S(2)}) collective-permute-start(f32[256,128]{1,0:T(8,128)S(1)} %scale.7.mine_ref), channel_id=1, source_target_pairs={{0,1},{1,0},{2,3},{3,2},{4,5},{5,4},{6,7},{7,6},{8,9},{9,8},{10,11... | collective-permute-start | bytes 393224 | tf_op jit(solution)/shard_map/ppermute | solution.py:189
  26.3 12.4 %collective-permute-start.7 = (f32[256,128]{1,0:T(8,128)S(1)}, f32[256,128]{1,0:T(8,128)S(1)}, u32[]{:S(2)}, u32[]{:S(2)}) collective-permute-start(f32[256,128]{1,0:T(8,128)S(1)} %scale.5.mine_ref), channel_id=1, source_target_pairs={{0,1},{1,0},{2,3},{3,2},{4,5},{5,4},{6,7},{7,6},{8,9},{9,8},{10,11... | collective-permute-start | bytes 393224 | tf_op jit(solution)/shard_map/ppermute | solution.py:189
  28.9 8.6 %collective-permute-start.5 = (f32[256,128]{1,0:T(8,128)S(1)}, f32[256,128]{1,0:T(8,128)S(1)}, u32[]{:S(2)}, u32[]{:S(2)}) collective-permute-start(f32[256,128]{1,0:T(8,128)S(1)} %scale.4.mine_ref), channel_id=1, source_target_pairs={{0,1},{1,0},{2,3},{3,2},{4,5},{5,4},{6,7},{7,6},{8,9},{9,8},{10,11... | collective-permute-start | bytes 393224 | tf_op jit(solution)/shard_map/ppermute | solution.py:189
  31.3 8.7 %collective-permute-start.12 = (bf16[4,2,2,32,128]{4,3,2,1,0:T(8,128)(2,1)S(1)}, bf16[4,2,2,32,128]{4,3,2,1,0:T(8,128)(2,1)S(1)}, u32[]{:S(2)}, u32[]{:S(2)}) collective-permute-start(bf16[4,2,2,32,128]{4,3,2,1,0:T(8,128)(2,1)S(1)} %get-tuple-element.145.refs_2_), channel_id=1, source_target_pairs={{0,8},{8,16},{16,24},{24,28},{28,20},{20,12},{12,4},{4,0},{1,9},{9... | collective-permute-start | bytes 393224 | tf_op jit(solution)/shard_map/ppermute | solution.py:284
  34.2 7.9 %collective-permute-start.13 = (bf16[4,2,2,32,128]{4,3,2,1,0:T(8,128)(2,1)S(1)}, bf16[4,2,2,32,128]{4,3,2,1,0:T(8,128)(2,1)S(1)}, u32[]{:S(2)}, u32[]{:S(2)}) collective-permute-start(bf16[4,2,2,32,128]{4,3,2,1,0:T(8,128)(2,1)S(1)} %get-tuple-element.146.refs_3_), channel_id=1, source_target_pairs={{0,8},{8,16},{16,24},{24,28},{28,20},{20,12},{12,4},{4,0},{1,9},{9... | collective-permute-start | bytes 393224 | tf_op jit(solution)/shard_map/ppermute | solution.py:284
  35.8 8.0 %collective-permute-start.37 = (bf16[4,2,2,32,128]{4,3,2,1,0:T(8,128)(2,1)S(1)}, bf16[4,2,2,32,128]{4,3,2,1,0:T(8,128)(2,1)S(1)}, u32[]{:S(2)}, u32[]{:S(2)}) collective-permute-start(bf16[4,2,2,32,128]{4,3,2,1,0:T(8,128)(2,1)S(1)} %get-tuple-element.161.refs_18_), channel_id=1, source_target_pairs={{0,4},{8,0},{16,8},{24,16},{28,24},{20,28},{12,20},{4,12},{1,5},{9... | collective-permute-start | bytes 393224 | tf_op jit(solution)/shard_map/ppermute | solution.py:284
  37.5 6.8 %collective-permute-start.38 = (bf16[4,2,2,32,128]{4,3,2,1,0:T(8,128)(2,1)S(1)}, bf16[4,2,2,32,128]{4,3,2,1,0:T(8,128)(2,1)S(1)}, u32[]{:S(2)}, u32[]{:S(2)}) collective-permute-start(bf16[4,2,2,32,128]{4,3,2,1,0:T(8,128)(2,1)S(1)} %get-tuple-element.162.refs_19_), channel_id=1, source_target_pairs={{0,4},{8,0},{16,8},{24,16},{28,24},{20,28},{12,20},{4,12},{1,5},{9... | collective-permute-start | bytes 393224 | tf_op jit(solution)/shard_map/ppermute | solution.py:284
  40.0 6.4 %collective-permute-start.14 = (bf16[4,2,2,32,128]{4,3,2,1,0:T(8,128)(2,1)S(1)}, bf16[4,2,2,32,128]{4,3,2,1,0:T(8,128)(2,1)S(1)}, u32[]{:S(2)}, u32[]{:S(2)}) collective-permute-start(bf16[4,2,2,32,128]{4,3,2,1,0:T(8,128)(2,1)S(1)} %broadcast_select_fusion.33), channel_id=1, source_target_pairs={{0,8},{8,16},{16,24},{24,28},{28,20},{20,12},{12,4},{4,0},{1,9},{9... | collective-permute-start | bytes 393224 | tf_op jit(solution)/shard_map/ppermute | solution.py:284
  42.1 7.1 %collective-permute-start.15 = (bf16[4,2,2,32,128]{4,3,2,1,0:T(8,128)(2,1)S(1)}, bf16[4,2,2,32,128]{4,3,2,1,0:T(8,128)(2,1)S(1)}, u32[]{:S(2)}, u32[]{:S(2)}) collective-permute-start(bf16[4,2,2,32,128]{4,3,2,1,0:T(8,128)(2,1)S(1)} %broadcast_select_fusion.32), channel_id=1, source_target_pairs={{0,8},{8,16},{16,24},{24,28},{28,20},{20,12},{12,4},{4,0},{1,9},{9... | collective-permute-start | bytes 393224 | tf_op jit(solution)/shard_map/ppermute | solution.py:284
  43.8 7.0 %collective-permute-start.39 = (bf16[4,2,2,32,128]{4,3,2,1,0:T(8,128)(2,1)S(1)}, bf16[4,2,2,32,128]{4,3,2,1,0:T(8,128)(2,1)S(1)}, u32[]{:S(2)}, u32[]{:S(2)}) collective-permute-start(bf16[4,2,2,32,128]{4,3,2,1,0:T(8,128)(2,1)S(1)} %broadcast_select_fusion.16), channel_id=1, source_target_pairs={{0,4},{8,0},{16,8},{24,16},{28,24},{20,28},{12,20},{4,12},{1,5},{9... | collective-permute-start | bytes 393224 | tf_op jit(solution)/shard_map/ppermute | solution.py:284
  44.3 7.1 %collective-permute-start.40 = (bf16[4,2,2,32,128]{4,3,2,1,0:T(8,128)(2,1)S(1)}, bf16[4,2,2,32,128]{4,3,2,1,0:T(8,128)(2,1)S(1)}, u32[]{:S(2)}, u32[]{:S(2)}) collective-permute-start(bf16[4,2,2,32,128]{4,3,2,1,0:T(8,128)(2,1)S(1)} %broadcast_select_fusion.15), channel_id=1, source_target_pairs={{0,4},{8,0},{16,8},{24,16},{28,24},{20,28},{12,20},{4,12},{1,5},{9... | collective-permute-start | bytes 393224 | tf_op jit(solution)/shard_map/ppermute | solution.py:284
  46.4 6.7 %collective-permute-start.16 = (bf16[4,2,2,32,128]{4,3,2,1,0:T(8,128)(2,1)S(1)}, bf16[4,2,2,32,128]{4,3,2,1,0:T(8,128)(2,1)S(1)}, u32[]{:S(2)}, u32[]{:S(2)}) collective-permute-start(bf16[4,2,2,32,128]{4,3,2,1,0:T(8,128)(2,1)S(1)} %broadcast_select_fusion.31), channel_id=1, source_target_pairs={{0,8},{8,16},{16,24},{24,28},{28,20},{20,12},{12,4},{4,0},{1,9},{9... | collective-permute-start | bytes 393224 | tf_op jit(solution)/shard_map/ppermute | solution.py:284
  49.2 6.4 %collective-permute-start.17 = (bf16[4,2,2,32,128]{4,3,2,1,0:T(8,128)(2,1)S(1)}, bf16[4,2,2,32,128]{4,3,2,1,0:T(8,128)(2,1)S(1)}, u32[]{:S(2)}, u32[]{:S(2)}) collective-permute-start(bf16[4,2,2,32,128]{4,3,2,1,0:T(8,128)(2,1)S(1)} %broadcast_select_fusion.30), channel_id=1, source_target_pairs={{0,8},{8,16},{16,24},{24,28},{28,20},{20,12},{12,4},{4,0},{1,9},{9... | collective-permute-start | bytes 393224 | tf_op jit(solution)/shard_map/ppermute | solution.py:284
  50.8 6.4 %collective-permute-start.41 = (bf16[4,2,2,32,128]{4,3,2,1,0:T(8,128)(2,1)S(1)}, bf16[4,2,2,32,128]{4,3,2,1,0:T(8,128)(2,1)S(1)}, u32[]{:S(2)}, u32[]{:S(2)}) collective-permute-start(bf16[4,2,2,32,128]{4,3,2,1,0:T(8,128)(2,1)S(1)} %broadcast_select_fusion.14), channel_id=1, source_target_pairs={{0,4},{8,0},{16,8},{24,16},{28,24},{20,28},{12,20},{4,12},{1,5},{9... | collective-permute-start | bytes 393224 | tf_op jit(solution)/shard_map/ppermute | solution.py:284
  51.4 7.8 %collective-permute-start.42 = (bf16[4,2,2,32,128]{4,3,2,1,0:T(8,128)(2,1)S(1)}, bf16[4,2,2,32,128]{4,3,2,1,0:T(8,128)(2,1)S(1)}, u32[]{:S(2)}, u32[]{:S(2)}) collective-permute-start(bf16[4,2,2,32,128]{4,3,2,1,0:T(8,128)(2,1)S(1)} %broadcast_select_fusion.13), channel_id=1, source_target_pairs={{0,4},{8,0},{16,8},{24,16},{28,24},{20,28},{12,20},{4,12},{1,5},{9... | collective-permute-start | bytes 393224 | tf_op jit(solution)/shard_map/ppermute | solution.py:284
  53.2 6.9 %collective-permute-start.18 = (bf16[4,2,2,32,128]{4,3,2,1,0:T(8,128)(2,1)S(1)}, bf16[4,2,2,32,128]{4,3,2,1,0:T(8,128)(2,1)S(1)}, u32[]{:S(2)}, u32[]{:S(2)}) collective-permute-start(bf16[4,2,2,32,128]{4,3,2,1,0:T(8,128)(2,1)S(1)} %broadcast_select_fusion.29), channel_id=1, source_target_pairs={{0,8},{8,16},{16,24},{24,28},{28,20},{20,12},{12,4},{4,0},{1,9},{9... | collective-permute-start | bytes 393224 | tf_op jit(solution)/shard_map/ppermute | solution.py:284
  55.7 6.4 %collective-permute-start.19 = (bf16[4,2,2,32,128]{4,3,2,1,0:T(8,128)(2,1)S(1)}, bf16[4,2,2,32,128]{4,3,2,1,0:T(8,128)(2,1)S(1)}, u32[]{:S(2)}, u32[]{:S(2)}) collective-permute-start(bf16[4,2,2,32,128]{4,3,2,1,0:T(8,128)(2,1)S(1)} %broadcast_select_fusion.28), channel_id=1, source_target_pairs={{0,8},{8,16},{16,24},{24,28},{28,20},{20,12},{12,4},{4,0},{1,9},{9... | collective-permute-start | bytes 393224 | tf_op jit(solution)/shard_map/ppermute | solution.py:284
  57.2 6.7 %collective-permute-start.43 = (bf16[4,2,2,32,128]{4,3,2,1,0:T(8,128)(2,1)S(1)}, bf16[4,2,2,32,128]{4,3,2,1,0:T(8,128)(2,1)S(1)}, u32[]{:S(2)}, u32[]{:S(2)}) collective-permute-start(bf16[4,2,2,32,128]{4,3,2,1,0:T(8,128)(2,1)S(1)} %broadcast_select_fusion.12), channel_id=1, source_target_pairs={{0,4},{8,0},{16,8},{24,16},{28,24},{20,28},{12,20},{4,12},{1,5},{9... | collective-permute-start | bytes 393224 | tf_op jit(solution)/shard_map/ppermute | solution.py:284
  59.2 7.2 %collective-permute-start.44 = (bf16[4,2,2,32,128]{4,3,2,1,0:T(8,128)(2,1)S(1)}, bf16[4,2,2,32,128]{4,3,2,1,0:T(8,128)(2,1)S(1)}, u32[]{:S(2)}, u32[]{:S(2)}) collective-permute-start(bf16[4,2,2,32,128]{4,3,2,1,0:T(8,128)(2,1)S(1)} %broadcast_select_fusion.11), channel_id=1, source_target_pairs={{0,4},{8,0},{16,8},{24,16},{28,24},{20,28},{12,20},{4,12},{1,5},{9... | collective-permute-start | bytes 393224 | tf_op jit(solution)/shard_map/ppermute | solution.py:284
  60.1 6.8 %collective-permute-start.20 = (bf16[4,2,2,32,128]{4,3,2,1,0:T(8,128)(2,1)S(1)}, bf16[4,2,2,32,128]{4,3,2,1,0:T(8,128)(2,1)S(1)}, u32[]{:S(2)}, u32[]{:S(2)}) collective-permute-start(bf16[4,2,2,32,128]{4,3,2,1,0:T(8,128)(2,1)S(1)} %broadcast_select_fusion.27), channel_id=1, source_target_pairs={{0,8},{8,16},{16,24},{24,28},{28,20},{20,12},{12,4},{4,0},{1,9},{9... | collective-permute-start | bytes 393224 | tf_op jit(solution)/shard_map/ppermute | solution.py:284
  62.1 6.7 %collective-permute-start.21 = (bf16[4,2,2,32,128]{4,3,2,1,0:T(8,128)(2,1)S(1)}, bf16[4,2,2,32,128]{4,3,2,1,0:T(8,128)(2,1)S(1)}, u32[]{:S(2)}, u32[]{:S(2)}) collective-permute-start(bf16[4,2,2,32,128]{4,3,2,1,0:T(8,128)(2,1)S(1)} %broadcast_select_fusion.26), channel_id=1, source_target_pairs={{0,8},{8,16},{16,24},{24,28},{28,20},{20,12},{12,4},{4,0},{1,9},{9... | collective-permute-start | bytes 393224 | tf_op jit(solution)/shard_map/ppermute | solution.py:284
  64.0 6.5 %collective-permute-start.45 = (bf16[4,2,2,32,128]{4,3,2,1,0:T(8,128)(2,1)S(1)}, bf16[4,2,2,32,128]{4,3,2,1,0:T(8,128)(2,1)S(1)}, u32[]{:S(2)}, u32[]{:S(2)}) collective-permute-start(bf16[4,2,2,32,128]{4,3,2,1,0:T(8,128)(2,1)S(1)} %broadcast_select_fusion.10), channel_id=1, source_target_pairs={{0,4},{8,0},{16,8},{24,16},{28,24},{20,28},{12,20},{4,12},{1,5},{9... | collective-permute-start | bytes 393224 | tf_op jit(solution)/shard_map/ppermute | solution.py:284
  66.9 6.2 %collective-permute-start.22 = (bf16[4,2,2,32,128]{4,3,2,1,0:T(8,128)(2,1)S(1)}, bf16[4,2,2,32,128]{4,3,2,1,0:T(8,128)(2,1)S(1)}, u32[]{:S(2)}, u32[]{:S(2)}) collective-permute-start(bf16[4,2,2,32,128]{4,3,2,1,0:T(8,128)(2,1)S(1)} %broadcast_select_fusion.25), channel_id=1, source_target_pairs={{0,8},{8,16},{16,24},{24,28},{28,20},{20,12},{12,4},{4,0},{1,9},{9... | collective-permute-start | bytes 393224 | tf_op jit(solution)/shard_map/ppermute | solution.py:284
  68.8 6.9 %collective-permute-start.23 = (bf16[4,2,2,32,128]{4,3,2,1,0:T(8,128)(2,1)S(1)}, bf16[4,2,2,32,128]{4,3,2,1,0:T(8,128)(2,1)S(1)}, u32[]{:S(2)}, u32[]{:S(2)}) collective-permute-start(bf16[4,2,2,32,128]{4,3,2,1,0:T(8,128)(2,1)S(1)} %broadcast_select_fusion.24), channel_id=1, source_target_pairs={{0,8},{8,16},{16,24},{24,28},{28,20},{20,12},{12,4},{4,0},{1,9},{9... | collective-permute-start | bytes 393224 | tf_op jit(solution)/shard_map/ppermute | solution.py:284
  70.5 7.0 %collective-permute-start.47 = (bf16[4,2,2,32,128]{4,3,2,1,0:T(8,128)(2,1)S(1)}, bf16[4,2,2,32,128]{4,3,2,1,0:T(8,128)(2,1)S(1)}, u32[]{:S(2)}, u32[]{:S(2)}) collective-permute-start(bf16[4,2,2,32,128]{4,3,2,1,0:T(8,128)(2,1)S(1)} %broadcast_select_fusion.8), channel_id=1, source_target_pairs={{0,4},{8,0},{16,8},{24,16},{28,24},{20,28},{12,20},{4,12},{1,5},{9... | collective-permute-start | bytes 393224 | tf_op jit(solution)/shard_map/ppermute | solution.py:284
  72.1 6.3 %collective-permute-start.48 = (bf16[4,2,2,32,128]{4,3,2,1,0:T(8,128)(2,1)S(1)}, bf16[4,2,2,32,128]{4,3,2,1,0:T(8,128)(2,1)S(1)}, u32[]{:S(2)}, u32[]{:S(2)}) collective-permute-start(bf16[4,2,2,32,128]{4,3,2,1,0:T(8,128)(2,1)S(1)} %broadcast_select_fusion.7), channel_id=1, source_target_pairs={{0,4},{8,0},{16,8},{24,16},{28,24},{20,28},{12,20},{4,12},{1,5},{9... | collective-permute-start | bytes 393224 | tf_op jit(solution)/shard_map/ppermute | solution.py:284
  73.2 6.7 %collective-permute-start.24 = (bf16[4,2,2,32,128]{4,3,2,1,0:T(8,128)(2,1)S(1)}, bf16[4,2,2,32,128]{4,3,2,1,0:T(8,128)(2,1)S(1)}, u32[]{:S(2)}, u32[]{:S(2)}) collective-permute-start(bf16[4,2,2,32,128]{4,3,2,1,0:T(8,128)(2,1)S(1)} %broadcast_select_fusion.23), channel_id=1, source_target_pairs={{0,8},{8,16},{16,24},{24,28},{28,20},{20,12},{12,4},{4,0},{1,9},{9... | collective-permute-start | bytes 393224 | tf_op jit(solution)/shard_map/ppermute | solution.py:284
  75.7 6.4 %collective-permute-start.25 = (bf16[4,2,2,32,128]{4,3,2,1,0:T(8,128)(2,1)S(1)}, bf16[4,2,2,32,128]{4,3,2,1,0:T(8,128)(2,1)S(1)}, u32[]{:S(2)}, u32[]{:S(2)}) collective-permute-start(bf16[4,2,2,32,128]{4,3,2,1,0:T(8,128)(2,1)S(1)} %broadcast_select_fusion.22), channel_id=1, source_target_pairs={{0,8},{8,16},{16,24},{24,28},{28,20},{20,12},{12,4},{4,0},{1,9},{9... | collective-permute-start | bytes 393224 | tf_op jit(solution)/shard_map/ppermute | solution.py:284
  77.5 6.3 %collective-permute-start.49 = (bf16[4,2,2,32,128]{4,3,2,1,0:T(8,128)(2,1)S(1)}, bf16[4,2,2,32,128]{4,3,2,1,0:T(8,128)(2,1)S(1)}, u32[]{:S(2)}, u32[]{:S(2)}) collective-permute-start(bf16[4,2,2,32,128]{4,3,2,1,0:T(8,128)(2,1)S(1)} %broadcast_select_fusion.6), channel_id=1, source_target_pairs={{0,4},{8,0},{16,8},{24,16},{28,24},{20,28},{12,20},{4,12},{1,5},{9... | collective-permute-start | bytes 393224 | tf_op jit(solution)/shard_map/ppermute | solution.py:284
  78.3 6.5 %collective-permute-start.50 = (bf16[4,2,2,32,128]{4,3,2,1,0:T(8,128)(2,1)S(1)}, bf16[4,2,2,32,128]{4,3,2,1,0:T(8,128)(2,1)S(1)}, u32[]{:S(2)}, u32[]{:S(2)}) collective-permute-start(bf16[4,2,2,32,128]{4,3,2,1,0:T(8,128)(2,1)S(1)} %broadcast_select_fusion.5), channel_id=1, source_target_pairs={{0,4},{8,0},{16,8},{24,16},{28,24},{20,28},{12,20},{4,12},{1,5},{9... | collective-permute-start | bytes 393224 | tf_op jit(solution)/shard_map/ppermute | solution.py:284
  79.9 6.4 %collective-permute-start.26 = (bf16[4,2,2,32,128]{4,3,2,1,0:T(8,128)(2,1)S(1)}, bf16[4,2,2,32,128]{4,3,2,1,0:T(8,128)(2,1)S(1)}, u32[]{:S(2)}, u32[]{:S(2)}) collective-permute-start(bf16[4,2,2,32,128]{4,3,2,1,0:T(8,128)(2,1)S(1)} %broadcast_select_fusion.21), channel_id=1, source_target_pairs={{0,8},{8,16},{16,24},{24,28},{28,20},{20,12},{12,4},{4,0},{1,9},{9... | collective-permute-start | bytes 393224 | tf_op jit(solution)/shard_map/ppermute | solution.py:284
  84.9 7.9 %collective-permute-start.52 = (bf16[4,2,2,32,128]{4,3,2,1,0:T(8,128)(2,1)S(1)}, bf16[4,2,2,32,128]{4,3,2,1,0:T(8,128)(2,1)S(1)}, u32[]{:S(2)}, u32[]{:S(2)}) collective-permute-start(bf16[4,2,2,32,128]{4,3,2,1,0:T(8,128)(2,1)S(1)} %broadcast_select_fusion.3), channel_id=1, source_target_pairs={{0,4},{8,0},{16,8},{24,16},{28,24},{20,28},{12,20},{4,12},{1,5},{9... | collective-permute-start | bytes 393224 | tf_op jit(solution)/shard_map/ppermute | solution.py:284
  86.3 6.6 %collective-permute-start.28 = (bf16[4,2,2,32,128]{4,3,2,1,0:T(8,128)(2,1)S(1)}, bf16[4,2,2,32,128]{4,3,2,1,0:T(8,128)(2,1)S(1)}, u32[]{:S(2)}, u32[]{:S(2)}) collective-permute-start(bf16[4,2,2,32,128]{4,3,2,1,0:T(8,128)(2,1)S(1)} %broadcast_select_fusion.19), channel_id=1, source_target_pairs={{0,8},{8,16},{16,24},{24,28},{28,20},{20,12},{12,4},{4,0},{1,9},{9... | collective-permute-start | bytes 393224 | tf_op jit(solution)/shard_map/ppermute | solution.py:284
  87.9 8.7 %collective-permute-start.29 = (bf16[4,2,2,32,128]{4,3,2,1,0:T(8,128)(2,1)S(1)}, bf16[4,2,2,32,128]{4,3,2,1,0:T(8,128)(2,1)S(1)}, u32[]{:S(2)}, u32[]{:S(2)}) collective-permute-start(bf16[4,2,2,32,128]{4,3,2,1,0:T(8,128)(2,1)S(1)} %broadcast_select_fusion.18), channel_id=1, source_target_pairs={{0,8},{8,16},{16,24},{24,28},{28,20},{20,12},{12,4},{4,0},{1,9},{9... | collective-permute-start | bytes 393224 | tf_op jit(solution)/shard_map/ppermute | solution.py:284
  90.0 6.4 %collective-permute-start.53 = (bf16[4,2,2,32,128]{4,3,2,1,0:T(8,128)(2,1)S(1)}, bf16[4,2,2,32,128]{4,3,2,1,0:T(8,128)(2,1)S(1)}, u32[]{:S(2)}, u32[]{:S(2)}) collective-permute-start(bf16[4,2,2,32,128]{4,3,2,1,0:T(8,128)(2,1)S(1)} %broadcast_select_fusion.2), channel_id=1, source_target_pairs={{0,4},{8,0},{16,8},{24,16},{28,24},{20,28},{12,20},{4,12},{1,5},{9... | collective-permute-start | bytes 393224 | tf_op jit(solution)/shard_map/ppermute | solution.py:284
  92.8 6.4 %collective-permute-start.54 = (bf16[4,2,2,32,128]{4,3,2,1,0:T(8,128)(2,1)S(1)}, bf16[4,2,2,32,128]{4,3,2,1,0:T(8,128)(2,1)S(1)}, u32[]{:S(2)}, u32[]{:S(2)}) collective-permute-start(bf16[4,2,2,32,128]{4,3,2,1,0:T(8,128)(2,1)S(1)} %broadcast_select_fusion.1), channel_id=1, source_target_pairs={{0,4},{8,0},{16,8},{24,16},{28,24},{20,28},{12,20},{4,12},{1,5},{9... | collective-permute-start | bytes 393224 | tf_op jit(solution)/shard_map/ppermute | solution.py:284
  93.0 6.3 %collective-permute-start.30 = (bf16[4,2,2,32,128]{4,3,2,1,0:T(8,128)(2,1)S(1)}, bf16[4,2,2,32,128]{4,3,2,1,0:T(8,128)(2,1)S(1)}, u32[]{:S(2)}, u32[]{:S(2)}) collective-permute-start(bf16[4,2,2,32,128]{4,3,2,1,0:T(8,128)(2,1)S(1)} %broadcast_select_fusion.17), channel_id=1, source_target_pairs={{0,8},{8,16},{16,24},{24,28},{28,20},{20,12},{12,4},{4,0},{1,9},{9... | collective-permute-start | bytes 393224 | tf_op jit(solution)/shard_map/ppermute | solution.py:284
  99.3 6.4 %collective-permute-start.56 = (bf16[4,2,2,32,128]{4,3,2,1,0:T(8,128)(2,1)S(1)}, bf16[4,2,2,32,128]{4,3,2,1,0:T(8,128)(2,1)S(1)}, u32[]{:S(2)}, u32[]{:S(2)}) collective-permute-start(bf16[4,2,2,32,128]{4,3,2,1,0:T(8,128)(2,1)S(1)} %collective-permute-done.54.refs_71_.refs_76_), channel_id=1, source_target_pairs={{0,4},{8,0},{16,8},{24,16},{28,24},{20,28},{12,20},{4,12},{1,5},{9... | collective-permute-start | bytes 393224 | tf_op jit(solution)/shard_map/ppermute | solution.py:284
  99.3 6.4 %collective-permute-start.32 = (bf16[4,2,2,32,128]{4,3,2,1,0:T(8,128)(2,1)S(1)}, bf16[4,2,2,32,128]{4,3,2,1,0:T(8,128)(2,1)S(1)}, u32[]{:S(2)}, u32[]{:S(2)}) collective-permute-start(bf16[4,2,2,32,128]{4,3,2,1,0:T(8,128)(2,1)S(1)} %collective-permute-done.30.refs_52_), channel_id=1, source_target_pairs={{0,8},{8,16},{16,24},{24,28},{28,20},{20,12},{12,4},{4,0},{1,9},{9... | collective-permute-start | bytes 393224 | tf_op jit(solution)/shard_map/ppermute | solution.py:284
  107.8 8.9 %collective-permute-start.35 = (bf16[4,2,2,32,128]{4,3,2,1,0:T(8,128)(2,1)S(1)}, bf16[4,2,2,32,128]{4,3,2,1,0:T(8,128)(2,1)S(1)}, u32[]{:S(2)}, u32[]{:S(2)}) collective-permute-start(bf16[4,2,2,32,128]{4,3,2,1,0:T(8,128)(2,1)S(1)} %collective-permute-done.33.refs_55_), channel_id=1, source_target_pairs={{0,8},{8,16},{16,24},{24,28},{28,20},{20,12},{12,4},{4,0},{1,9},{9... | collective-permute-start | bytes 393224 | tf_op jit(solution)/shard_map/ppermute | solution.py:284
  110.6 6.2 %collective-permute-start.60 = (bf16[4,2,2,32,128]{4,3,2,1,0:T(8,128)(2,1)S(1)}, bf16[4,2,2,32,128]{4,3,2,1,0:T(8,128)(2,1)S(1)}, u32[]{:S(2)}, u32[]{:S(2)}) collective-permute-start(bf16[4,2,2,32,128]{4,3,2,1,0:T(8,128)(2,1)S(1)} %collective-permute-done.58.refs_80_), channel_id=1, source_target_pairs={{0,4},{8,0},{16,8},{24,16},{28,24},{20,28},{12,20},{4,12},{1,5},{9... | collective-permute-start | bytes 393224 | tf_op jit(solution)/shard_map/ppermute | solution.py:284
  110.7 6.1 %collective-permute-start.36 = (bf16[4,2,2,32,128]{4,3,2,1,0:T(8,128)(2,1)S(1)}, bf16[4,2,2,32,128]{4,3,2,1,0:T(8,128)(2,1)S(1)}, u32[]{:S(2)}, u32[]{:S(2)}) collective-permute-start(bf16[4,2,2,32,128]{4,3,2,1,0:T(8,128)(2,1)S(1)} %collective-permute-done.34.refs_56_), channel_id=1, source_target_pairs={{0,8},{8,16},{16,24},{24,28},{28,20},{20,12},{12,4},{4,0},{1,9},{9... | collective-permute-start | bytes 393224 | tf_op jit(solution)/shard_map/ppermute | solution.py:284
  (18 other events, 122.5 us)
